TPU v7x, 32 devices: a whole 2x2x4 slice. The times are simulated.
32 devices in a mesh: gx: 2 (over x), yz: 16 (over z, y, core).
Axes of the slice: x: 2, y: 2, z: 4, core: 2. Of those that a mesh axis runs over, the one named last changes fastest.
Arguments:
- system_source_term: float32 [320, 4096], P(None, ('gx', 'yz')), may hold values from -200 to 200
- mass_plus_source: float32 [320, 4096], P(None, ('gx', 'yz')), may hold values from 1 to 4
- lifted_upwind_coupling: float32 [480, 4096], P(None, ('gx', 'yz')), may hold values from 0.5 to 2
- frozen_direction_derivative: float32 [75, 4096], P(None, ('gx', 'yz')), may hold values from -3 to 3
- first_solve_matrix: float32 [320, 320], replicated, may hold values from -0.3125 to 0.3125
- final_solve_matrix: float32 [320, 320], replicated, may hold values from -0.3125 to 0.3125
- middle_cell_matrices: float32 [320, 4096], P(None, ('gx', 'yz')), may hold values from 0.3 to 3
- adjacent_table_slots: int32 [6, 4096], P(None, ('gx', 'yz')), may hold values from 0 to 1264, as said below
- plane_outgoing_cells: int32 [32, 2, 16], P(('gx', 'yz')), may hold values from 0 to 127
- band_outgoing_cells: int32 [32, 2, 16], P(('gx', 'yz')), may hold values from 0 to 127
- small_side_table_slot: int32 [32, 352], P(('gx', 'yz')), may hold values from 0 to 768, as said below
- proprietor_mortar_index: int32 [32, 352], P(('gx', 'yz')), may hold values from 0 to 80, as said below
- outgoing_quadrant_index: int32 [32, 352], P(('gx', 'yz')), may hold values from 0 to 3, as said below
- incoming_mortar_index: int32 [32, 352], P(('gx', 'yz')), may hold values from 0 to 80
- incoming_quadrant_index: int32 [32, 352], P(('gx', 'yz')), may hold values from 0 to 3, as said below
- coarse_mortar_table_slot: int32 [32, 80], P(('gx', 'yz')), may hold values from 0 to 767
Outputs:
- newton_update: float32 [320, 4096], P(None, ('gx', 'yz'))
Inputs may be any that keep to these rules, and one draw needn't show every extreme that they name: `adjacent_table_slots`: column of the neighbour trace in the device's table; 1264 marks a boundary face. `small_side_table_slot`: 768 marks an empty slot, exactly where proprietor_mortar_index is 80. Send slot (m, c) of device (g, k) and receive slot (k, c) of device (g, m) hold the same tile: there proprietor_mortar_index, outgoing_quadrant_index equal incoming_mortar_index, incoming_quadrant_index here; 80 marks an empty slot; no position of an owner's hanging face is sent twice; the live hanging faces of an owner are its first ones; from one device to one owner go at most 22 tiles, a bound reached in every draw; in each gx plane one owner receives 4 * 80 tiles. `outgoing_quadrant_index`: 0 in empty slots. `incoming_quadrant_index`: 0 in empty slots.
All inputs are finite; a program needn't handle non-finite values.
Results may differ from a plain program's by a relative error of at most 0.0003.
Values sent between devices are 32-bit elements; how exact they have to be, the bound alone decides.
No kernel may reach another device: no remote copies, remote signals or barrier semaphores. Data moves between devices by JAX's collectives and lax.ppermute only.
A program may use at most 64 MiB of HBM per device.

v0:
```python
import jax
import jax.numpy as jnp
import numpy as np
from jax import lax
from jax.sharding import PartitionSpec as P

ITERS = 2


maximum_depth = lax.Precision.HIGHEST
epsilon = 1e-06


def with_halo(shard, sides, width, wrap):
    for axis, dim in sides:
        size, length = (lax.axis_size(axis), shard.shape[dim])
        up = [(i, (i + 1) % size) for i in range(size if wrap else size - 1)]
        down = [(j, i) for i, j in up]
        last = lax.slice_in_dim(shard, length - width, length, axis=dim)
        leading = lax.slice_in_dim(shard, 0, width, axis=dim)
        before = lax.ppermute(last, axis, up)
        after = lax.ppermute(leading, axis, down)
        shard = jnp.concatenate([before, shard, after], axis=dim)
    return shard


def gll_tables():
    inv_root = 1.0 / np.sqrt(5.0)
    gll_points = np.array([-1.0, -inv_root, inv_root, 1.0])
    weights = np.array([1.0, 5.0, 5.0, 1.0]) / 6.0

    def lagrange(points):
        values_at = np.ones((len(points), 4))
        for table_slot_index in range(4):
            for m in range(4):
                if m != table_slot_index:
                    values_at[:, table_slot_index] = (
                        values_at[:, table_slot_index]
                        * (points - gll_points[m])
                        / (gll_points[table_slot_index] - gll_points[m])
                    )
        return values_at

    derivative = np.zeros((4, 4))
    for i in range(4):
        for table_slot_index in range(4):
            summed = 0.0
            for m in range(4):
                if m != table_slot_index:
                    product_term = 1.0 / (gll_points[table_slot_index] - gll_points[m])
                    for n in range(4):
                        if n != table_slot_index and n != m:
                            product_term = (
                                product_term
                                * (gll_points[i] - gll_points[n])
                                / (gll_points[table_slot_index] - gll_points[n])
                            )
                    summed = summed + product_term
            derivative[i, table_slot_index] = summed
    halves = [lagrange((gll_points - 1.0) / 2.0), lagrange((gll_points + 1.0) / 2.0)]
    half_projections = [
        0.5 * (1.0 / weights)[:, None] * halve.T * weights[None, :] for halve in halves
    ]
    interpolate = np.stack([np.kron(halves[q // 2], halves[q % 2]) for q in range(4)])
    projection = np.stack(
        [np.kron(half_projections[q // 2], half_projections[q % 2]) for q in range(4)]
    )
    identity_four = np.eye(4)
    node_derivative = np.stack(
        [
            np.kron(derivative, np.kron(identity_four, identity_four)),
            np.kron(identity_four, np.kron(derivative, identity_four)),
            np.kron(identity_four, np.kron(identity_four, derivative)),
        ]
    )
    selection = np.zeros((6, 16, 64))
    for face_id in range(6):
        direction = face_id // 2
        fixed_node = 0 if face_id % 2 == 0 else 3
        for first in range(4):
            for second in range(4):
                if direction == 0:
                    node = fixed_node * 16 + first * 4 + second
                elif direction == 1:
                    node = first * 16 + fixed_node * 4 + second
                else:
                    node = first * 16 + second * 4 + fixed_node
                selection[face_id, first * 4 + second, node] = 1.0
    lifting = selection.transpose(2, 0, 1)
    return (
        jnp.asarray(node_derivative, jnp.float32),
        jnp.asarray(interpolate, jnp.float32),
        jnp.asarray(projection, jnp.float32),
        jnp.asarray(selection, jnp.float32),
        jnp.asarray(lifting, jnp.float32),
    )


def own_traces(argument_array, selection):
    local_count = argument_array.shape[1]
    nodal_view = argument_array.reshape(5, 64, local_count)
    faces = jnp.einsum("fsn,ane->asfe", selection, nodal_view, precision=maximum_depth)
    return faces.reshape(80, 6 * local_count)


def jacobian(
    argument_array,
    own_faces,
    near_faces,
    mass_plus_source,
    lifted_upwind_coupling,
    frozen_direction_derivative,
    node_derivative,
    lifting,
):
    local_count = argument_array.shape[1]
    nodal_view = argument_array.reshape(5, 64, local_count)
    flux_blocks = frozen_direction_derivative.reshape(3, 5, 5, local_count)
    flux_terms = jnp.einsum("dabe,bne->dane", flux_blocks, nodal_view, precision=maximum_depth)
    derived = jnp.einsum("dmn,dane->ame", node_derivative, flux_terms, precision=maximum_depth)
    difference = (own_faces - near_faces).reshape(5, 16, 6, local_count)
    coupling = lifted_upwind_coupling.reshape(6, 5, 16, local_count)
    lifted = jnp.einsum(
        "nfs,fase,asfe->ane", lifting, coupling, difference, precision=maximum_depth
    )
    return mass_plus_source * argument_array + (derived + lifted).reshape(320, local_count)


def solve_cell_system(argument_array, first_solve_matrix, final_solve_matrix, middle_cell_matrices):
    interior_share = jnp.dot(
        first_solve_matrix,
        argument_array,
        precision=maximum_depth,
        preferred_element_type=jnp.float32,
    )
    return jnp.dot(
        final_solve_matrix,
        middle_cell_matrices * interior_share,
        precision=maximum_depth,
        preferred_element_type=jnp.float32,
    )


def mortar_sums(received, incoming_mortar_index, incoming_quadrant_index, projection, hang_count):
    slot_count = received.shape[1]
    face_values = received.reshape(5, 16, slot_count)
    candidates = jnp.einsum("qmn,anc->qamc", projection, face_values, precision=maximum_depth)
    selector_q = (
        incoming_quadrant_index[None, :] == jnp.arange(4, dtype=jnp.int32)[:, None]
    ).astype(jnp.float32)
    projected = jnp.sum(candidates * selector_q[:, None, None, :], axis=0).reshape(80, slot_count)
    onehot = (
        incoming_mortar_index[:, None] == jnp.arange(hang_count, dtype=jnp.int32)[None, :]
    ).astype(jnp.float32)
    return jnp.dot(projected, onehot, precision=maximum_depth, preferred_element_type=jnp.float32)


def fine_replies(coarse_cols, outgoing_quadrant_index, interpolate):
    slot_count = coarse_cols.shape[1]
    face_values = coarse_cols.reshape(5, 16, slot_count)
    candidates = jnp.einsum("qmn,anc->qamc", interpolate, face_values, precision=maximum_depth)
    selector_q = (
        outgoing_quadrant_index[None, :] == jnp.arange(4, dtype=jnp.int32)[:, None]
    ).astype(jnp.float32)
    return jnp.sum(candidates * selector_q[:, None, None, :], axis=0).reshape(80, slot_count)


def least_squares(beta_norm, columns):
    steps_count = len(columns)
    zero_value = jnp.zeros((), jnp.float32)
    target = [beta_norm] + [zero_value] * steps_count
    rotations = []
    upper_rows = []
    for table_slot_index in range(steps_count):
        column = list(columns[table_slot_index])
        for i in range(len(rotations)):
            cos_value, sine_value = rotations[i]
            first_new = cos_value * column[i] + sine_value * column[i + 1]
            second = cos_value * column[i + 1] - sine_value * column[i]
            column[i] = first_new
            column[i + 1] = second
        radius = jnp.sqrt(
            column[table_slot_index] * column[table_slot_index]
            + column[table_slot_index + 1] * column[table_slot_index + 1]
        )
        cos_value = column[table_slot_index] / radius
        sine_value = column[table_slot_index + 1] / radius
        column[table_slot_index] = radius
        rotations.append((cos_value, sine_value))
        target[table_slot_index + 1] = -sine_value * target[table_slot_index]
        target[table_slot_index] = cos_value * target[table_slot_index]
        upper_rows.append(column[: table_slot_index + 1])
    coeffs = [zero_value] * steps_count
    for table_slot_index in reversed(range(steps_count)):
        running = target[table_slot_index]
        for k in range(table_slot_index + 1, steps_count):
            running = running - upper_rows[k][table_slot_index] * coeffs[k]
        coeffs[table_slot_index] = running / upper_rows[table_slot_index][table_slot_index]
    return coeffs


def merged_global(partial_values):
    return lax.psum(partial_values, ("gx", "yz"))


def on_device(
    system_source_term,
    mass_plus_source,
    lifted_upwind_coupling,
    frozen_direction_derivative,
    first_solve_matrix,
    final_solve_matrix,
    middle_cell_matrices,
    adjacent_table_slots,
    plane_outgoing_cells,
    band_outgoing_cells,
    small_side_table_slot,
    proprietor_mortar_index,
    outgoing_quadrant_index,
    incoming_mortar_index,
    incoming_quadrant_index,
    coarse_mortar_table_slot,
):
    node_derivative, interpolate, projection, selection, lifting = gll_tables()
    local_count = system_source_term.shape[1]
    hang_count = coarse_mortar_table_slot.shape[1]
    halo_width = plane_outgoing_cells.shape[2]
    near_index = adjacent_table_slots.reshape(-1)
    defect_array = solve_cell_system(
        system_source_term, first_solve_matrix, final_solve_matrix, middle_cell_matrices
    )
    beta_norm = jnp.sqrt(
        merged_global(jnp.stack([jnp.sum(defect_array * defect_array)]))[0] + epsilon
    )
    arnoldi_directions = [defect_array / beta_norm]
    columns = []
    for table_slot_index in range(ITERS):
        argument_array = arnoldi_directions[table_slot_index]
        own_faces = own_traces(argument_array, selection)
        slab_buffer = jnp.stack(
            [
                jnp.take(own_faces, plane_outgoing_cells[0, 0], axis=1),
                jnp.take(own_faces, local_count + plane_outgoing_cells[0, 1], axis=1),
            ]
        ).reshape(2, 80 * halo_width)
        slab_padded = with_halo(slab_buffer, (("gx", 0),), 1, False)
        side_buffer = jnp.stack(
            [
                jnp.take(own_faces, 2 * local_count + band_outgoing_cells[0, 0], axis=1),
                jnp.take(own_faces, 3 * local_count + band_outgoing_cells[0, 1], axis=1),
            ]
        ).reshape(2, 80 * halo_width)
        side_padded = with_halo(side_buffer, (("yz", 0),), 1, True)
        fine_send = jnp.take(
            own_faces, small_side_table_slot[0], axis=1, mode="fill", fill_value=0.0
        )
        coarse = jnp.take(own_faces, coarse_mortar_table_slot[0], axis=1)
        outgoing = jnp.take(coarse, incoming_mortar_index[0], axis=1, mode="fill", fill_value=0.0)
        fine_recv = lax.all_to_all(fine_send, "yz", split_axis=1, concat_axis=1, tiled=True)
        coarse_cols = lax.all_to_all(outgoing, "yz", split_axis=1, concat_axis=1, tiled=True)
        hang_sum = mortar_sums(
            fine_recv, incoming_mortar_index[0], incoming_quadrant_index[0], projection, hang_count
        )
        replies = fine_replies(coarse_cols, outgoing_quadrant_index[0], interpolate)
        trace_table = jnp.concatenate(
            [
                own_faces,
                slab_padded[0].reshape(80, halo_width),
                slab_padded[3].reshape(80, halo_width),
                side_padded[0].reshape(80, halo_width),
                side_padded[3].reshape(80, halo_width),
                hang_sum,
                replies,
            ],
            axis=1,
        )
        near_faces = jnp.take(trace_table, near_index, axis=1, mode="fill", fill_value=0.0)
        scratch_storage = solve_cell_system(
            jacobian(
                argument_array,
                own_faces,
                near_faces,
                mass_plus_source,
                lifted_upwind_coupling,
                frozen_direction_derivative,
                node_derivative,
                lifting,
            ),
            first_solve_matrix,
            final_solve_matrix,
            middle_cell_matrices,
        )
        column = []
        locals_list = [
            jnp.sum(scratch_storage * arnoldi_directions[i]) for i in range(table_slot_index + 1)
        ] + [jnp.sum(scratch_storage * scratch_storage)]
        totals = merged_global(jnp.stack(locals_list))
        squared = totals[table_slot_index + 1]
        for i in range(table_slot_index + 1):
            coefficient = totals[i]
            scratch_storage = scratch_storage - coefficient * arnoldi_directions[i]
            squared = squared - coefficient * coefficient
            column.append(coefficient)
        new_norm = jnp.sqrt(squared + epsilon)
        column.append(new_norm)
        columns.append(column)
        arnoldi_directions.append(scratch_storage / new_norm)
    coeffs = least_squares(beta_norm, columns)
    newton_update = coeffs[0] * arnoldi_directions[0]
    table_slot_index = 1
    newton_update = newton_update + coeffs[table_slot_index] * arnoldi_directions[table_slot_index]
    return newton_update


def solution(mesh):
    return jax.shard_map(
        on_device,
        mesh=mesh,
        in_specs=(
            P(None, ("gx", "yz")),
            P(None, ("gx", "yz")),
            P(None, ("gx", "yz")),
            P(None, ("gx", "yz")),
            P(),
            P(),
            P(None, ("gx", "yz")),
            P(None, ("gx", "yz")),
            P(("gx", "yz"), None, None),
            P(("gx", "yz"), None, None),
            P(("gx", "yz"), None),
            P(("gx", "yz"), None),
            P(("gx", "yz"), None),
            P(("gx", "yz"), None),
            P(("gx", "yz"), None),
            P(("gx", "yz"), None),
        ),
        out_specs=P(None, ("gx", "yz")),
        check_vma=False,
    )
```

profile of v0, /device:TPU:0, one launch (start us, length us, event | category | flops | bytes accessed | tf_op | source)
XLA Modules:
  0.0 263.5 jit_solution(4759819469362136421)
XLA Ops:
  0.0 1.0 copy-done
  1.0 1.5 convolution_multiply_fusion
  2.6 2.2 multiply_reduce_fusion.3
  4.8 42.2 %psum.21 = f32[1]{0:T(128)} all-reduce(f32[1]{0:T(128)} %bitcast), channel_id=1, replica_groups=mesh['gx'=2,'yz'=16] {'gx','yz'}, use_global_device_ids=true, to_apply=%region_1.0 | all-reduce | flops 1 | bytes 8 | tf_op jit(solution)/shard_map/psum | solution.py:203
  49.9 4.2 %collective-permute-start = (f32[1,1280]{1,0:T(1,128)S(1)}, f32[1,1280]{1,0:T(1,128)S(1)}, u32[]{:S(2)}, u32[]{:S(2)}) collective-permute-start(f32[1,1280]{1,0:T(1,128)S(1)} %slice.64), channel_id=1, source_target_pairs={{0,16},{1,17},{2,18},{3,19},{4,20},{5,21},{6,22},{7,23},{8,24},{9,... | collective-permute-start | bytes 15368 | tf_op jit(solution)/shard_map/ppermute | solution.py:21
  55.6 1.3 collective-permute-start.1
  59.8 4.4 %collective-permute-start.3 = (f32[1,1280]{1,0:T(1,128)}, f32[1,1280]{1,0:T(1,128)S(1)}, u32[]{:S(2)}, u32[]{:S(2)}) collective-permute-start(f32[1,1280]{1,0:T(1,128)} %slice.70), channel_id=1, source_target_pairs={{1,0},{2,1},{3,2},{4,3},{5,4},{6,5},{7,6},{8,7},{9,8},{10,9},{11,1... | collective-permute-start | bytes 15368 | tf_op jit(solution)/shard_map/ppermute | solution.py:22
  64.9 1.1 gather_fusion.4
  66.1 0.7 all_to_all.24
  66.8 4.2 %all-to-all-start = ((f32[80,16,22]{0,2,1:T(8,128)}), f32[80,16,22]{0,2,1:T(8,128)}, u32[]{:S(2)}, u32[]{:S(2)}) async-start(f32[80,16,22]{0,2,1:T(8,128)} %all_to_all.24), calls=%async_computation | async-start | bytes 393216 | tf_op jit(solution)/shard_map/all_to_all | solution.py:259
  73.4 1.0 copy.180
  77.0 3.7 %convolution_bitcast_fusion.1 = f32[3,5,64,128]{2,1,0,3:T(8,128)S(1)} fusion(f32[5,64,128,1]{1,0,3,2:T(8,128)} %copy.180, f32[3,5,5,128]{2,1,0,3:T(8,128)S(1)} %copy.130), kind=kOutput, calls=%fused_computation.17 | convolution fusion | flops 7372800 | bytes 693760 | tf_op jit(solution)/shard_map/dabe,bne->dane/dot_general | solution.py:119
  80.6 2.0 convolution_bitcast_fusion.13
  82.7 1.1 gather_fusion.6
  86.0 5.9 %all-to-all-start.1 = ((f32[80,16,22]{0,2,1:T(8,128)}), f32[80,16,22]{0,2,1:T(8,128)S(1)}, u32[]{:S(2)}, u32[]{:S(2)}) async-start(f32[80,16,22]{0,2,1:T(8,128)} %all_to_all.26), calls=%async_computation.1 | async-start | bytes 393216 | tf_op jit(solution)/shard_map/all_to_all | solution.py:260
  92.0 2.1 copy.142
  94.0 1.4 reshape.366
  95.4 5.5 %all-to-all-done.1 = f32[80,16,22]{0,2,1:T(8,128)S(1)} async-done(((f32[80,16,22]{0,2,1:T(8,128)}), f32[80,16,22]{0,2,1:T(8,128)S(1)}, u32[]{:S(2)}, u32[]{:S(2)}) %all-to-all-start.1) | async-done | bytes 112672 | tf_op jit(solution)/shard_map/all_to_all | solution.py:260
  100.9 1.2 copy.144
  102.0 1.4 reshape.368
  104.1 1.3 fusion.4
  105.4 1.1 convolution_dynamic-update-slice_fusion.1
  106.5 2.6 gather_fusion.7
  109.1 1.2 copy.152
  110.3 0.8 bitcast_subtract_fusion.1
  111.1 1.0 reshape.174
  112.1 1.1 bitcast_multiply_fusion.1
  113.2 1.3 fusion.10
  115.1 1.2 fusion.17
  116.3 1.3 pad_maximum_fusion
  117.6 38.6 %psum.22 = f32[2]{0:T(128)S(1)} all-reduce(f32[2]{0:T(128)S(1)} %pad_maximum_fusion), channel_id=1, replica_groups=mesh['gx'=2,'yz'=16] {'gx','yz'}, use_global_device_ids=true, to_apply=%region_6.12 | all-reduce | flops 2 | bytes 16 | tf_op jit(solution)/shard_map/psum | solution.py:203
  163.6 1.6 gather_fusion.12
  165.2 0.7 gather_fusion.13
  166.7 1.0 copy.187
  167.7 3.7 %convolution_bitcast_fusion = f32[3,5,64,128]{2,1,0,3:T(8,128)S(1)} fusion(f32[5,64,128,1]{1,0,3,2:T(8,128)} %copy.187, f32[3,5,5,128]{2,1,0,3:T(8,128)S(1)} %copy.130), kind=kOutput, calls=%fused_computation.16 | convolution fusion | flops 7372800 | bytes 693760 | tf_op jit(solution)/shard_map/dabe,bne->dane/dot_general | solution.py:119
  171.5 1.3 convolution_bitcast_fusion.10
  173.0 4.2 %collective-permute-start.4 = (f32[1,1280]{1,0:T(1,128)S(1)}, f32[1,1280]{1,0:T(1,128)S(1)}, u32[]{:S(2)}, u32[]{:S(2)}) collective-permute-start(f32[1,1280]{1,0:T(1,128)S(1)} %slice.73), channel_id=1, source_target_pairs={{0,16},{1,17},{2,18},{3,19},{4,20},{5,21},{6,22},{7,23},{8,24},{9,... | collective-permute-start | bytes 15368 | tf_op jit(solution)/shard_map/ppermute | solution.py:21
  177.4 1.3 collective-permute-start.5
  179.2 4.5 %collective-permute-start.7 = (f32[1,1280]{1,0:T(1,128)S(1)}, f32[1,1280]{1,0:T(1,128)S(1)}, u32[]{:S(2)}, u32[]{:S(2)}) collective-permute-start(f32[1,1280]{1,0:T(1,128)S(1)} %slice.76), channel_id=1, source_target_pairs={{1,0},{2,1},{3,2},{4,3},{5,4},{6,5},{7,6},{8,7},{9,8},{10,9},{11,1... | collective-permute-start | bytes 15368 | tf_op jit(solution)/shard_map/ppermute | solution.py:22
  184.5 3.5 %all-to-all-start.2 = ((f32[80,16,22]{0,2,1:T(8,128)}), f32[80,16,22]{0,2,1:T(8,128)S(1)}, u32[]{:S(2)}, u32[]{:S(2)}) async-start(f32[80,16,22]{0,2,1:T(8,128)} %all_to_all.28), calls=%async_computation.2 | async-start | bytes 393216 | tf_op jit(solution)/shard_map/all_to_all | solution.py:259
  188.1 1.1 gather_fusion.14
  190.8 6.1 %all-to-all-done.2 = f32[80,16,22]{0,2,1:T(8,128)S(1)} async-done(((f32[80,16,22]{0,2,1:T(8,128)}), f32[80,16,22]{0,2,1:T(8,128)S(1)}, u32[]{:S(2)}, u32[]{:S(2)}) %all-to-all-start.2) | async-done | bytes 112672 | tf_op jit(solution)/shard_map/all_to_all | solution.py:259
  197.0 3.7 %all-to-all-start.3 = ((f32[80,16,22]{0,2,1:T(8,128)}), f32[80,16,22]{0,2,1:T(8,128)S(1)}, u32[]{:S(2)}, u32[]{:S(2)}) async-start(f32[80,16,22]{0,2,1:T(8,128)} %all_to_all.30), calls=%async_computation.3 | async-start | bytes 393216 | tf_op jit(solution)/shard_map/all_to_all | solution.py:260
  202.0 7.4 %all-to-all-done.3 = f32[80,16,22]{0,2,1:T(8,128)S(1)} async-done(((f32[80,16,22]{0,2,1:T(8,128)}), f32[80,16,22]{0,2,1:T(8,128)S(1)}, u32[]{:S(2)}, u32[]{:S(2)}) %all-to-all-start.3) | async-done | bytes 112672 | tf_op jit(solution)/shard_map/all_to_all | solution.py:260
  211.2 1.6 gather_fusion.15
  214.6 1.2 fusion.20
  215.8 2.0 pad_maximum_fusion.1
  217.8 38.5 %psum.23 = f32[3]{0:T(128)S(1)} all-reduce(f32[3]{0:T(128)S(1)} %pad_maximum_fusion.1), channel_id=1, replica_groups=mesh['gx'=2,'yz'=16] {'gx','yz'}, use_global_device_ids=true, to_apply=%region_12.18 | all-reduce | flops 3 | bytes 24 | tf_op jit(solution)/shard_map/psum | solution.py:203
  (266 shorter events, 30.1 us)
Async XLA Ops:
  0.0 47.7 %copy-start.19 = (f32[6,16,64,1]{2,1,0,3:T(8,128)S(1)}, f32[6,16,64,1]{2,1,0,3:T(8,128)}, u32[]{:S(2)}) copy-start(f32[6,16,64,1]{2,1,0,3:T(8,128)} %constant.85) | copy-start | bytes 73732
  2.6 46.4 %copy-start.58 = (s32[1,2,16]{2,1,0:T(2,128)S(1)}, s32[1,2,16]{2,1,0:T(2,128)}, u32[]{:S(2)}) copy-start(s32[1,2,16]{2,1,0:T(2,128)} %param.39) | copy-start | bytes 388
  47.6 67.5 %copy-start.3 = (f32[128,320]{0,1:T(8,128)}, f32[128,320]{0,1:T(8,128)S(1)}, u32[]{:S(2)}) copy-start(f32[128,320]{0,1:T(8,128)S(1)} %broadcast_divide_fusion) | copy-start | bytes 491524
  47.7 9.2 %copy-start.59 = (s32[1,2,16]{2,1,0:T(2,128)S(1)}, s32[1,2,16]{2,1,0:T(2,128)}, u32[]{:S(2)}) copy-start(s32[1,2,16]{2,1,0:T(2,128)} %param.40) | copy-start | bytes 388
  48.1 16.1 %copy-start.54 = (s32[1,352]{1,0:T(1,128)S(1)}, s32[1,352]{1,0:T(1,128)}, u32[]{:S(2)}) copy-start(s32[1,352]{1,0:T(1,128)} %param.41) | copy-start | bytes 4228
  49.0 5.8 %copy-start.44 = (pred[16]{0:T(512)(128)(4,1)}, pred[16]{0:T(512)(128)(4,1)S(1)}, u32[]{:S(2)}) copy-start(pred[16]{0:T(512)(128)(4,1)S(1)} %get-tuple-element.19) | copy-start | bytes 52
  49.9 35.3 %collective-permute-start = (f32[1,1280]{1,0:T(1,128)S(1)}, f32[1,1280]{1,0:T(1,128)S(1)}, u32[]{:S(2)}, u32[]{:S(2)}) collective-permute-start(f32[1,1280]{1,0:T(1,128)S(1)} %slice.64), channel_id=1, source_target_pairs={{0,16},{1,17},{2,18},{3,19},{4,20},{5,21},{6,22},{7,23},{8,24},{9,... | collective-permute-start | bytes 15368 | tf_op jit(solution)/shard_map/ppermute | solution.py:21
  55.6 29.8 %collective-permute-start.1 = (f32[1,1280]{1,0:T(1,128)}, f32[1,1280]{1,0:T(1,128)S(1)}, u32[]{:S(2)}, u32[]{:S(2)}) collective-permute-start(f32[1,1280]{1,0:T(1,128)} %slice.66), channel_id=1, source_target_pairs={{16,0},{17,1},{18,2},{19,3},{20,4},{21,5},{22,6},{23,7},{24,8},{25... | collective-permute-start | bytes 15368 | tf_op jit(solution)/shard_map/ppermute | solution.py:22
  58.3 27.2 %collective-permute-start.2 = (f32[1,1280]{1,0:T(1,128)}, f32[1,1280]{1,0:T(1,128)S(1)}, u32[]{:S(2)}, u32[]{:S(2)}) collective-permute-start(f32[1,1280]{1,0:T(1,128)} %slice.68), channel_id=1, source_target_pairs={{0,1},{1,2},{2,3},{3,4},{4,5},{5,6},{6,7},{7,8},{8,9},{9,10},{10,1... | collective-permute-start | bytes 15368 | tf_op jit(solution)/shard_map/ppermute | solution.py:21
  59.0 12.1 %copy-start.60 = (s32[1,80]{1,0:T(1,128)S(1)}, s32[1,80]{1,0:T(1,128)}, u32[]{:S(2)}) copy-start(s32[1,80]{1,0:T(1,128)} %param.45) | copy-start | bytes 964
  59.0 13.2 %copy-start.55 = (s32[1,352]{1,0:T(1,128)S(1)}, s32[1,352]{1,0:T(1,128)}, u32[]{:S(2)}) copy-start(s32[1,352]{1,0:T(1,128)} %param.43) | copy-start | bytes 4228
  59.0 13.8 %copy-start.33 = (s32[6,128]{1,0:T(8,128)S(1)}, s32[6,128]{1,0:T(8,128)}, u32[]{:S(2)}) copy-start(s32[6,128]{1,0:T(8,128)} %param.38) | copy-start | bytes 9220
  59.8 26.0 %collective-permute-start.3 = (f32[1,1280]{1,0:T(1,128)}, f32[1,1280]{1,0:T(1,128)S(1)}, u32[]{:S(2)}, u32[]{:S(2)}) collective-permute-start(f32[1,1280]{1,0:T(1,128)} %slice.70), channel_id=1, source_target_pairs={{1,0},{2,1},{3,2},{4,3},{5,4},{6,5},{7,6},{8,7},{9,8},{10,9},{11,1... | collective-permute-start | bytes 15368 | tf_op jit(solution)/shard_map/ppermute | solution.py:22
  64.3 9.1 %copy-start.40 = (pred[352]{0:T(512)(128)(4,1)}, pred[352]{0:T(512)(128)(4,1)S(1)}, u32[]{:S(2)}) copy-start(pred[352]{0:T(512)(128)(4,1)S(1)} %compare_and_fusion.3) | copy-start | bytes 1060
  66.0 8.4 %copy-start.27 = (f32[75,128]{1,0:T(8,128)S(1)}, f32[75,128]{1,0:T(8,128)}, u32[]{:S(2)}) copy-start(f32[75,128]{1,0:T(8,128)} %param.34) | copy-start | bytes 115204
  66.8 19.1 %all-to-all-start = ((f32[80,16,22]{0,2,1:T(8,128)}), f32[80,16,22]{0,2,1:T(8,128)}, u32[]{:S(2)}, u32[]{:S(2)}) async-start(f32[80,16,22]{0,2,1:T(8,128)} %all_to_all.24), calls=%async_computation | async-start | bytes 393216 | tf_op jit(solution)/shard_map/all_to_all | solution.py:259
  71.0 4.0 %copy-start.56 = (s32[1,352]{1,0:T(1,128)S(1)}, s32[1,352]{1,0:T(1,128)}, u32[]{:S(2)}) copy-start(s32[1,352]{1,0:T(1,128)} %param.44) | copy-start | bytes 4228
  71.0 4.6 %copy-start.57 = (s32[1,352]{1,0:T(1,128)S(1)}, s32[1,352]{1,0:T(1,128)}, u32[]{:S(2)}) copy-start(s32[1,352]{1,0:T(1,128)} %param.42) | copy-start | bytes 4228
  76.3 4.3 %copy-start.39 = (s32[1024]{0:T(1024)}, s32[1024]{0:T(1024)S(1)}, u32[]{:S(2)}) copy-start(s32[1024]{0:T(1024)S(1)} %pad_clamp_fusion.2) | copy-start | bytes 12292
  76.9 5.8 %copy-start.29 = (s32[1024]{0:T(1024)}, s32[1024]{0:T(1024)S(1)}, u32[]{:S(2)}) copy-start(s32[1024]{0:T(1024)S(1)} %pad_clamp_fusion.1) | copy-start | bytes 12292
  76.9 5.7 %copy-start.52 = (pred[80]{0:T(512)(128)(4,1)S(1)}, pred[80]{0:T(512)(128)(4,1)}, u32[]{:S(2)}) copy-start(pred[80]{0:T(512)(128)(4,1)} %compare_and_fusion.2) | copy-start | bytes 244
  86.0 14.9 %all-to-all-start.1 = ((f32[80,16,22]{0,2,1:T(8,128)}), f32[80,16,22]{0,2,1:T(8,128)S(1)}, u32[]{:S(2)}, u32[]{:S(2)}) async-start(f32[80,16,22]{0,2,1:T(8,128)} %all_to_all.26), calls=%async_computation.1 | async-start | bytes 393216 | tf_op jit(solution)/shard_map/all_to_all | solution.py:260
  91.9 11.5 %copy-start.21 = (f32[4,16,16,1]{2,1,0,3:T(8,128)S(1)}, f32[4,16,16,1]{2,1,0,3:T(8,128)}, u32[]{:S(2)}) copy-start(f32[4,16,16,1]{2,1,0,3:T(8,128)} %constant.87) | copy-start | bytes 12292
  106.5 3.8 %copy-start.6 = (f32[5,16,6,128]{3,2,1,0:T(8,128)S(1)}, f32[5,16,6,128]{3,2,1,0:T(8,128)}, u32[]{:S(2)}) copy-start(f32[5,16,6,128]{3,2,1,0:T(8,128)} %copy-done.5) | copy-start | bytes 737284
  106.5 3.8 %copy-start.34 = (pred[768]{0:T(1024)(128)(4,1)S(1)}, pred[768]{0:T(1024)(128)(4,1)}, u32[]{:S(2)}) copy-start(pred[768]{0:T(1024)(128)(4,1)} %compare_and_fusion) | copy-start | bytes 2308
  109.1 4.1 %copy-start.17 = (f32[64,6,16,1]{0,2,1,3:T(8,128)S(1)}, f32[64,6,16,1]{0,2,1,3:T(8,128)}, u32[]{:S(2)}) copy-start(f32[64,6,16,1]{0,2,1,3:T(8,128)} %constant.88) | copy-start | bytes 73732
  110.3 4.2 %copy-start.12 = (f32[320,128]{1,0:T(8,128)S(1)}, f32[320,128]{1,0:T(8,128)}, u32[]{:S(2)}) copy-start(f32[320,128]{1,0:T(8,128)} %param.32) | copy-start | bytes 491524
  114.5 45.0 %copy-start.20 = (f32[6,16,64,1]{2,1,0,3:T(8,128)S(1)}, f32[6,16,64,1]{2,1,0,3:T(8,128)}, u32[]{:S(2)}) copy-start(f32[6,16,64,1]{2,1,0,3:T(8,128)} %constant.85) | copy-start | bytes 73732
  167.7 5.0 %copy-start.45 = (pred[16]{0:T(512)(128)(4,1)S(1)}, pred[16]{0:T(512)(128)(4,1)}, u32[]{:S(2)}) copy-start(pred[16]{0:T(512)(128)(4,1)} %copy-done.44) | copy-start | bytes 52
  167.7 5.0 %copy-start.47 = (pred[16]{0:T(512)(128)(4,1)S(1)}, pred[16]{0:T(512)(128)(4,1)}, u32[]{:S(2)}) copy-start(pred[16]{0:T(512)(128)(4,1)} %copy-done.46) | copy-start | bytes 52
  167.7 11.0 %copy-start.49 = (pred[16]{0:T(512)(128)(4,1)S(1)}, pred[16]{0:T(512)(128)(4,1)}, u32[]{:S(2)}) copy-start(pred[16]{0:T(512)(128)(4,1)} %copy-done.48) | copy-start | bytes 52
  167.7 11.0 %copy-start.51 = (pred[16]{0:T(512)(128)(4,1)S(1)}, pred[16]{0:T(512)(128)(4,1)}, u32[]{:S(2)}) copy-start(pred[16]{0:T(512)(128)(4,1)} %copy-done.50) | copy-start | bytes 52
  171.4 12.3 %copy-start.14 = (f32[352,80]{1,0:T(8,128)S(1)}, f32[352,80]{1,0:T(8,128)}, u32[]{:S(2)}) copy-start(f32[352,80]{1,0:T(8,128)} %gather_fusion.12) | copy-start | bytes 337924
  171.4 12.3 %copy-start.41 = (pred[352]{0:T(512)(128)(4,1)S(1)}, pred[352]{0:T(512)(128)(4,1)}, u32[]{:S(2)}) copy-start(pred[352]{0:T(512)(128)(4,1)} %copy-done.40) | copy-start | bytes 1060
  171.4 16.6 %copy-start.53 = (pred[80]{0:T(512)(128)(4,1)S(1)}, pred[80]{0:T(512)(128)(4,1)}, u32[]{:S(2)}) copy-start(pred[80]{0:T(512)(128)(4,1)} %compare_and_fusion.2) | copy-start | bytes 244
  171.4 16.7 %copy-start.30 = (s32[1024]{0:T(1024)S(1)}, s32[1024]{0:T(1024)}, u32[]{:S(2)}) copy-start(s32[1024]{0:T(1024)} %copy-done.29) | copy-start | bytes 12292
  172.7 16.5 %copy-start.43 = (pred[352]{0:T(512)(128)(4,1)S(1)}, pred[352]{0:T(512)(128)(4,1)}, u32[]{:S(2)}) copy-start(pred[352]{0:T(512)(128)(4,1)} %compare_and_fusion.1) | copy-start | bytes 1060
  173.0 17.1 %collective-permute-start.4 = (f32[1,1280]{1,0:T(1,128)S(1)}, f32[1,1280]{1,0:T(1,128)S(1)}, u32[]{:S(2)}, u32[]{:S(2)}) collective-permute-start(f32[1,1280]{1,0:T(1,128)S(1)} %slice.73), channel_id=1, source_target_pairs={{0,16},{1,17},{2,18},{3,19},{4,20},{5,21},{6,22},{7,23},{8,24},{9,... | collective-permute-start | bytes 15368 | tf_op jit(solution)/shard_map/ppermute | solution.py:21
  177.4 12.9 %collective-permute-start.5 = (f32[1,1280]{1,0:T(1,128)S(1)}, f32[1,1280]{1,0:T(1,128)S(1)}, u32[]{:S(2)}, u32[]{:S(2)}) collective-permute-start(f32[1,1280]{1,0:T(1,128)S(1)} %slice.74), channel_id=1, source_target_pairs={{16,0},{17,1},{18,2},{19,3},{20,4},{21,5},{22,6},{23,7},{24,8},{25... | collective-permute-start | bytes 15368 | tf_op jit(solution)/shard_map/ppermute | solution.py:22
  179.0 11.5 %collective-permute-start.6 = (f32[1,1280]{1,0:T(1,128)S(1)}, f32[1,1280]{1,0:T(1,128)S(1)}, u32[]{:S(2)}, u32[]{:S(2)}) collective-permute-start(f32[1,1280]{1,0:T(1,128)S(1)} %slice.75), channel_id=1, source_target_pairs={{0,1},{1,2},{2,3},{3,4},{4,5},{5,6},{6,7},{7,8},{8,9},{9,10},{10,1... | collective-permute-start | bytes 15368 | tf_op jit(solution)/shard_map/ppermute | solution.py:21
  179.2 11.4 %collective-permute-start.7 = (f32[1,1280]{1,0:T(1,128)S(1)}, f32[1,1280]{1,0:T(1,128)S(1)}, u32[]{:S(2)}, u32[]{:S(2)}) collective-permute-start(f32[1,1280]{1,0:T(1,128)S(1)} %slice.76), channel_id=1, source_target_pairs={{1,0},{2,1},{3,2},{4,3},{5,4},{6,5},{7,6},{8,7},{9,8},{10,9},{11,1... | collective-permute-start | bytes 15368 | tf_op jit(solution)/shard_map/ppermute | solution.py:22
  184.5 12.5 %all-to-all-start.2 = ((f32[80,16,22]{0,2,1:T(8,128)}), f32[80,16,22]{0,2,1:T(8,128)S(1)}, u32[]{:S(2)}, u32[]{:S(2)}) async-start(f32[80,16,22]{0,2,1:T(8,128)} %all_to_all.28), calls=%async_computation.2 | async-start | bytes 393216 | tf_op jit(solution)/shard_map/all_to_all | solution.py:259
  189.3 12.2 %copy-start.23 = (f32[4,16,16,1]{2,1,0,3:T(8,128)S(1)}, f32[4,16,16,1]{2,1,0,3:T(8,128)}, u32[]{:S(2)}) copy-start(f32[4,16,16,1]{2,1,0,3:T(8,128)} %constant.86) | copy-start | bytes 12292
  189.3 12.2 %copy-start.24 = (f32[4,352]{1,0:T(4,128)S(1)}, f32[4,352]{1,0:T(4,128)}, u32[]{:S(2)}) copy-start(f32[4,352]{1,0:T(4,128)} %fusion.27) | copy-start | bytes 16900
  197.0 12.5 %all-to-all-start.3 = ((f32[80,16,22]{0,2,1:T(8,128)}), f32[80,16,22]{0,2,1:T(8,128)S(1)}, u32[]{:S(2)}, u32[]{:S(2)}) async-start(f32[80,16,22]{0,2,1:T(8,128)} %all_to_all.30), calls=%async_computation.3 | async-start | bytes 393216 | tf_op jit(solution)/shard_map/all_to_all | solution.py:260
  200.7 9.4 %copy-start.22 = (f32[4,16,16,1]{2,1,0,3:T(8,128)S(1)}, f32[4,16,16,1]{2,1,0,3:T(8,128)}, u32[]{:S(2)}) copy-start(f32[4,16,16,1]{2,1,0,3:T(8,128)} %constant.87) | copy-start | bytes 12292
  201.1 9.7 %copy-start.26 = (s32[352]{0:T(512)S(1)}, s32[352]{0:T(512)}, u32[]{:S(2)}) copy-start(s32[352]{0:T(512)} %copy-done.25) | copy-start | bytes 4228
  201.4 9.8 %copy-start.28 = (s32[1024]{0:T(1024)S(1)}, s32[1024]{0:T(1024)}, u32[]{:S(2)}) copy-start(s32[1024]{0:T(1024)} %pad_clamp_fusion) | copy-start | bytes 12292
  (25 other events, 42.1 us)
where the time goes:
time: 265 us; the launch traced here: 264 us
  blocking collectives  119 us (45%)
  local copies, waits for them, and re-layouts  40.4 us (15%)
  starting transfers between devices  37.3 us (14%)
  matrix products  24.4 us (9%)
  waiting for transfers between devices  19.1 us (7%)
  other arithmetic  12.4 us (5%)
  between operations  10.7 us (4%)
    psum x3, blocking collectives, merged_global(): return lax.psum(partial_values, ('gx', 'yz'))  119 us
    all_to_all x2, waiting for transfers between devices, on_device(): lax.all_to_all(outgoing, 'yz', split_axis=1, concat_axis=1, tiled=True)  12.9 us
    ppermute x4, starting transfers between devices, with_halo(): after = lax.ppermute(leading, axis, down)  11.5 us
    all_to_all x2, starting transfers between devices, on_device(): lax.all_to_all(outgoing, 'yz', split_axis=1, concat_axis=1, tiled=True)  9.68 us
    ppermute x4, starting transfers between devices, with_halo(): before = lax.ppermute(last, axis, up)  8.41 us
    all_to_all x2, starting transfers between devices, on_device(): lax.all_to_all(fine_send, 'yz', split_axis=1, concat_axis=1, tiled=True)  7.7 us
    dot_general x2, matrix products, jacobian(): jnp.einsum('dabe,bne->dane', flux_blocks, nodal_view, precision=maximum_d...  7.32 us
    all_to_all x2, waiting for transfers between devices, on_device(): lax.all_to_all(fine_send, 'yz', split_axis=1, concat_axis=1, tiled=True)  6.14 us
  transfers between devices with their start and end apart: 12, of which 3 were waited for; matrix products, arithmetic and copies ran while one was open for 10% of the time, Pallas kernels for 0%

commit v1 on v0

v1 whole, which is shorter than its diff:
```python
import functools

import jax
import jax.numpy as jnp
import numpy as np
from jax import lax
from jax.experimental import pallas as pl
from jax.experimental.pallas import tpu as pltpu
from jax.sharding import PartitionSpec as P

EPS = 1e-06
NODES = 4
VARS = 5
TILE = VARS * NODES * NODES
DOFS = TILE * NODES
FACES = 6
HALF = 32
K2_SCALE = 2.0**-20
F32 = jnp.float32
BF16 = jnp.bfloat16


def gll_tables():
    root = 1.0 / np.sqrt(5.0)
    points = np.array([-1.0, -root, root, 1.0])
    weights = np.array([1.0, 5.0, 5.0, 1.0]) / 6.0

    def lagrange(at):
        values = np.ones((len(at), 4))
        for j in range(4):
            for m in range(4):
                if m != j:
                    values[:, j] = values[:, j] * (at - points[m]) / (points[j] - points[m])
        return values

    derivative = np.zeros((4, 4))
    for i in range(4):
        for j in range(4):
            total = 0.0
            for m in range(4):
                if m != j:
                    term = 1.0 / (points[j] - points[m])
                    for n in range(4):
                        if n != j and n != m:
                            term = term * (points[i] - points[n]) / (points[j] - points[n])
                    total = total + term
            derivative[i, j] = total
    halves = [lagrange((points - 1.0) / 2.0), lagrange((points + 1.0) / 2.0)]
    projections = [0.5 * (1.0 / weights)[:, None] * h.T * weights[None, :] for h in halves]
    interpolate = [np.kron(halves[q // 2], halves[q % 2]) for q in range(4)]
    project = [np.kron(projections[q // 2], projections[q % 2]) for q in range(4)]
    return derivative, interpolate, project


def pieces(matrix):
    value = np.asarray(matrix, np.float32)
    high = value.astype(jnp.bfloat16)
    low = (value - high.astype(np.float32)).astype(jnp.bfloat16)
    return high, low


def constant_matrices():
    derivative, interpolate, project = gll_tables()
    eye_vars = np.eye(VARS)
    blocks = [np.kron(eye_vars, m) for m in project + interpolate] + [np.eye(TILE)]
    tiles = np.concatenate(pieces(np.concatenate(blocks, axis=1)), axis=0)
    eye = np.eye(4)
    volume = np.concatenate(
        [
            np.kron(derivative, np.kron(eye, eye)),
            np.kron(eye, np.kron(derivative, eye)),
            np.kron(eye, np.kron(eye, derivative)),
        ],
        axis=1,
    )
    volume = np.concatenate(pieces(volume), axis=0)
    return jnp.asarray(tiles), jnp.asarray(volume)


def split(x):
    high = x.astype(BF16)
    low = (x - high.astype(F32)).astype(BF16)
    return high, low


def mm(a, b):
    return jnp.dot(a, b, preferred_element_type=F32)


def mm3(a_high, a_low, b):
    columns = b.shape[1]
    b_high, b_low = split(b)
    first = mm(a_high, jnp.concatenate([b_high, b_low], axis=1))
    return first[:, :columns] + (first[:, columns:] + mm(a_low, b_high))


def solve_cells(x, first_ref, final_ref, mid_ref):
    inner = mm3(first_ref[0], first_ref[1], x)
    return mm3(final_ref[0], final_ref[1], mid_ref[...] * inner)


def face_rows(ref, face):
    end = NODES - 1 if face % 2 else 0
    if face // 2 == 0:
        return jnp.concatenate(
            [ref[pl.ds(a * 64 + end * 16, 16), :] for a in range(VARS)], axis=0
        )
    if face // 2 == 1:
        return jnp.concatenate(
            [ref[pl.ds(g * 16 + end * 4, 4), :] for g in range(VARS * 4)], axis=0
        )
    return ref[pl.ds(end, TILE, stride=4), :]


def add_to_face(ref, face, value):
    end = NODES - 1 if face % 2 else 0
    if face // 2 == 0:
        for a in range(VARS):
            ref[pl.ds(a * 64 + end * 16, 16), :] += value[a * 16 : a * 16 + 16]
    elif face // 2 == 1:
        for g in range(VARS * 4):
            ref[pl.ds(g * 16 + end * 4, 4), :] += value[g * 4 : g * 4 + 4]
    else:
        ref[pl.ds(end, TILE, stride=4), :] += value


def all_traces(ref):
    return jnp.concatenate([face_rows(ref, f) for f in range(FACES)], axis=1)


def two_pieces(x):
    high, low = split(x)
    return jnp.concatenate([high, low], axis=0)


def one_hot(condition):
    return jnp.where(condition, 1.0, 0.0).astype(BF16)


def lane_row(length):
    return lax.broadcasted_iota(jnp.int32, (1, length), 1)


def pack_send(field_ref, send_hot_ref, codes, tiles_ref, send_ref, slab_ref):
    groups = send_ref.shape[0]
    lanes = groups * 2 * HALF
    gathered = mm(two_pieces(all_traces(field_ref)), send_hot_ref[...])
    high, low = gathered[:TILE], gathered[TILE:]
    slab_ref[...] = high[:, lanes:] + low[:, lanes:]
    high, low = high[:, :lanes].astype(BF16), low[:, :lanes].astype(BF16)
    masks = [one_hot(codes == q) for q in range(9)]
    high_stack = jnp.concatenate([high * m for m in masks], axis=0)
    low_stack = jnp.concatenate([low * m for m in masks], axis=0)
    result = mm(tiles_ref[...], high_stack)
    result = result[:TILE] + (result[TILE:] + mm(tiles_ref[:TILE], low_stack))
    left = lane_row(128) < 2 * HALF
    middle = TILE // 2
    for pair in range(groups // 2):
        block = result[:, pair * 128 : pair * 128 + 128]
        top, bottom = block[:middle], block[middle:]
        send_ref[2 * pair] = jnp.where(left, top, pltpu.roll(bottom, 64, 1))
        send_ref[2 * pair + 1] = jnp.where(left, pltpu.roll(top, 64, 1), bottom)


def unpack_received(recv_ref):
    left = lane_row(128) < 2 * HALF
    blocks = []
    for pair in range(recv_ref.shape[0] // 2):
        even, odd = recv_ref[2 * pair], recv_ref[2 * pair + 1]
        top = jnp.where(left, even, pltpu.roll(odd, 64, 1))
        bottom = jnp.where(left, pltpu.roll(even, 64, 1), odd)
        blocks.append(jnp.concatenate([top, bottom], axis=0))
    return jnp.concatenate(blocks, axis=1)


def place_lanes(rows, groups, cap):
    lane = lane_row(groups * 2 * HALF)
    within = lane % HALF
    target = jnp.where(within < cap, (lane // (2 * HALF)) * cap + within, -1)
    slots = lax.broadcasted_iota(jnp.int32, (rows.shape[1], lane.shape[1]), 0)
    return mm(rows, one_hot(slots == target))


def index_tables(
    place, devices, cap, halo, hang, elements, small, outq, inc, inq, coarse, band, plane
):
    gx_index, gx_size, yz_index, groups = devices
    traces = FACES * elements
    as_f = lambda x: x.astype(F32)
    coarse_hot = one_hot(
        lax.broadcasted_iota(jnp.int32, (hang, inc.shape[1]), 0) == inc
    )
    high, low = coarse // 8, coarse % 8
    pad = jnp.zeros((6, hang), F32)
    pick = mm(jnp.concatenate([as_f(high), as_f(low), pad], axis=0).astype(BF16), coarse_hot)
    rows = jnp.concatenate(
        [
            as_f(small // 8),
            as_f(small % 8),
            jnp.where(inc < hang, pick[0:1], float(traces // 8)),
            jnp.where(inc < hang, pick[1:2], 0.0),
            as_f(outq),
            as_f(inq),
            as_f(inc),
            jnp.zeros_like(pick[0:1]),
        ],
        axis=0,
    ).astype(BF16)
    placed = place_lanes(rows, groups, cap).astype(jnp.int32)
    lane = lane_row(groups * 2 * HALF)
    group, within, second = lane // (2 * HALF), lane % HALF, (lane // HALF) % 2
    is_slot = within < cap
    step = halo // 2
    side = (within >= cap) & (within < cap + step)
    position = within - cap + step * second
    up = lax.rem(yz_index + 1, groups)
    down = lax.rem(yz_index + groups - 1, groups)
    lower_columns = jnp.zeros_like(lane) + traces
    upper_columns = lower_columns
    for j in range(halo):
        lower_columns = jnp.where(position == j, 2 * elements + band[0, 0, j], lower_columns)
        upper_columns = jnp.where(position == j, 3 * elements + band[0, 1, j], upper_columns)
    side_send = jnp.where(
        group == up, upper_columns, jnp.where(group == down, lower_columns, traces)
    )
    fine_id = placed[0:1] * 8 + placed[1:2]
    coarse_id = placed[2:3] * 8 + placed[3:4]
    slot_id = jnp.where(second == 0, fine_id, coarse_id)
    send_id = jnp.where(is_slot, slot_id, jnp.where(side, side_send, traces))
    codes = jnp.where(
        is_slot, jnp.where(second == 0, placed[4:5], 4 + placed[5:6]), 8
    )
    slab_lane = lane_row(128)
    slab_id = jnp.zeros_like(slab_lane) + traces
    for j in range(halo):
        slab_id = jnp.where(slab_lane == j, plane[0, 0, j], slab_id)
        slab_id = jnp.where(slab_lane == halo + j, elements + plane[0, 1, j], slab_id)
    send_id = jnp.concatenate([send_id, slab_id], axis=1)

    first_hang = traces + 4 * halo
    side_recv = jnp.where(
        group == down,
        traces + 2 * halo + position,
        jnp.where(group == up, traces + 3 * halo + position, -1),
    )
    mortar = placed[6:7]
    fine_recv = jnp.where(mortar < hang, first_hang + mortar, -1)
    reply_recv = first_hang + hang + group * cap + within
    recv_id = jnp.where(
        is_slot, jnp.where(second == 0, fine_recv, reply_recv), jnp.where(side, side_recv, -1)
    )
    from_upper = (slab_lane < halo) & (gx_index < gx_size - 1)
    from_lower = (slab_lane >= halo) & (slab_lane < 2 * halo) & (gx_index > 0)
    slab_recv = jnp.where(
        from_upper,
        traces + halo + slab_lane,
        jnp.where(from_lower, traces + slab_lane - halo, -1),
    )
    recv_id = jnp.concatenate([recv_id, slab_recv], axis=1)
    return send_id, codes, recv_id


def start_kernel(
    gx_size,
    source_ref,
    first_ref,
    final_ref,
    mid_ref,
    small_ref,
    outq_ref,
    inc_ref,
    inq_ref,
    coarse_ref,
    band_ref,
    plane_ref,
    where_ref,
    tiles_ref,
    field_ref,
    send_ref,
    slab_ref,
    send_hot_ref,
    codes_ref,
    recv_id_ref,
    first_out_ref,
    final_out_ref,
):
    elements = source_ref.shape[1]
    groups = send_ref.shape[0]
    for ref, out in ((first_ref, first_out_ref), (final_ref, final_out_ref)):
        out[0], out[1] = split(ref[...])
    field_ref[...] = solve_cells(source_ref[...], first_out_ref, final_out_ref, mid_ref)
    send_id, codes, recv_id = index_tables(
        None,
        (where_ref[0], gx_size, where_ref[1], groups),
        small_ref.shape[1] // groups,
        band_ref.shape[2],
        coarse_ref.shape[1],
        elements,
        small_ref[...],
        outq_ref[...],
        inc_ref[...],
        inq_ref[...],
        coarse_ref[...],
        band_ref,
        plane_ref,
    )
    columns = lax.broadcasted_iota(jnp.int32, (FACES * elements, send_id.shape[1]), 0)
    send_hot_ref[...] = one_hot(columns == send_id)
    codes_ref[...] = jnp.broadcast_to(codes, codes_ref.shape)
    recv_id_ref[...] = jnp.broadcast_to(recv_id, recv_id_ref.shape)
    pack_send(field_ref, send_hot_ref, codes, tiles_ref, send_ref, slab_ref)


def local_part(
    field_ref, mass_ref, coupling_ref, flux_ref, adjacent_ref, volume_ref, local_ref
):
    elements = field_ref.shape[1]
    traces = all_traces(field_ref)
    columns = lax.broadcasted_iota(jnp.int32, (FACES * elements, elements), 0)
    stacked = two_pieces(traces)
    parts = []
    for a in range(VARS):
        flux = []
        for d in range(3):
            total = None
            for b in range(VARS):
                row = d * 25 + a * VARS + b
                term = flux_ref[row : row + 1, :] * field_ref[b * 64 : b * 64 + 64, :]
                total = term if total is None else total + term
            flux.append(total)
        parts.append(jnp.concatenate(flux, axis=0))
    derived = mm3(volume_ref[:64], volume_ref[64:], jnp.concatenate(parts, axis=1))
    for a in range(VARS):
        rows = slice(a * 64, a * 64 + 64)
        local_ref[rows, :] = (
            mass_ref[rows, :] * field_ref[rows, :]
            + derived[:, a * elements : (a + 1) * elements]
        )
    for f in range(FACES):
        near = mm(stacked, one_hot(columns == adjacent_ref[f : f + 1, :]))
        near = near[:TILE] + near[TILE:]
        own = traces[:, f * elements : (f + 1) * elements]
        add_to_face(
            local_ref, f, coupling_ref[f * TILE : (f + 1) * TILE, :] * (own - near)
        )


def first_local_kernel(
    field_ref,
    mass_ref,
    coupling_ref,
    flux_ref,
    adjacent_ref,
    volume_ref,
    recv_id_ref,
    local_ref,
    recv_hot_ref,
):
    local_part(field_ref, mass_ref, coupling_ref, flux_ref, adjacent_ref, volume_ref, local_ref)
    elements = field_ref.shape[1]
    ids = jnp.transpose(recv_id_ref[...])[:, 0:1]
    for f in range(FACES):
        recv_hot_ref[:, f * elements : (f + 1) * elements] = one_hot(
            ids == adjacent_ref[f : f + 1, :]
        )


def total_of(x):
    return jnp.sum(jnp.sum(x, axis=0, keepdims=True), axis=1, keepdims=True)


def put(values):
    lane = lane_row(128)
    row = jnp.zeros((1, 128), F32)
    for position, value in values:
        row = jnp.where(lane == position, value, row)
    return row


def second_local_kernel(
    field_ref,
    mass_ref,
    coupling_ref,
    flux_ref,
    adjacent_ref,
    volume_ref,
    start_ref,
    local_ref,
    partial_ref,
):
    local_part(field_ref, mass_ref, coupling_ref, flux_ref, adjacent_ref, volume_ref, local_ref)
    k0, k1 = start_ref[...], field_ref[...]
    partial_ref[...] = put(
        [(0, total_of(k0 * k0)), (1, total_of(k0 * k1)), (2, total_of(k1 * k1))]
    )


def finish_product(
    recv_ref, slab_ref, recv_hot_ref, coupling_ref, local_ref, first_ref, final_ref, mid_ref, work_ref
):
    elements = local_ref.shape[1]
    received = jnp.concatenate([unpack_received(recv_ref), slab_ref[...]], axis=1)
    near = mm(two_pieces(received), recv_hot_ref[...])
    near = near[:TILE] + near[TILE:]
    work_ref[...] = local_ref[...]
    for f in range(FACES):
        add_to_face(
            work_ref,
            f,
            -coupling_ref[f * TILE : (f + 1) * TILE, :] * near[:, f * elements : (f + 1) * elements],
        )
    return solve_cells(work_ref[...], first_ref, final_ref, mid_ref)


def middle_kernel(
    recv_ref,
    slab_in_ref,
    recv_hot_ref,
    coupling_ref,
    local_ref,
    first_ref,
    final_ref,
    mid_ref,
    send_hot_ref,
    codes_ref,
    tiles_ref,
    field_ref,
    send_ref,
    slab_ref,
    work_ref,
):
    field_ref[...] = finish_product(
        recv_ref, slab_in_ref, recv_hot_ref, coupling_ref, local_ref, first_ref, final_ref, mid_ref, work_ref
    )
    pack_send(field_ref, send_hot_ref, codes_ref[0:1, :], tiles_ref, send_ref, slab_ref)


def last_kernel(
    recv_ref,
    slab_in_ref,
    recv_hot_ref,
    coupling_ref,
    local_ref,
    first_ref,
    final_ref,
    mid_ref,
    start_ref,
    field_ref,
    partial_ref,
    out_ref,
    work_ref,
):
    k2 = K2_SCALE * finish_product(
        recv_ref, slab_in_ref, recv_hot_ref, coupling_ref, local_ref, first_ref, final_ref, mid_ref, work_ref
    )
    row = partial_ref[...] + put(
        [
            (3, total_of(k2 * start_ref[...])),
            (4, total_of(k2 * field_ref[...])),
            (5, total_of(k2 * k2)),
        ]
    )
    out_ref[...] = jnp.broadcast_to(row.reshape(1, 1, 128), out_ref.shape)


def combine_kernel(rows_ref, start_ref, field_ref, out_ref):
    totals = jnp.sum(rows_ref[:, 0, :], axis=0, keepdims=True)
    lane = lane_row(128)
    g00, g01, g11, g02, g12, g22 = [
        jnp.sum(jnp.where(lane == i, totals, 0.0), axis=1, keepdims=True) for i in range(6)
    ]
    scale = 1.0 / K2_SCALE
    beta = jnp.sqrt(g00 + EPS)
    n00, n01, n11 = g00 / beta / beta, g01 / beta / beta, g11 / beta / beta
    h00 = n01
    w_sq = jnp.maximum(n11 - 2.0 * h00 * n01 + h00 * h00 * n00, 0.0)
    h10 = jnp.sqrt(w_sq + EPS)
    unit = beta * h10
    s = scale / unit
    t = h00 * K2_SCALE
    x0 = (g02 - t * g01) * s / beta
    x1 = ((g12 - t * g11) * s - h00 * ((g02 - t * g01) * s)) / unit
    xx = (((g22 - t * g12) - t * (g12 - t * g11)) * s) * s
    v01 = (n01 - h00 * n00) / h10
    v11 = w_sq / h10 / h10
    h01 = x0
    h11 = x1 - h01 * v01
    rest = xx - 2.0 * h01 * x0 + h01 * h01 * n00
    rest = rest - 2.0 * h11 * h11 + h11 * h11 * v11
    h21 = jnp.sqrt(jnp.maximum(rest, 0.0) + EPS)
    radius0 = jnp.sqrt(h00 * h00 + h10 * h10)
    c0, s0 = h00 / radius0, h10 / radius0
    target1 = -s0 * beta
    target0 = c0 * beta
    upper = c0 * h01 + s0 * h11
    lower = c0 * h11 - s0 * h01
    radius1 = jnp.sqrt(lower * lower + h21 * h21)
    y1 = (lower / radius1) * target1 / radius1
    y0 = (target0 - upper * y1) / radius0
    along1 = y1 / unit
    along0 = y0 / beta - along1 * h00
    out_ref[...] = along0 * start_ref[...] + along1 * field_ref[...]


def vmem(count):
    return [pl.BlockSpec(memory_space=pltpu.VMEM)] * count


def call(kernel, outs, args, smem=(), scratch=(), flops=0):
    specs = [
        pl.BlockSpec(memory_space=pltpu.SMEM if i in smem else pltpu.VMEM)
        for i in range(len(args))
    ]
    return pl.pallas_call(
        kernel,
        out_shape=outs,
        in_specs=specs,
        out_specs=jax.tree.map(lambda _: pl.BlockSpec(memory_space=pltpu.VMEM), outs),
        scratch_shapes=list(scratch),
        cost_estimate=pl.CostEstimate(
            flops=flops, bytes_accessed=sum(a.size * a.dtype.itemsize for a in args), transcendentals=0
        ),
        compiler_params=pltpu.CompilerParams(vmem_limit_bytes=48 * 2**20),
    )(*args)


def on_device(
    source,
    mass,
    coupling,
    flux,
    first,
    final,
    mid,
    adjacent,
    plane,
    band,
    small,
    proprietor,
    outq,
    inc,
    inq,
    coarse,
):
    del proprietor
    tiles, volume = constant_matrices()
    gx_size, groups = lax.axis_size("gx"), lax.axis_size("yz")
    elements = source.shape[1]
    traces = FACES * elements
    lanes = groups * 2 * HALF
    struct = jax.ShapeDtypeStruct
    field = struct((DOFS, elements), F32)
    send = struct((groups, TILE // 2, 128), F32)
    slab = struct((TILE, 128), F32)
    where = jnp.stack([lax.axis_index("gx"), lax.axis_index("yz")]).astype(jnp.int32)

    k0, send0, slab0, send_hot, codes, recv_id, first2, final2 = call(
        functools.partial(start_kernel, gx_size),
        (
            field,
            send,
            slab,
            struct((traces, lanes + 128), BF16),
            struct((8, lanes), jnp.int32),
            struct((8, lanes + 128), jnp.int32),
            struct((2, DOFS, DOFS), BF16),
            struct((2, DOFS, DOFS), BF16),
        ),
        (source, first, final, mid, small, outq, inc, inq, coarse, band, plane, where, tiles),
        smem=(9, 10, 11),
        flops=10**9,
    )

    up = [(i, i + 1) for i in range(gx_size - 1)]
    down = [(j, i) for i, j in up]

    def exchange(send, slab):
        if gx_size == 2:
            slab = lax.ppermute(slab, "gx", up + down)
        else:
            halo = plane.shape[2]
            lower = lax.ppermute(slab, "gx", up)
            upper = lax.ppermute(slab, "gx", down)
            slab = jnp.where(lane_row(128) < halo, upper, lower)
        return lax.all_to_all(send, "yz", 0, 0, tiled=True), slab

    recv0, slab0 = exchange(send0, slab0)
    local0, recv_hot = call(
        first_local_kernel,
        (field, struct((lanes + 128, traces), BF16)),
        (k0, mass, coupling, flux, adjacent, volume, recv_id),
        flops=10**9,
    )
    work = pltpu.VMEM((DOFS, elements), F32)
    k1, send1, slab1 = call(
        middle_kernel,
        (field, send, slab),
        (recv0, slab0, recv_hot, coupling, local0, first2, final2, mid, send_hot, codes, tiles),
        scratch=[work],
        flops=10**9,
    )
    recv1, slab1 = exchange(send1, slab1)
    local1, partial = call(
        second_local_kernel,
        (field, struct((1, 128), F32)),
        (k1, mass, coupling, flux, adjacent, volume, k0),
        flops=10**9,
    )
    rows = call(
        last_kernel,
        struct((gx_size * groups, 1, 128), F32),
        (recv1, slab1, recv_hot, coupling, local1, first2, final2, mid, k0, k1, partial),
        scratch=[work],
        flops=10**9,
    )
    rows = lax.all_to_all(rows, ("gx", "yz"), 0, 0, tiled=True)
    return call(combine_kernel, field, (rows, k0, k1), flops=10**6)


def solution(mesh):
    by_column = P(None, ("gx", "yz"))
    by_row = P(("gx", "yz"), None)
    by_plane = P(("gx", "yz"), None, None)
    return jax.shard_map(
        on_device,
        mesh=mesh,
        in_specs=(by_column,) * 4
        + (P(), P())
        + (by_column,) * 2
        + (by_plane,) * 2
        + (by_row,) * 6,
        out_specs=by_column,
        check_vma=False,
    )
```

time: 265 us -> 73.9 us (0.28)
  blocking collectives: 119 us -> 10 us
  matrix products: 24.4 us -> 0 us
  starting transfers between devices: 37.3 us -> 14.1 us
  other arithmetic: 12.4 us -> 0.07 us
  waiting for transfers between devices: 19.1 us -> 6.92 us
  Pallas kernels: 0 us -> 11.5 us
  between operations: 10.7 us -> 0.11 us
  local copies, waits for them, and re-layouts: 40.4 us -> 29.9 us
    psum x3 -> x0, blocking collectives: 119 us -> none  [merged_global(): return lax.psum(partial_values, ('gx', 'yz'))]
    unnamed x134 -> x80, local copies, waits for them, and re-layouts: 3.74 us -> 29.9 us
    dot_general x20 -> x0, matrix products: 24.4 us -> none  [the longest x2 7.32 us: jacobian(): jnp.einsum('dabe,bne->dane', flux_blocks, nodal_view, precision=maximum_d...]
    ppermute x8 -> x2, starting transfers between devices: 19.9 us -> 3.1 us  [exchange(): slab = lax.ppermute(slab, 'gx', up + down)]
    gather x18 -> x0, local copies, waits for them, and re-layouts: 16.7 us -> none  [the longest x4 5.46 us: on_device(): jnp.take(trace_table, near_index, axis=1, mode='fill', fill_value=0.0)]
    all_to_all x4 -> x2, waiting for transfers between devices: 19 us -> 6.92 us  [exchange(): return (lax.all_to_all(send, 'yz', 0, 0, tiled=True), slab)]
    pallas_call x0 -> x6, Pallas kernels: none -> 11.5 us  [call(): pl.pallas_call(kernel, out_shape=outs, in_specs=specs, out_specs=jax.tree...]
    all_to_all x0 -> x1, blocking collectives: none -> 10 us  [on_device(): rows = lax.all_to_all(rows, ('gx', 'yz'), 0, 0, tiled=True)]
  transfers between devices with their start and end apart: 12 -> 4, of which waited for: 3 -> 2; matrix products, arithmetic and copies ran while one was open for 10% -> 0% of each run, Pallas kernels for 0% -> 3%
where the time goes in v1:
time: 73.9 us; the launch traced here: 72.7 us
  local copies, waits for them, and re-layouts  29.9 us (40%)
  starting transfers between devices  14.1 us (19%)
  Pallas kernels  11.5 us (16%)
  blocking collectives  10 us (14%)
  waiting for transfers between devices  6.92 us (9%)
    unnamed x80, local copies, waits for them, and re-layouts  29.9 us
    pallas_call x6, Pallas kernels, call(): pl.pallas_call(kernel, out_shape=outs, in_specs=specs, out_specs=jax.tree...  11.5 us
    all_to_all x2, starting transfers between devices, exchange(): return (lax.all_to_all(send, 'yz', 0, 0, tiled=True), slab)  11 us
    all_to_all x1, blocking collectives, on_device(): rows = lax.all_to_all(rows, ('gx', 'yz'), 0, 0, tiled=True)  10 us
    all_to_all x2, waiting for transfers between devices, exchange(): return (lax.all_to_all(send, 'yz', 0, 0, tiled=True), slab)  6.92 us
    ppermute x2, starting transfers between devices, exchange(): slab = lax.ppermute(slab, 'gx', up + down)  3.1 us
  transfers between devices with their start and end apart: 4, of which 2 were waited for; matrix products, arithmetic and copies ran while one was open for 0% of the time, Pallas kernels for 3%

profile of v1, /device:TPU:0, one launch (start us, length us, event | category | flops | bytes accessed | tf_op | source)
XLA Modules:
  0.0 72.7 jit_solution(4269150009645439951)
XLA Ops:
  0.1 0.9 %copy-done.2 = f32[320,128]{1,0:T(8,128)S(1)} copy-done((f32[320,128]{1,0:T(8,128)S(1)}, f32[320,128]{1,0:T(8,128)}, u32[]{:S(2)}) %copy-start.2) | copy-done | bytes 163864
  1.0 0.9 %copy-done.12 = bf16[160,720]{1,0:T(8,128)(2,1)S(1)} copy-done((bf16[160,720]{1,0:T(8,128)(2,1)S(1)}, bf16[160,720]{1,0:T(8,128)(2,1)}, u32[]{:S(2)}) %copy-start.12) | copy-done | bytes 230424
  1.9 1.0 %copy-done.20 = f32[320,320]{1,0:T(8,128)S(1)} copy-done((f32[320,320]{1,0:T(8,128)S(1)}, f32[320,320]{1,0:T(8,128)}, u32[]{:S(2)}) %copy-start.20) | copy-done | bytes 409624
  3.0 1.0 %copy-done.21 = f32[320,320]{1,0:T(8,128)S(1)} copy-done((f32[320,320]{1,0:T(8,128)S(1)}, f32[320,320]{1,0:T(8,128)}, u32[]{:S(2)}) %copy-start.21) | copy-done | bytes 409624
  4.0 0.9 %copy-done.22 = f32[320,128]{1,0:T(8,128)S(1)} copy-done((f32[320,128]{1,0:T(8,128)S(1)}, f32[320,128]{1,0:T(8,128)}, u32[]{:S(2)}) %copy-start.22) | copy-done | bytes 163864
  4.9 0.7 copy-done.29
  5.6 0.7 copy-done.30
  6.3 0.7 copy-done.31
  7.0 0.7 copy-done.32
  7.6 0.7 copy-done.33
  8.3 0.7 copy-done.34
  9.0 0.7 copy-done.35
  9.7 3.4 %shard_map.163 = (f32[320,128]{1,0:T(8,128)S(1)}, f32[16,40,128]{2,1,0:T(8,128)}, f32[80,128]{1,0:T(8,128)}, bf16[768,1152]{1,0:T(8,128)(2,1)S(1)}, s32[8,1024]{...) custom-call(f32[320,128]{1,0:T(8,128)S(1)} %copy-done.22, ...), custom_call_target="tpu_custom_call" | custom-call | flops 1000000000 | bytes 1383496 | tf_op jit(solution)/shard_map/pallas_call | solution.py:514
  13.0 1.2 %copy-done = bf16[768,1152]{1,0:T(8,128)(2,1)} copy-done((bf16[768,1152]{1,0:T(8,128)(2,1)}, bf16[768,1152]{1,0:T(8,128)(2,1)S(1)}, u32[]{:S(2)}) %copy-start) | copy-done | bytes 1769496
  14.3 0.7 copy-done.4
  16.2 7.4 %all-to-all-start = ((f32[16,40,128]{2,1,0:T(8,128)}), f32[16,40,128]{2,1,0:T(8,128)S(1)}, u32[]{:S(2)}, u32[]{:S(2)}) async-start(f32[16,40,128]{2,1,0:T(8,128)} %get-tuple-element.20), calls=%async_computation | async-start | bytes 655360 | tf_op jit(solution)/shard_map/all_to_all | solution.py:585
  23.6 1.5 %collective-permute-start = (f32[80,128]{1,0:T(8,128)}, f32[80,128]{1,0:T(8,128)S(1)}, u32[]{:S(2)}, u32[]{:S(2)}) collective-permute-start(f32[80,128]{1,0:T(8,128)} %get-tuple-element.21), channel_id=1, source_target_pairs={{0,16},{16,0},{1,17},{17,1},{2,18},{18,2},{3,19},{19,3},{4,20},{20... | collective-permute-start | bytes 122888 | tf_op jit(solution)/shard_map/ppermute | solution.py:579
  25.1 0.9 %copy-done.5 = f32[320,128]{1,0:T(8,128)S(1)} copy-done((f32[320,128]{1,0:T(8,128)S(1)}, f32[320,128]{1,0:T(8,128)}, u32[]{:S(2)}) %copy-start.5) | copy-done | bytes 163864
  26.1 0.9 %copy-done.23 = f32[320,128]{1,0:T(8,128)S(1)} copy-done((f32[320,128]{1,0:T(8,128)S(1)}, f32[320,128]{1,0:T(8,128)}, u32[]{:S(2)}) %copy-start.23) | copy-done | bytes 163864
  27.0 0.8 %copy-done.25 = f32[75,128]{1,0:T(8,128)S(1)} copy-done((f32[75,128]{1,0:T(8,128)S(1)}, f32[75,128]{1,0:T(8,128)}, u32[]{:S(2)}) %copy-start.25) | copy-done | bytes 38424
  27.8 0.8 %copy-done.36 = bf16[128,192]{1,0:T(8,128)(2,1)S(1)} copy-done((bf16[128,192]{1,0:T(8,128)(2,1)S(1)}, bf16[128,192]{1,0:T(8,128)(2,1)}, u32[]{:S(2)}) %copy-start.36) | copy-done | bytes 49176
  28.6 0.8 %copy-done.39 = s32[8,1152]{1,0:T(8,128)S(1)} copy-done((s32[8,1152]{1,0:T(8,128)S(1)}, s32[8,1152]{1,0:T(8,128)}, u32[]{:S(2)}) %copy-start.39) | copy-done | bytes 36888
  29.4 1.3 %shard_map.164 = (f32[320,128]{1,0:T(8,128)S(1)}, bf16[1152,768]{1,0:T(8,128)(2,1)S(1)}) custom-call(f32[320,128]{1,0:T(8,128)S(1)} %copy-done.5, f32[320,128]{1,0:T(8,128)S(1)} %copy-done.23, f32[480,128]{1,0:T(8,128)S(1)} %copy-done.1, f32[75,128]{1,0:T(8,128)S(1)} %copy-done.25, s32[6,128]{1,0:T(8,128)S(1)} %copy-done.28, ...), custom_call_target="tpu_custom_call" | custom-call | flops 1000000000 | bytes 700928 | tf_op jit(solution)/shard_map/pallas_call | solution.py:514
  30.7 0.7 copy-done.14
  31.3 3.3 %all-to-all-done.recv_ref = f32[16,40,128]{2,1,0:T(8,128)S(1)} async-done(((f32[16,40,128]{2,1,0:T(8,128)}), f32[16,40,128]{2,1,0:T(8,128)S(1)}, u32[]{:S(2)}, u32[]{:S(2)}) %all-to-all-start) | async-done | bytes 327712 | tf_op jit(solution)/shard_map/all_to_all | solution.py:585
  34.7 0.9 %copy-done.13 = bf16[160,720]{1,0:T(8,128)(2,1)S(1)} copy-done((bf16[160,720]{1,0:T(8,128)(2,1)S(1)}, bf16[160,720]{1,0:T(8,128)(2,1)}, u32[]{:S(2)}) %copy-start.13) | copy-done | bytes 230424
  35.6 0.9 %copy-done.15 = f32[320,128]{1,0:T(8,128)S(1)} copy-done((f32[320,128]{1,0:T(8,128)S(1)}, f32[320,128]{1,0:T(8,128)}, u32[]{:S(2)}) %copy-start.15) | copy-done | bytes 163864
  36.5 0.8 %copy-done.19 = s32[8,1024]{1,0:T(8,128)S(1)} copy-done((s32[8,1024]{1,0:T(8,128)S(1)}, s32[8,1024]{1,0:T(8,128)}, u32[]{:S(2)}) %copy-start.19) | copy-done | bytes 32792
  37.3 3.8 %shard_map.165 = (f32[320,128]{1,0:T(8,128)S(1)}, f32[16,40,128]{2,1,0:T(8,128)S(1)}, f32[80,128]{1,0:T(8,128)S(1)}) custom-call(f32[16,40,128]{2,1,0:T(8,128)S(1)} %all-to-all-done.recv_ref, f32[80,128]{1,0:T(8,128)S(1)} %collective-permute-done.slab_in_ref, bf16[1152,768]{1,0:T(8,128)(2,1)S(1)} %get-tuple-element.24.recv_hot_ref, ...), custom_call_target="tpu_custom_call" | custom-call | flops 1000000000 | bytes 5563392 | tf_op jit(solution)/shard_map/pallas_call | solution.py:514
  41.1 0.7 copy-done.8
  41.7 0.7 copy-done.11
  42.4 0.6 copy-done.27
  43.1 3.5 %all-to-all-start.1 = ((f32[16,40,128]{2,1,0:T(8,128)}), f32[16,40,128]{2,1,0:T(8,128)S(1)}, u32[]{:S(2)}, u32[]{:S(2)}) async-start(f32[16,40,128]{2,1,0:T(8,128)} %copy-done.11), calls=%async_computation.1 | async-start | bytes 655360 | tf_op jit(solution)/shard_map/all_to_all | solution.py:585
  46.6 1.6 %collective-permute-start.1 = (f32[80,128]{1,0:T(8,128)}, f32[80,128]{1,0:T(8,128)S(1)}, u32[]{:S(2)}, u32[]{:S(2)}) collective-permute-start(f32[80,128]{1,0:T(8,128)} %copy-done.27), channel_id=1, source_target_pairs={{0,16},{16,0},{1,17},{17,1},{2,18},{18,2},{3,19},{19,3},{4,20},{20... | collective-permute-start | bytes 122888 | tf_op jit(solution)/shard_map/ppermute | solution.py:579
  48.2 0.9 %copy-done.6 = f32[320,128]{1,0:T(8,128)S(1)} copy-done((f32[320,128]{1,0:T(8,128)S(1)}, f32[320,128]{1,0:T(8,128)}, u32[]{:S(2)}) %copy-start.6) | copy-done | bytes 163864
  49.1 0.9 %copy-done.9 = f32[320,128]{1,0:T(8,128)S(1)} copy-done((f32[320,128]{1,0:T(8,128)S(1)}, f32[320,128]{1,0:T(8,128)}, u32[]{:S(2)}) %copy-start.9) | copy-done | bytes 163864
  50.0 0.9 %copy-done.24 = f32[320,128]{1,0:T(8,128)S(1)} copy-done((f32[320,128]{1,0:T(8,128)S(1)}, f32[320,128]{1,0:T(8,128)}, u32[]{:S(2)}) %copy-start.24) | copy-done | bytes 163864
  50.9 0.8 %copy-done.26 = f32[75,128]{1,0:T(8,128)S(1)} copy-done((f32[75,128]{1,0:T(8,128)S(1)}, f32[75,128]{1,0:T(8,128)}, u32[]{:S(2)}) %copy-start.26) | copy-done | bytes 38424
  51.7 0.8 %copy-done.37 = bf16[128,192]{1,0:T(8,128)(2,1)S(1)} copy-done((bf16[128,192]{1,0:T(8,128)(2,1)S(1)}, bf16[128,192]{1,0:T(8,128)(2,1)}, u32[]{:S(2)}) %copy-start.37) | copy-done | bytes 49176
  52.5 0.8 %shard_map.166 = (f32[320,128]{1,0:T(8,128)S(1)}, f32[1,128]{1,0:T(1,128)S(1)}) custom-call(f32[320,128]{1,0:T(8,128)S(1)} %copy-done.9, f32[320,128]{1,0:T(8,128)S(1)} %copy-done.24, f32[480,128]{1,0:T(8,128)S(1)} %copy-done.1, f32[75,128]{1,0:T(8,128)S(1)} %copy-done.26, s32[6,128]{1,0:T(8,128)S(1)} %copy-done.28, bf16[128,192]{1,0:T(8,128)(2,1)S(1)} %copy-done.37, ...), custom_call_target="tpu_custom_call" | custom-call | flops 1000000000 | bytes 827904 | tf_op jit(solution)/shard_map/pallas_call | solution.py:514
  53.4 0.7 copy-done.16
  54.1 3.6 %all-to-all-done.1.recv_ref = f32[16,40,128]{2,1,0:T(8,128)S(1)} async-done(((f32[16,40,128]{2,1,0:T(8,128)}), f32[16,40,128]{2,1,0:T(8,128)S(1)}, u32[]{:S(2)}, u32[]{:S(2)}) %all-to-all-start.1) | async-done | bytes 327712 | tf_op jit(solution)/shard_map/all_to_all | solution.py:585
  57.6 0.9 %copy-done.7 = f32[320,128]{1,0:T(8,128)S(1)} copy-done((f32[320,128]{1,0:T(8,128)S(1)}, f32[320,128]{1,0:T(8,128)}, u32[]{:S(2)}) %copy-start.7) | copy-done | bytes 163864
  58.6 0.9 %copy-done.10 = f32[320,128]{1,0:T(8,128)S(1)} copy-done((f32[320,128]{1,0:T(8,128)S(1)}, f32[320,128]{1,0:T(8,128)}, u32[]{:S(2)}) %copy-start.10) | copy-done | bytes 163864
  59.5 0.9 %copy-done.17 = f32[320,128]{1,0:T(8,128)S(1)} copy-done((f32[320,128]{1,0:T(8,128)S(1)}, f32[320,128]{1,0:T(8,128)}, u32[]{:S(2)}) %copy-start.17) | copy-done | bytes 163864
  60.4 1.4 %shard_map.167 = f32[32,1,128]{2,1,0:T(1,128)S(1)} custom-call(f32[16,40,128]{2,1,0:T(8,128)S(1)} %all-to-all-done.1.recv_ref, f32[80,128]{1,0:T(8,128)S(1)} %collective-permute-done.1.slab_in_ref, bf16[1152,768]{1,0:T(8,128)(2,1)S(1)} %get-tuple-element.24.recv_hot_ref, f32[480,128]{1,0:T(8,128)S(1)} %copy-done.1, f32[320,128]{1,0:T(8,128)S(1)} %copy-done.17, ...), custom_call_target="tpu_custom_call" | custom-call | flops 1000000000 | bytes 3858944 | tf_op jit(solution)/shard_map/pallas_call | solution.py:514
  61.8 10.0 %all_to_all.15.rows_ref = f32[32,1,128]{2,1,0:T(1,128)S(1)} all-to-all(f32[32,1,128]{2,1,0:T(1,128)S(1)} %shard_map.167), channel_id=1, replica_groups=mesh['gx'=2,'yz'=16] {'gx','yz'}, dimensions={0} | all-to-all | bytes 32768 | tf_op jit(solution)/shard_map/all_to_all | solution.py:616
  71.8 0.9 %shard_map.168 = f32[320,128]{1,0:T(8,128)} custom-call(f32[32,1,128]{2,1,0:T(1,128)S(1)} %all_to_all.15.rows_ref, f32[320,128]{1,0:T(8,128)S(1)} %copy-done.7, f32[320,128]{1,0:T(8,128)S(1)} %copy-done.10), custom_call_target="tpu_custom_call" | custom-call | flops 1000000 | bytes 344064 | tf_op jit(solution)/shard_map/pallas_call | solution.py:514
  (48 shorter events, 1.4 us)
Async XLA Ops:
  0.1 0.9 %copy-start.2 = (f32[320,128]{1,0:T(8,128)S(1)}, f32[320,128]{1,0:T(8,128)}, u32[]{:S(2)}) copy-start(f32[320,128]{1,0:T(8,128)} %mid_ref.5) | copy-start | bytes 491524
  1.0 0.9 %copy-start.12 = (bf16[160,720]{1,0:T(8,128)(2,1)S(1)}, bf16[160,720]{1,0:T(8,128)(2,1)}, u32[]{:S(2)}) copy-start(bf16[160,720]{1,0:T(8,128)(2,1)} %constant.13.clone.tiles_ref) | copy-start | bytes 691204
  1.9 1.0 %copy-start.20 = (f32[320,320]{1,0:T(8,128)S(1)}, f32[320,320]{1,0:T(8,128)}, u32[]{:S(2)}) copy-start(f32[320,320]{1,0:T(8,128)} %first_ref.1) | copy-start | bytes 1228804
  3.0 1.0 %copy-start.21 = (f32[320,320]{1,0:T(8,128)S(1)}, f32[320,320]{1,0:T(8,128)}, u32[]{:S(2)}) copy-start(f32[320,320]{1,0:T(8,128)} %final_ref.1) | copy-start | bytes 1228804
  4.0 0.9 %copy-start.22 = (f32[320,128]{1,0:T(8,128)S(1)}, f32[320,128]{1,0:T(8,128)}, u32[]{:S(2)}) copy-start(f32[320,128]{1,0:T(8,128)} %source_ref.1) | copy-start | bytes 491524
  4.9 0.7 copy-start.29
  5.6 0.7 copy-start.30
  6.3 0.7 copy-start.31
  7.0 0.7 copy-start.32
  7.6 0.7 copy-start.33
  8.3 0.7 copy-start.34
  9.0 0.7 copy-start.35
  9.7 15.5 %copy-start.1 = (f32[480,128]{1,0:T(8,128)S(1)}, f32[480,128]{1,0:T(8,128)}, u32[]{:S(2)}) copy-start(f32[480,128]{1,0:T(8,128)} %coupling_ref.7) | copy-start | bytes 737284
  9.7 15.5 %copy-start.28 = (s32[6,128]{1,0:T(8,128)S(1)}, s32[6,128]{1,0:T(8,128)}, u32[]{:S(2)}) copy-start(s32[6,128]{1,0:T(8,128)} %adjacent_ref.3) | copy-start | bytes 9220
  13.0 1.2 %copy-start = (bf16[768,1152]{1,0:T(8,128)(2,1)}, bf16[768,1152]{1,0:T(8,128)(2,1)S(1)}, u32[]{:S(2)}) copy-start(bf16[768,1152]{1,0:T(8,128)(2,1)S(1)} %get-tuple-element.28.send_hot_ref) | copy-start | bytes 5308420
  14.3 0.7 copy-start.4
  14.9 0.6 copy-start.18
  15.6 0.6 copy-start.38
  16.2 18.5 %all-to-all-start = ((f32[16,40,128]{2,1,0:T(8,128)}), f32[16,40,128]{2,1,0:T(8,128)S(1)}, u32[]{:S(2)}, u32[]{:S(2)}) async-start(f32[16,40,128]{2,1,0:T(8,128)} %get-tuple-element.20), calls=%async_computation | async-start | bytes 655360 | tf_op jit(solution)/shard_map/all_to_all | solution.py:585
  23.6 7.7 %collective-permute-start = (f32[80,128]{1,0:T(8,128)}, f32[80,128]{1,0:T(8,128)S(1)}, u32[]{:S(2)}, u32[]{:S(2)}) collective-permute-start(f32[80,128]{1,0:T(8,128)} %get-tuple-element.21), channel_id=1, source_target_pairs={{0,16},{16,0},{1,17},{17,1},{2,18},{18,2},{3,19},{19,3},{4,20},{20... | collective-permute-start | bytes 122888 | tf_op jit(solution)/shard_map/ppermute | solution.py:579
  25.1 0.9 %copy-start.5 = (f32[320,128]{1,0:T(8,128)S(1)}, f32[320,128]{1,0:T(8,128)}, u32[]{:S(2)}) copy-start(f32[320,128]{1,0:T(8,128)} %copy-done.4) | copy-start | bytes 491524
  26.1 0.9 %copy-start.23 = (f32[320,128]{1,0:T(8,128)S(1)}, f32[320,128]{1,0:T(8,128)}, u32[]{:S(2)}) copy-start(f32[320,128]{1,0:T(8,128)} %mass_ref.3) | copy-start | bytes 491524
  27.0 0.8 %copy-start.25 = (f32[75,128]{1,0:T(8,128)S(1)}, f32[75,128]{1,0:T(8,128)}, u32[]{:S(2)}) copy-start(f32[75,128]{1,0:T(8,128)} %flux_ref.3) | copy-start | bytes 115204
  27.8 0.8 %copy-start.36 = (bf16[128,192]{1,0:T(8,128)(2,1)S(1)}, bf16[128,192]{1,0:T(8,128)(2,1)}, u32[]{:S(2)}) copy-start(bf16[128,192]{1,0:T(8,128)(2,1)} %constant.14.clone.volume_ref) | copy-start | bytes 147460
  28.6 0.8 %copy-start.39 = (s32[8,1152]{1,0:T(8,128)S(1)}, s32[8,1152]{1,0:T(8,128)}, u32[]{:S(2)}) copy-start(s32[8,1152]{1,0:T(8,128)} %copy-done.38) | copy-start | bytes 110596
  29.4 5.3 %copy-start.3 = (f32[320,128]{1,0:T(8,128)S(1)}, f32[320,128]{1,0:T(8,128)}, u32[]{:S(2)}) copy-start(f32[320,128]{1,0:T(8,128)} %mid_ref.5) | copy-start | bytes 491524
  30.7 0.7 copy-start.14
  34.7 0.9 %copy-start.13 = (bf16[160,720]{1,0:T(8,128)(2,1)S(1)}, bf16[160,720]{1,0:T(8,128)(2,1)}, u32[]{:S(2)}) copy-start(bf16[160,720]{1,0:T(8,128)(2,1)} %constant.13.clone.tiles_ref) | copy-start | bytes 691204
  35.6 0.9 %copy-start.15 = (f32[320,128]{1,0:T(8,128)S(1)}, f32[320,128]{1,0:T(8,128)}, u32[]{:S(2)}) copy-start(f32[320,128]{1,0:T(8,128)} %copy-done.14) | copy-start | bytes 491524
  36.5 0.8 %copy-start.19 = (s32[8,1024]{1,0:T(8,128)S(1)}, s32[8,1024]{1,0:T(8,128)}, u32[]{:S(2)}) copy-start(s32[8,1024]{1,0:T(8,128)} %copy-done.18) | copy-start | bytes 98308
  41.1 0.7 copy-start.8
  41.7 0.7 copy-start.11
  42.4 0.6 copy-start.27
  43.1 14.6 %all-to-all-start.1 = ((f32[16,40,128]{2,1,0:T(8,128)}), f32[16,40,128]{2,1,0:T(8,128)S(1)}, u32[]{:S(2)}, u32[]{:S(2)}) async-start(f32[16,40,128]{2,1,0:T(8,128)} %copy-done.11), calls=%async_computation.1 | async-start | bytes 655360 | tf_op jit(solution)/shard_map/all_to_all | solution.py:585
  46.6 7.4 %collective-permute-start.1 = (f32[80,128]{1,0:T(8,128)}, f32[80,128]{1,0:T(8,128)S(1)}, u32[]{:S(2)}, u32[]{:S(2)}) collective-permute-start(f32[80,128]{1,0:T(8,128)} %copy-done.27), channel_id=1, source_target_pairs={{0,16},{16,0},{1,17},{17,1},{2,18},{18,2},{3,19},{19,3},{4,20},{20... | collective-permute-start | bytes 122888 | tf_op jit(solution)/shard_map/ppermute | solution.py:579
  48.2 0.9 %copy-start.6 = (f32[320,128]{1,0:T(8,128)S(1)}, f32[320,128]{1,0:T(8,128)}, u32[]{:S(2)}) copy-start(f32[320,128]{1,0:T(8,128)} %copy-done.4) | copy-start | bytes 491524
  49.1 0.9 %copy-start.9 = (f32[320,128]{1,0:T(8,128)S(1)}, f32[320,128]{1,0:T(8,128)}, u32[]{:S(2)}) copy-start(f32[320,128]{1,0:T(8,128)} %copy-done.8) | copy-start | bytes 491524
  50.0 0.9 %copy-start.24 = (f32[320,128]{1,0:T(8,128)S(1)}, f32[320,128]{1,0:T(8,128)}, u32[]{:S(2)}) copy-start(f32[320,128]{1,0:T(8,128)} %mass_ref.3) | copy-start | bytes 491524
  50.9 0.8 %copy-start.26 = (f32[75,128]{1,0:T(8,128)S(1)}, f32[75,128]{1,0:T(8,128)}, u32[]{:S(2)}) copy-start(f32[75,128]{1,0:T(8,128)} %flux_ref.3) | copy-start | bytes 115204
  51.7 0.8 %copy-start.37 = (bf16[128,192]{1,0:T(8,128)(2,1)S(1)}, bf16[128,192]{1,0:T(8,128)(2,1)}, u32[]{:S(2)}) copy-start(bf16[128,192]{1,0:T(8,128)(2,1)} %constant.14.clone.volume_ref) | copy-start | bytes 147460
  53.4 0.7 copy-start.16
  57.6 0.9 %copy-start.7 = (f32[320,128]{1,0:T(8,128)S(1)}, f32[320,128]{1,0:T(8,128)}, u32[]{:S(2)}) copy-start(f32[320,128]{1,0:T(8,128)} %copy-done.4) | copy-start | bytes 491524
  58.6 0.9 %copy-start.10 = (f32[320,128]{1,0:T(8,128)S(1)}, f32[320,128]{1,0:T(8,128)}, u32[]{:S(2)}) copy-start(f32[320,128]{1,0:T(8,128)} %copy-done.8) | copy-start | bytes 491524
  59.5 0.9 %copy-start.17 = (f32[320,128]{1,0:T(8,128)S(1)}, f32[320,128]{1,0:T(8,128)}, u32[]{:S(2)}) copy-start(f32[320,128]{1,0:T(8,128)} %copy-done.16) | copy-start | bytes 491524

commit v2 on v1

--- a/solution.py
+++ b/solution.py
@@ -181,18 +181,20 @@
     return mm(rows, one_hot(slots == target))
 
 
-def index_tables(
-    place, devices, cap, halo, hang, elements, small, outq, inc, inq, coarse, band, plane
-):
-    gx_index, gx_size, yz_index, groups = devices
+def index_tables(cap, small, outq, inc, inq, coarse, band, plane, elements, sizes):
+    gx_size, groups = sizes
+    gx_index, yz_index = lax.axis_index("gx"), lax.axis_index("yz")
+    hang, halo = coarse.shape[1], band.shape[1]
     traces = FACES * elements
     as_f = lambda x: x.astype(F32)
     coarse_hot = one_hot(
         lax.broadcasted_iota(jnp.int32, (hang, inc.shape[1]), 0) == inc
     )
-    high, low = coarse // 8, coarse % 8
     pad = jnp.zeros((6, hang), F32)
-    pick = mm(jnp.concatenate([as_f(high), as_f(low), pad], axis=0).astype(BF16), coarse_hot)
+    pick = mm(
+        jnp.concatenate([as_f(coarse // 8), as_f(coarse % 8), pad], axis=0).astype(BF16),
+        coarse_hot,
+    )
     rows = jnp.concatenate(
         [
             as_f(small // 8),
@@ -215,26 +217,35 @@
     position = within - cap + step * second
     up = lax.rem(yz_index + 1, groups)
     down = lax.rem(yz_index + groups - 1, groups)
-    lower_columns = jnp.zeros_like(lane) + traces
-    upper_columns = lower_columns
-    for j in range(halo):
-        lower_columns = jnp.where(position == j, 2 * elements + band[0, 0, j], lower_columns)
-        upper_columns = jnp.where(position == j, 3 * elements + band[0, 1, j], upper_columns)
+    slab_lane = lane_row(128)
+    target = jnp.concatenate(
+        [
+            jnp.where(side, position, -1),
+            jnp.where(slab_lane < 2 * halo, slab_lane % halo, -1),
+        ],
+        axis=1,
+    )
+    slots = lax.broadcasted_iota(jnp.int32, (halo, target.shape[1]), 0)
+    halo_rows = jnp.concatenate([as_f(band), as_f(plane), jnp.zeros((4, halo), F32)], axis=0)
+    edge = mm(halo_rows.astype(BF16), one_hot(slots == target)).astype(jnp.int32)
+    lanes = lane.shape[1]
     side_send = jnp.where(
-        group == up, upper_columns, jnp.where(group == down, lower_columns, traces)
-    )
-    fine_id = placed[0:1] * 8 + placed[1:2]
-    coarse_id = placed[2:3] * 8 + placed[3:4]
-    slot_id = jnp.where(second == 0, fine_id, coarse_id)
+        group == up,
+        3 * elements + edge[1:2, :lanes],
+        jnp.where(group == down, 2 * elements + edge[0:1, :lanes], traces),
+    )
+    slot_id = jnp.where(
+        second == 0, placed[0:1] * 8 + placed[1:2], placed[2:3] * 8 + placed[3:4]
+    )
     send_id = jnp.where(is_slot, slot_id, jnp.where(side, side_send, traces))
     codes = jnp.where(
         is_slot, jnp.where(second == 0, placed[4:5], 4 + placed[5:6]), 8
     )
-    slab_lane = lane_row(128)
-    slab_id = jnp.zeros_like(slab_lane) + traces
-    for j in range(halo):
-        slab_id = jnp.where(slab_lane == j, plane[0, 0, j], slab_id)
-        slab_id = jnp.where(slab_lane == halo + j, elements + plane[0, 1, j], slab_id)
+    slab_id = jnp.where(
+        slab_lane < halo,
+        edge[2:3, lanes:],
+        jnp.where(slab_lane < 2 * halo, elements + edge[3:4, lanes:], traces),
+    )
     send_id = jnp.concatenate([send_id, slab_id], axis=1)
 
     first_hang = traces + 4 * halo
@@ -260,55 +271,62 @@
     return send_id, codes, recv_id
 
 
-def start_kernel(
-    gx_size,
-    source_ref,
-    first_ref,
-    final_ref,
-    mid_ref,
-    small_ref,
-    outq_ref,
-    inc_ref,
-    inq_ref,
-    coarse_ref,
-    band_ref,
-    plane_ref,
-    where_ref,
-    tiles_ref,
-    field_ref,
-    send_ref,
-    slab_ref,
-    send_hot_ref,
-    codes_ref,
-    recv_id_ref,
-    first_out_ref,
-    final_out_ref,
-):
-    elements = source_ref.shape[1]
-    groups = send_ref.shape[0]
-    for ref, out in ((first_ref, first_out_ref), (final_ref, final_out_ref)):
-        out[0], out[1] = split(ref[...])
-    field_ref[...] = solve_cells(source_ref[...], first_out_ref, final_out_ref, mid_ref)
+class Loads:
+    def __init__(self, sources, buffers, sems):
+        self.buffers = list(buffers)
+        self.copies = [
+            pltpu.make_async_copy(s, b, sems.at[i])
+            for i, (s, b) in enumerate(zip(sources, buffers))
+        ]
+        for copy in self.copies:
+            copy.start()
+
+    def __getitem__(self, i):
+        if self.copies[i] is not None:
+            self.copies[i].wait()
+            self.copies[i] = None
+        return self.buffers[i]
+
+
+def start_kernel(sizes, *refs):
+    loads = Loads(refs[:12], refs[20:32], refs[40])
+    tables = [loads[i] for i in range(7)]
+    outs, stage, sems = refs[12:20], refs[32:40], refs[41]
+    field, send, slab, send_hot, codes_ref, recv_id_ref, first2, final2 = stage
+    copies = [pltpu.make_async_copy(s, o, sems.at[i]) for i, (s, o) in enumerate(zip(stage, outs))]
+    elements = field.shape[1]
+    groups = send.shape[0]
+    small, outq, inc, inq, coarse, band, plane = tables
     send_id, codes, recv_id = index_tables(
-        None,
-        (where_ref[0], gx_size, where_ref[1], groups),
-        small_ref.shape[1] // groups,
-        band_ref.shape[2],
-        coarse_ref.shape[1],
+        small.shape[1] // groups,
+        small[...],
+        outq[...],
+        inc[...],
+        inq[...],
+        coarse[...],
+        band[0],
+        plane[0],
         elements,
-        small_ref[...],
-        outq_ref[...],
-        inc_ref[...],
-        inq_ref[...],
-        coarse_ref[...],
-        band_ref,
-        plane_ref,
-    )
+        sizes,
+    )
+    codes_ref[...] = jnp.broadcast_to(codes, codes_ref.shape)
+    copies[4].start()
+    recv_id_ref[...] = jnp.broadcast_to(recv_id, recv_id_ref.shape)
+    copies[5].start()
     columns = lax.broadcasted_iota(jnp.int32, (FACES * elements, send_id.shape[1]), 0)
-    send_hot_ref[...] = one_hot(columns == send_id)
-    codes_ref[...] = jnp.broadcast_to(codes, codes_ref.shape)
-    recv_id_ref[...] = jnp.broadcast_to(recv_id, recv_id_ref.shape)
-    pack_send(field_ref, send_hot_ref, codes, tiles_ref, send_ref, slab_ref)
+    send_hot[...] = one_hot(columns == send_id)
+    copies[3].start()
+    first2[0], first2[1] = split(loads[7][...])
+    copies[6].start()
+    final2[0], final2[1] = split(loads[8][...])
+    copies[7].start()
+    field[...] = solve_cells(loads[9][...], first2, final2, loads[10])
+    copies[0].start()
+    pack_send(field, send_hot, codes, loads[11], send, slab)
+    copies[1].start()
+    copies[2].start()
+    for copy in copies:
+        copy.wait()
 
 
 def local_part(
@@ -345,24 +363,21 @@
         )
 
 
-def first_local_kernel(
-    field_ref,
-    mass_ref,
-    coupling_ref,
-    flux_ref,
-    adjacent_ref,
-    volume_ref,
-    recv_id_ref,
-    local_ref,
-    recv_hot_ref,
-):
-    local_part(field_ref, mass_ref, coupling_ref, flux_ref, adjacent_ref, volume_ref, local_ref)
-    elements = field_ref.shape[1]
-    ids = jnp.transpose(recv_id_ref[...])[:, 0:1]
+def first_local_kernel(*refs):
+    loads = Loads(refs[:7], refs[9:16], refs[18])
+    (local_out, hot_out), (local, recv_hot), sems = refs[7:9], refs[16:18], refs[19]
+    elements = local.shape[1]
+    ids = jnp.transpose(loads[0][...])[:, 0:1]
+    adjacent = loads[1]
     for f in range(FACES):
-        recv_hot_ref[:, f * elements : (f + 1) * elements] = one_hot(
-            ids == adjacent_ref[f : f + 1, :]
-        )
+        recv_hot[:, f * elements : (f + 1) * elements] = one_hot(ids == adjacent[f : f + 1, :])
+    hot_copy = pltpu.make_async_copy(recv_hot, hot_out, sems.at[0])
+    hot_copy.start()
+    local_part(loads[2], loads[3], loads[4], loads[5], adjacent, loads[6], local)
+    copy = pltpu.make_async_copy(local, local_out, sems.at[1])
+    copy.start()
+    copy.wait()
+    hot_copy.wait()
 
 
 def total_of(x):
@@ -377,93 +392,72 @@
     return row
 
 
-def second_local_kernel(
-    field_ref,
-    mass_ref,
-    coupling_ref,
-    flux_ref,
-    adjacent_ref,
-    volume_ref,
-    start_ref,
-    local_ref,
-    partial_ref,
-):
-    local_part(field_ref, mass_ref, coupling_ref, flux_ref, adjacent_ref, volume_ref, local_ref)
-    k0, k1 = start_ref[...], field_ref[...]
-    partial_ref[...] = put(
+def second_local_kernel(*refs):
+    loads = Loads(refs[:7], refs[9:16], refs[18])
+    (local_out, partial_out), (local, partial), sems = refs[7:9], refs[16:18], refs[19]
+    adjacent = loads[0]
+    local_part(loads[1], loads[2], loads[3], loads[4], adjacent, loads[5], local)
+    copy = pltpu.make_async_copy(local, local_out, sems.at[0])
+    copy.start()
+    k0, k1 = loads[6][...], loads[1][...]
+    partial[...] = put(
         [(0, total_of(k0 * k0)), (1, total_of(k0 * k1)), (2, total_of(k1 * k1))]
     )
-
-
-def finish_product(
-    recv_ref, slab_ref, recv_hot_ref, coupling_ref, local_ref, first_ref, final_ref, mid_ref, work_ref
-):
-    elements = local_ref.shape[1]
+    row_copy = pltpu.make_async_copy(partial, partial_out, sems.at[1])
+    row_copy.start()
+    copy.wait()
+    row_copy.wait()
+
+
+def finish_product(recv_ref, slab_ref, loads, work_ref):
     received = jnp.concatenate([unpack_received(recv_ref), slab_ref[...]], axis=1)
-    near = mm(two_pieces(received), recv_hot_ref[...])
+    near = mm(two_pieces(received), loads[0][...])
     near = near[:TILE] + near[TILE:]
-    work_ref[...] = local_ref[...]
+    coupling, local = loads[1], loads[2]
+    elements = local.shape[1]
+    work_ref[...] = local[...]
     for f in range(FACES):
         add_to_face(
             work_ref,
             f,
-            -coupling_ref[f * TILE : (f + 1) * TILE, :] * near[:, f * elements : (f + 1) * elements],
+            -coupling[f * TILE : (f + 1) * TILE, :] * near[:, f * elements : (f + 1) * elements],
         )
-    return solve_cells(work_ref[...], first_ref, final_ref, mid_ref)
-
-
-def middle_kernel(
-    recv_ref,
-    slab_in_ref,
-    recv_hot_ref,
-    coupling_ref,
-    local_ref,
-    first_ref,
-    final_ref,
-    mid_ref,
-    send_hot_ref,
-    codes_ref,
-    tiles_ref,
-    field_ref,
-    send_ref,
-    slab_ref,
-    work_ref,
-):
-    field_ref[...] = finish_product(
-        recv_ref, slab_in_ref, recv_hot_ref, coupling_ref, local_ref, first_ref, final_ref, mid_ref, work_ref
-    )
-    pack_send(field_ref, send_hot_ref, codes_ref[0:1, :], tiles_ref, send_ref, slab_ref)
-
-
-def last_kernel(
-    recv_ref,
-    slab_in_ref,
-    recv_hot_ref,
-    coupling_ref,
-    local_ref,
-    first_ref,
-    final_ref,
-    mid_ref,
-    start_ref,
-    field_ref,
-    partial_ref,
-    out_ref,
-    work_ref,
-):
-    k2 = K2_SCALE * finish_product(
-        recv_ref, slab_in_ref, recv_hot_ref, coupling_ref, local_ref, first_ref, final_ref, mid_ref, work_ref
-    )
-    row = partial_ref[...] + put(
+    inner = mm3(loads[3][0], loads[3][1], work_ref[...])
+    return mm3(loads[5][0], loads[5][1], loads[4][...] * inner)
+
+
+def middle_kernel(*refs):
+    recv, slab_in = refs[:2]
+    loads = Loads(refs[2:11], refs[14:23], refs[27])
+    outs, stage, work, sems = refs[11:14], refs[23:26], refs[26], refs[28]
+    copies = [pltpu.make_async_copy(s, o, sems.at[i]) for i, (s, o) in enumerate(zip(stage, outs))]
+    field, send, slab = stage
+    field[...] = finish_product(recv, slab_in, loads, work)
+    copies[0].start()
+    pack_send(field, loads[6], loads[7][0:1, :], loads[8], send, slab)
+    copies[1].start()
+    copies[2].start()
+    for copy in copies:
+        copy.wait()
+
+
+def last_kernel(*refs):
+    recv, slab_in = refs[:2]
+    loads = Loads(refs[2:11], refs[12:21], refs[22])
+    out, work = refs[11], refs[21]
+    k2 = K2_SCALE * finish_product(recv, slab_in, loads, work)
+    row = loads[8][...] + put(
         [
-            (3, total_of(k2 * start_ref[...])),
-            (4, total_of(k2 * field_ref[...])),
+            (3, total_of(k2 * loads[6][...])),
+            (4, total_of(k2 * loads[7][...])),
             (5, total_of(k2 * k2)),
         ]
     )
-    out_ref[...] = jnp.broadcast_to(row.reshape(1, 1, 128), out_ref.shape)
-
-
-def combine_kernel(rows_ref, start_ref, field_ref, out_ref):
+    out[...] = jnp.broadcast_to(row.reshape(1, 1, 128), out.shape)
+
+
+def combine_kernel(rows_ref, start_ref, field_ref, out_ref, sems):
+    del sems
     totals = jnp.sum(rows_ref[:, 0, :], axis=0, keepdims=True)
     lane = lane_row(128)
     g00, g01, g11, g02, g12, g22 = [
@@ -502,25 +496,29 @@
     out_ref[...] = along0 * start_ref[...] + along1 * field_ref[...]
 
 
-def vmem(count):
-    return [pl.BlockSpec(memory_space=pltpu.VMEM)] * count
-
-
-def call(kernel, outs, args, smem=(), scratch=(), flops=0):
-    specs = [
-        pl.BlockSpec(memory_space=pltpu.SMEM if i in smem else pltpu.VMEM)
-        for i in range(len(args))
-    ]
+def call(kernel, outs, args, held=0, staged=True, scratch=()):
+    in_vmem, in_place = pl.BlockSpec(memory_space=pltpu.VMEM), pl.BlockSpec(memory_space=pl.ANY)
+    moved = args[held:]
+    buffers = [pltpu.VMEM(a.shape, a.dtype) for a in moved]
+    out_list = jax.tree.leaves(outs)
+    if staged:
+        buffers += [pltpu.VMEM(o.shape, o.dtype) for o in out_list]
+    buffers += list(scratch)
+    buffers.append(pltpu.SemaphoreType.DMA((max(len(moved), 1),)))
+    if staged:
+        buffers.append(pltpu.SemaphoreType.DMA((len(out_list),)))
     return pl.pallas_call(
         kernel,
         out_shape=outs,
-        in_specs=specs,
-        out_specs=jax.tree.map(lambda _: pl.BlockSpec(memory_space=pltpu.VMEM), outs),
-        scratch_shapes=list(scratch),
+        in_specs=[in_vmem] * held + [in_place] * len(moved),
+        out_specs=jax.tree.map(lambda _: in_place if staged else in_vmem, outs),
+        scratch_shapes=buffers,
         cost_estimate=pl.CostEstimate(
-            flops=flops, bytes_accessed=sum(a.size * a.dtype.itemsize for a in args), transcendentals=0
+            flops=10**9,
+            bytes_accessed=sum(a.size * a.dtype.itemsize for a in args),
+            transcendentals=0,
         ),
-        compiler_params=pltpu.CompilerParams(vmem_limit_bytes=48 * 2**20),
+        compiler_params=pltpu.CompilerParams(vmem_limit_bytes=40 * 2**20),
     )(*args)
 
 
@@ -552,10 +550,9 @@
     field = struct((DOFS, elements), F32)
     send = struct((groups, TILE // 2, 128), F32)
     slab = struct((TILE, 128), F32)
-    where = jnp.stack([lax.axis_index("gx"), lax.axis_index("yz")]).astype(jnp.int32)
 
     k0, send0, slab0, send_hot, codes, recv_id, first2, final2 = call(
-        functools.partial(start_kernel, gx_size),
+        functools.partial(start_kernel, (gx_size, groups)),
         (
             field,
             send,
@@ -566,9 +563,7 @@
             struct((2, DOFS, DOFS), BF16),
             struct((2, DOFS, DOFS), BF16),
         ),
-        (source, first, final, mid, small, outq, inc, inq, coarse, band, plane, where, tiles),
-        smem=(9, 10, 11),
-        flops=10**9,
+        (small, outq, inc, inq, coarse, band, plane, first, final, source, mid, tiles),
     )
 
     up = [(i, i + 1) for i in range(gx_size - 1)]
@@ -588,33 +583,34 @@
     local0, recv_hot = call(
         first_local_kernel,
         (field, struct((lanes + 128, traces), BF16)),
-        (k0, mass, coupling, flux, adjacent, volume, recv_id),
-        flops=10**9,
+        (recv_id, adjacent, k0, mass, coupling, flux, volume),
     )
     work = pltpu.VMEM((DOFS, elements), F32)
+    solve_args = (coupling, local0, first2, mid, final2)
     k1, send1, slab1 = call(
         middle_kernel,
         (field, send, slab),
-        (recv0, slab0, recv_hot, coupling, local0, first2, final2, mid, send_hot, codes, tiles),
+        (recv0, slab0, recv_hot) + solve_args + (send_hot, codes, tiles),
+        held=2,
         scratch=[work],
-        flops=10**9,
     )
     recv1, slab1 = exchange(send1, slab1)
     local1, partial = call(
         second_local_kernel,
         (field, struct((1, 128), F32)),
-        (k1, mass, coupling, flux, adjacent, volume, k0),
-        flops=10**9,
-    )
+        (adjacent, k1, mass, coupling, flux, volume, k0),
+    )
+    solve_args = (coupling, local1, first2, mid, final2)
     rows = call(
         last_kernel,
         struct((gx_size * groups, 1, 128), F32),
-        (recv1, slab1, recv_hot, coupling, local1, first2, final2, mid, k0, k1, partial),
+        (recv1, slab1, recv_hot) + solve_args + (k0, k1, partial),
+        held=2,
+        staged=False,
         scratch=[work],
-        flops=10**9,
     )
     rows = lax.all_to_all(rows, ("gx", "yz"), 0, 0, tiled=True)
-    return call(combine_kernel, field, (rows, k0, k1), flops=10**6)
+    return call(combine_kernel, field, (rows, k0, k1), held=3, staged=False)
 
 
 def solution(mesh):

time: 73.9 us -> 84.1 us (1.14)
  Pallas kernels: 11.5 us -> 21.6 us
  local copies, waits for them, and re-layouts: 29.9 us -> 32.9 us
  waiting for transfers between devices: 6.92 us -> 4.46 us
    pallas_call x6, Pallas kernels: 11.5 us -> 21.6 us  [call(): pl.pallas_call(kernel, out_shape=outs, in_specs=[in_vmem] * held + [in_pl...]
    unnamed x80 -> x86, local copies, waits for them, and re-layouts: 29.9 us -> 32.9 us
    all_to_all x2, waiting for transfers between devices: 6.92 us -> 4.46 us  [exchange(): return (lax.all_to_all(send, 'yz', 0, 0, tiled=True), slab)]
    all_to_all x2, starting transfers between devices: 11 us -> 11.9 us  [exchange(): return (lax.all_to_all(send, 'yz', 0, 0, tiled=True), slab)]
    ppermute x2, starting transfers between devices: 3.1 us -> 2.19 us  [exchange(): slab = lax.ppermute(slab, 'gx', up + down)]
  transfers between devices with their start and end apart: 4 -> 4, of which waited for: 2 -> 2; matrix products, arithmetic and copies ran while one was open for 0% -> 0% of each run, Pallas kernels for 3% -> 7%
where the time goes in v2:
time: 84.1 us; the launch traced here: 82.9 us
  local copies, waits for them, and re-layouts  32.9 us (39%)
  Pallas kernels  21.6 us (26%)
  starting transfers between devices  14.1 us (17%)
  blocking collectives  9.84 us (12%)
  waiting for transfers between devices  4.46 us (5%)
    unnamed x86, local copies, waits for them, and re-layouts  32.9 us
    pallas_call x6, Pallas kernels, call(): pl.pallas_call(kernel, out_shape=outs, in_specs=[in_vmem] * held + [in_pl...  21.6 us
    all_to_all x2, starting transfers between devices, exchange(): return (lax.all_to_all(send, 'yz', 0, 0, tiled=True), slab)  11.9 us
    all_to_all x1, blocking collectives, on_device(): rows = lax.all_to_all(rows, ('gx', 'yz'), 0, 0, tiled=True)  9.84 us
    all_to_all x2, waiting for transfers between devices, exchange(): return (lax.all_to_all(send, 'yz', 0, 0, tiled=True), slab)  4.46 us
    ppermute x2, starting transfers between devices, exchange(): slab = lax.ppermute(slab, 'gx', up + down)  2.19 us
  transfers between devices with their start and end apart: 4, of which 2 were waited for; matrix products, arithmetic and copies ran while one was open for 0% of the time, Pallas kernels for 7%

profile of v2, /device:TPU:0, one launch (start us, length us, event | category | flops | bytes accessed | tf_op | source)
XLA Modules:
  0.0 82.9 jit_solution(5735916659336690562)
XLA Ops:
  0.0 1.0 %copy-done.3 = f32[320,128]{1,0:T(8,128)S(1)} copy-done((f32[320,128]{1,0:T(8,128)S(1)}, f32[320,128]{1,0:T(8,128)}, u32[]{:S(2)}) %copy-start.3) | copy-done | bytes 163864
  1.0 0.9 %copy-done.7 = bf16[160,720]{1,0:T(8,128)(2,1)S(1)} copy-done((bf16[160,720]{1,0:T(8,128)(2,1)S(1)}, bf16[160,720]{1,0:T(8,128)(2,1)}, u32[]{:S(2)}) %copy-start.7) | copy-done | bytes 230424
  1.9 1.0 %copy-done.22 = f32[320,320]{1,0:T(8,128)S(1)} copy-done((f32[320,320]{1,0:T(8,128)S(1)}, f32[320,320]{1,0:T(8,128)}, u32[]{:S(2)}) %copy-start.22) | copy-done | bytes 409624
  2.9 1.0 %copy-done.23 = f32[320,320]{1,0:T(8,128)S(1)} copy-done((f32[320,320]{1,0:T(8,128)S(1)}, f32[320,320]{1,0:T(8,128)}, u32[]{:S(2)}) %copy-start.23) | copy-done | bytes 409624
  4.0 0.9 %copy-done.24 = f32[320,128]{1,0:T(8,128)S(1)} copy-done((f32[320,128]{1,0:T(8,128)S(1)}, f32[320,128]{1,0:T(8,128)}, u32[]{:S(2)}) %copy-start.24) | copy-done | bytes 163864
  4.9 0.7 copy-done.32
  5.6 0.7 copy-done.33
  6.2 0.7 copy-done.34
  6.9 0.7 copy-done.35
  7.6 0.7 copy-done.36
  8.3 0.7 copy-done.37
  9.0 0.7 copy-done.38
  9.6 5.6 %shard_map.163 = (f32[320,128]{1,0:T(8,128)S(1)}, f32[16,40,128]{2,1,0:T(8,128)S(1)}, f32[80,128]{1,0:T(8,128)S(1)}, bf16[768,1152]{1,0:T(8,128)(2,1)S(1)}, s32[...) custom-call(s32[1,352]{1,0:T(1,128)S(1)} %copy-done.32, ...), custom_call_target="tpu_custom_call" | custom-call | flops 1000000000 | bytes 1383488 | tf_op jit(solution)/shard_map/pallas_call | solution.py:510
  15.3 1.3 %copy-done = bf16[768,1152]{1,0:T(8,128)(2,1)} copy-done((bf16[768,1152]{1,0:T(8,128)(2,1)}, bf16[768,1152]{1,0:T(8,128)(2,1)S(1)}, u32[]{:S(2)}) %copy-start) | copy-done | bytes 1769496
  16.5 0.7 copy-done.6
  17.3 0.7 copy-done.9
  19.7 7.4 %all-to-all-start = ((f32[16,40,128]{2,1,0:T(8,128)}), f32[16,40,128]{2,1,0:T(8,128)S(1)}, u32[]{:S(2)}, u32[]{:S(2)}) async-start(f32[16,40,128]{2,1,0:T(8,128)} %copy-done.6), calls=%async_computation | async-start | bytes 655360 | tf_op jit(solution)/shard_map/all_to_all | solution.py:580
  27.2 1.6 %collective-permute-start = (f32[80,128]{1,0:T(8,128)}, f32[80,128]{1,0:T(8,128)S(1)}, u32[]{:S(2)}, u32[]{:S(2)}) collective-permute-start(f32[80,128]{1,0:T(8,128)} %copy-done.30), channel_id=1, source_target_pairs={{0,16},{16,0},{1,17},{17,1},{2,18},{18,2},{3,19},{19,3},{4,20},{20... | collective-permute-start | bytes 122888 | tf_op jit(solution)/shard_map/ppermute | solution.py:574
  28.7 0.9 %copy-done.10 = f32[320,128]{1,0:T(8,128)S(1)} copy-done((f32[320,128]{1,0:T(8,128)S(1)}, f32[320,128]{1,0:T(8,128)}, u32[]{:S(2)}) %copy-start.10) | copy-done | bytes 163864
  29.6 0.9 %copy-done.25 = f32[320,128]{1,0:T(8,128)S(1)} copy-done((f32[320,128]{1,0:T(8,128)S(1)}, f32[320,128]{1,0:T(8,128)}, u32[]{:S(2)}) %copy-start.25) | copy-done | bytes 163864
  30.6 0.8 copy-done.27
  31.3 0.8 %copy-done.39 = bf16[128,192]{1,0:T(8,128)(2,1)S(1)} copy-done((bf16[128,192]{1,0:T(8,128)(2,1)S(1)}, bf16[128,192]{1,0:T(8,128)(2,1)}, u32[]{:S(2)}) %copy-start.39) | copy-done | bytes 49176
  32.2 0.8 copy-done.42
  32.9 3.1 %shard_map.164 = (f32[320,128]{1,0:T(8,128)S(1)}, bf16[1152,768]{1,0:T(8,128)(2,1)S(1)}) custom-call(s32[8,1152]{1,0:T(8,128)S(1)} %copy-done.42, s32[6,128]{1,0:T(8,128)S(1)} %copy-done.31, f32[320,128]{1,0:T(8,128)S(1)} %copy-done.10, f32[320,128]{1,0:T(8,128)S(1)} %copy-done.25, f32[480,128]{1,0:T(8,128)S(1)} %copy-done.2, f32[75,128]{1,0:T(8,128)S(1)} %copy-done.27, ...), custom_call_target="tpu_custom_call" | custom-call | flops 1000000000 | bytes 700928 | tf_op jit(solution)/shard_map/pallas_call | solution.py:510
  36.1 0.7 copy-done.16
  36.8 1.5 %all-to-all-done.refs_0_ = f32[16,40,128]{2,1,0:T(8,128)S(1)} async-done(((f32[16,40,128]{2,1,0:T(8,128)}), f32[16,40,128]{2,1,0:T(8,128)S(1)}, u32[]{:S(2)}, u32[]{:S(2)}) %all-to-all-start) | async-done | bytes 327712 | tf_op jit(solution)/shard_map/all_to_all | solution.py:580
  38.2 1.5 %copy-done.1 = bf16[768,1152]{1,0:T(8,128)(2,1)S(1)} copy-done((bf16[768,1152]{1,0:T(8,128)(2,1)S(1)}, bf16[768,1152]{1,0:T(8,128)(2,1)}, u32[]{:S(2)}) %copy-start.1) | copy-done | bytes 1769496
  39.7 0.9 %copy-done.8 = bf16[160,720]{1,0:T(8,128)(2,1)S(1)} copy-done((bf16[160,720]{1,0:T(8,128)(2,1)S(1)}, bf16[160,720]{1,0:T(8,128)(2,1)}, u32[]{:S(2)}) %copy-start.8) | copy-done | bytes 230424
  40.7 0.9 %copy-done.17 = f32[320,128]{1,0:T(8,128)S(1)} copy-done((f32[320,128]{1,0:T(8,128)S(1)}, f32[320,128]{1,0:T(8,128)}, u32[]{:S(2)}) %copy-start.17) | copy-done | bytes 163864
  41.6 0.8 copy-done.21
  42.3 5.6 %shard_map.165 = (f32[320,128]{1,0:T(8,128)S(1)}, f32[16,40,128]{2,1,0:T(8,128)S(1)}, f32[80,128]{1,0:T(8,128)S(1)}) custom-call(f32[16,40,128]{2,1,0:T(8,128)S(1)} %all-to-all-done.refs_0_, f32[80,128]{1,0:T(8,128)S(1)} %collective-permute-done.refs_1_, bf16[1152,768]{1,0:T(8,128)(2,1)S(1)} %get-tuple-element.24.refs_2_, f32[480,128]{1,0:T(8,128)S(1)} %copy-done.2, ...), custom_call_target="tpu_custom_call" | custom-call | flops 1000000000 | bytes 5563392 | tf_op jit(solution)/shard_map/pallas_call | solution.py:510
  47.9 0.7 copy-done.5
  48.6 0.7 copy-done.13
  49.9 4.5 %all-to-all-start.1 = ((f32[16,40,128]{2,1,0:T(8,128)}), f32[16,40,128]{2,1,0:T(8,128)S(1)}, u32[]{:S(2)}, u32[]{:S(2)}) async-start(f32[16,40,128]{2,1,0:T(8,128)} %copy-done.5), calls=%async_computation.1 | async-start | bytes 655360 | tf_op jit(solution)/shard_map/all_to_all | solution.py:580
  55.0 0.9 %copy-done.11 = f32[320,128]{1,0:T(8,128)S(1)} copy-done((f32[320,128]{1,0:T(8,128)S(1)}, f32[320,128]{1,0:T(8,128)}, u32[]{:S(2)}) %copy-start.11) | copy-done | bytes 163864
  55.9 0.9 %copy-done.14 = f32[320,128]{1,0:T(8,128)S(1)} copy-done((f32[320,128]{1,0:T(8,128)S(1)}, f32[320,128]{1,0:T(8,128)}, u32[]{:S(2)}) %copy-start.14) | copy-done | bytes 163864
  56.8 0.9 %copy-done.26 = f32[320,128]{1,0:T(8,128)S(1)} copy-done((f32[320,128]{1,0:T(8,128)S(1)}, f32[320,128]{1,0:T(8,128)}, u32[]{:S(2)}) %copy-start.26) | copy-done | bytes 163864
  57.8 0.8 copy-done.28
  58.5 0.8 %copy-done.40 = bf16[128,192]{1,0:T(8,128)(2,1)S(1)} copy-done((bf16[128,192]{1,0:T(8,128)(2,1)S(1)}, bf16[128,192]{1,0:T(8,128)(2,1)}, u32[]{:S(2)}) %copy-start.40) | copy-done | bytes 49176
  59.4 2.4 %shard_map.166 = (f32[320,128]{1,0:T(8,128)S(1)}, f32[1,128]{1,0:T(1,128)S(1)}) custom-call(s32[6,128]{1,0:T(8,128)S(1)} %copy-done.31, f32[320,128]{1,0:T(8,128)S(1)} %copy-done.14, f32[320,128]{1,0:T(8,128)S(1)} %copy-done.26, f32[480,128]{1,0:T(8,128)S(1)} %copy-done.2, f32[75,128]{1,0:T(8,128)S(1)} %copy-done.28, bf16[128,192]{1,0:T(8,128)(2,1)S(1)} %copy-done.40, ...), custom_call_target="tpu_custom_call" | custom-call | flops 1000000000 | bytes 827904 | tf_op jit(solution)/shard_map/pallas_call | solution.py:510
  61.8 0.7 copy-done.18
  62.5 3.0 %all-to-all-done.1.refs_0_ = f32[16,40,128]{2,1,0:T(8,128)S(1)} async-done(((f32[16,40,128]{2,1,0:T(8,128)}), f32[16,40,128]{2,1,0:T(8,128)S(1)}, u32[]{:S(2)}, u32[]{:S(2)}) %all-to-all-start.1) | async-done | bytes 327712 | tf_op jit(solution)/shard_map/all_to_all | solution.py:580
  65.4 0.9 %copy-done.12 = f32[320,128]{1,0:T(8,128)S(1)} copy-done((f32[320,128]{1,0:T(8,128)S(1)}, f32[320,128]{1,0:T(8,128)}, u32[]{:S(2)}) %copy-start.12) | copy-done | bytes 163864
  66.4 0.9 %copy-done.15 = f32[320,128]{1,0:T(8,128)S(1)} copy-done((f32[320,128]{1,0:T(8,128)S(1)}, f32[320,128]{1,0:T(8,128)}, u32[]{:S(2)}) %copy-start.15) | copy-done | bytes 163864
  67.3 0.9 %copy-done.19 = f32[320,128]{1,0:T(8,128)S(1)} copy-done((f32[320,128]{1,0:T(8,128)S(1)}, f32[320,128]{1,0:T(8,128)}, u32[]{:S(2)}) %copy-start.19) | copy-done | bytes 163864
  68.2 4.0 %shard_map.167 = f32[32,1,128]{2,1,0:T(1,128)S(1)} custom-call(f32[16,40,128]{2,1,0:T(8,128)S(1)} %all-to-all-done.1.refs_0_, f32[80,128]{1,0:T(8,128)S(1)} %collective-permute-done.1.refs_1_, bf16[1152,768]{1,0:T(8,128)(2,1)S(1)} %get-tuple-element.24.refs_2_, f32[480,128]{1,0:T(8,128)S(1)} %copy-done.2, f32[320,128]{1,0:T(8,128)S(1)} %copy-done.19, ...), custom_call_target="tpu_custom_call" | custom-call | flops 1000000000 | bytes 3858944 | tf_op jit(solution)/shard_map/pallas_call | solution.py:510
  72.2 9.8 %all_to_all.15.rows_ref = f32[32,1,128]{2,1,0:T(1,128)S(1)} all-to-all(f32[32,1,128]{2,1,0:T(1,128)S(1)} %shard_map.167), channel_id=1, replica_groups=mesh['gx'=2,'yz'=16] {'gx','yz'}, dimensions={0} | all-to-all | bytes 32768 | tf_op jit(solution)/shard_map/all_to_all | solution.py:612
  82.1 0.9 %shard_map.168 = f32[320,128]{1,0:T(8,128)} custom-call(f32[32,1,128]{2,1,0:T(1,128)S(1)} %all_to_all.15.rows_ref, f32[320,128]{1,0:T(8,128)S(1)} %copy-done.12, f32[320,128]{1,0:T(8,128)S(1)} %copy-done.15), custom_call_target="tpu_custom_call" | custom-call | flops 1000000000 | bytes 344064 | tf_op jit(solution)/shard_map/pallas_call | solution.py:510
  (53 shorter events, 3.1 us)
Async XLA Ops:
  0.0 28.7 %copy-start.2 = (f32[480,128]{1,0:T(8,128)S(1)}, f32[480,128]{1,0:T(8,128)}, u32[]{:S(2)}) copy-start(f32[480,128]{1,0:T(8,128)} %refs_3_.9) | copy-start | bytes 737284
  0.0 1.0 %copy-start.3 = (f32[320,128]{1,0:T(8,128)S(1)}, f32[320,128]{1,0:T(8,128)}, u32[]{:S(2)}) copy-start(f32[320,128]{1,0:T(8,128)} %refs_6_.6) | copy-start | bytes 491524
  1.0 0.9 %copy-start.7 = (bf16[160,720]{1,0:T(8,128)(2,1)S(1)}, bf16[160,720]{1,0:T(8,128)(2,1)}, u32[]{:S(2)}) copy-start(bf16[160,720]{1,0:T(8,128)(2,1)} %constant.4.clone.refs_11_.refs_10_) | copy-start | bytes 691204
  1.9 1.0 %copy-start.22 = (f32[320,320]{1,0:T(8,128)S(1)}, f32[320,320]{1,0:T(8,128)}, u32[]{:S(2)}) copy-start(f32[320,320]{1,0:T(8,128)} %refs_7_.1) | copy-start | bytes 1228804
  2.9 1.0 %copy-start.23 = (f32[320,320]{1,0:T(8,128)S(1)}, f32[320,320]{1,0:T(8,128)}, u32[]{:S(2)}) copy-start(f32[320,320]{1,0:T(8,128)} %refs_8_.1) | copy-start | bytes 1228804
  4.0 0.9 %copy-start.24 = (f32[320,128]{1,0:T(8,128)S(1)}, f32[320,128]{1,0:T(8,128)}, u32[]{:S(2)}) copy-start(f32[320,128]{1,0:T(8,128)} %refs_9_.1) | copy-start | bytes 491524
  4.9 0.7 copy-start.32
  5.6 0.7 copy-start.33
  6.2 0.7 copy-start.34
  6.9 0.7 copy-start.35
  7.6 0.7 copy-start.36
  8.3 0.7 copy-start.37
  9.0 0.7 copy-start.38
  9.6 19.1 %copy-start.31 = (s32[6,128]{1,0:T(8,128)S(1)}, s32[6,128]{1,0:T(8,128)}, u32[]{:S(2)}) copy-start(s32[6,128]{1,0:T(8,128)} %refs_0_.3) | copy-start | bytes 9220
  15.3 1.3 %copy-start = (bf16[768,1152]{1,0:T(8,128)(2,1)}, bf16[768,1152]{1,0:T(8,128)(2,1)S(1)}, u32[]{:S(2)}) copy-start(bf16[768,1152]{1,0:T(8,128)(2,1)S(1)} %get-tuple-element.28.refs_8_) | copy-start | bytes 5308420
  16.5 0.7 copy-start.6
  17.2 0.7 copy-start.9
  17.9 0.6 copy-start.20
  18.5 0.6 copy-start.30
  19.1 0.6 copy-start.41
  19.7 18.5 %all-to-all-start = ((f32[16,40,128]{2,1,0:T(8,128)}), f32[16,40,128]{2,1,0:T(8,128)S(1)}, u32[]{:S(2)}, u32[]{:S(2)}) async-start(f32[16,40,128]{2,1,0:T(8,128)} %copy-done.6), calls=%async_computation | async-start | bytes 655360 | tf_op jit(solution)/shard_map/all_to_all | solution.py:580
  27.2 9.6 %collective-permute-start = (f32[80,128]{1,0:T(8,128)}, f32[80,128]{1,0:T(8,128)S(1)}, u32[]{:S(2)}, u32[]{:S(2)}) collective-permute-start(f32[80,128]{1,0:T(8,128)} %copy-done.30), channel_id=1, source_target_pairs={{0,16},{16,0},{1,17},{17,1},{2,18},{18,2},{3,19},{19,3},{4,20},{20... | collective-permute-start | bytes 122888 | tf_op jit(solution)/shard_map/ppermute | solution.py:574
  28.7 0.9 %copy-start.10 = (f32[320,128]{1,0:T(8,128)S(1)}, f32[320,128]{1,0:T(8,128)}, u32[]{:S(2)}) copy-start(f32[320,128]{1,0:T(8,128)} %copy-done.9) | copy-start | bytes 491524
  29.6 0.9 %copy-start.25 = (f32[320,128]{1,0:T(8,128)S(1)}, f32[320,128]{1,0:T(8,128)}, u32[]{:S(2)}) copy-start(f32[320,128]{1,0:T(8,128)} %refs_2_.3) | copy-start | bytes 491524
  30.6 0.8 copy-start.27
  31.3 0.8 %copy-start.39 = (bf16[128,192]{1,0:T(8,128)(2,1)S(1)}, bf16[128,192]{1,0:T(8,128)(2,1)}, u32[]{:S(2)}) copy-start(bf16[128,192]{1,0:T(8,128)(2,1)} %constant.5.clone.refs_6_.refs_5_) | copy-start | bytes 147460
  32.2 0.8 copy-start.42
  32.9 5.3 %copy-start.4 = (f32[320,128]{1,0:T(8,128)S(1)}, f32[320,128]{1,0:T(8,128)}, u32[]{:S(2)}) copy-start(f32[320,128]{1,0:T(8,128)} %refs_6_.6) | copy-start | bytes 491524
  36.1 0.7 copy-start.16
  38.2 1.5 %copy-start.1 = (bf16[768,1152]{1,0:T(8,128)(2,1)S(1)}, bf16[768,1152]{1,0:T(8,128)(2,1)}, u32[]{:S(2)}) copy-start(bf16[768,1152]{1,0:T(8,128)(2,1)} %copy-done) | copy-start | bytes 5308420
  39.7 0.9 %copy-start.8 = (bf16[160,720]{1,0:T(8,128)(2,1)S(1)}, bf16[160,720]{1,0:T(8,128)(2,1)}, u32[]{:S(2)}) copy-start(bf16[160,720]{1,0:T(8,128)(2,1)} %constant.4.clone.refs_11_.refs_10_) | copy-start | bytes 691204
  40.7 0.9 %copy-start.17 = (f32[320,128]{1,0:T(8,128)S(1)}, f32[320,128]{1,0:T(8,128)}, u32[]{:S(2)}) copy-start(f32[320,128]{1,0:T(8,128)} %copy-done.16) | copy-start | bytes 491524
  41.6 0.8 copy-start.21
  47.9 0.7 copy-start.5
  48.6 0.7 copy-start.13
  49.3 0.6 copy-start.29
  49.9 15.5 %all-to-all-start.1 = ((f32[16,40,128]{2,1,0:T(8,128)}), f32[16,40,128]{2,1,0:T(8,128)S(1)}, u32[]{:S(2)}, u32[]{:S(2)}) async-start(f32[16,40,128]{2,1,0:T(8,128)} %copy-done.5), calls=%async_computation.1 | async-start | bytes 655360 | tf_op jit(solution)/shard_map/all_to_all | solution.py:580
  54.4 8.1 %collective-permute-start.1 = (f32[80,128]{1,0:T(8,128)}, f32[80,128]{1,0:T(8,128)S(1)}, u32[]{:S(2)}, u32[]{:S(2)}) collective-permute-start(f32[80,128]{1,0:T(8,128)} %copy-done.29), channel_id=1, source_target_pairs={{0,16},{16,0},{1,17},{17,1},{2,18},{18,2},{3,19},{19,3},{4,20},{20... | collective-permute-start | bytes 122888 | tf_op jit(solution)/shard_map/ppermute | solution.py:574
  55.0 0.9 %copy-start.11 = (f32[320,128]{1,0:T(8,128)S(1)}, f32[320,128]{1,0:T(8,128)}, u32[]{:S(2)}) copy-start(f32[320,128]{1,0:T(8,128)} %copy-done.9) | copy-start | bytes 491524
  55.9 0.9 %copy-start.14 = (f32[320,128]{1,0:T(8,128)S(1)}, f32[320,128]{1,0:T(8,128)}, u32[]{:S(2)}) copy-start(f32[320,128]{1,0:T(8,128)} %copy-done.13) | copy-start | bytes 491524
  56.8 0.9 %copy-start.26 = (f32[320,128]{1,0:T(8,128)S(1)}, f32[320,128]{1,0:T(8,128)}, u32[]{:S(2)}) copy-start(f32[320,128]{1,0:T(8,128)} %refs_2_.3) | copy-start | bytes 491524
  57.8 0.8 copy-start.28
  58.5 0.8 %copy-start.40 = (bf16[128,192]{1,0:T(8,128)(2,1)S(1)}, bf16[128,192]{1,0:T(8,128)(2,1)}, u32[]{:S(2)}) copy-start(bf16[128,192]{1,0:T(8,128)(2,1)} %constant.5.clone.refs_6_.refs_5_) | copy-start | bytes 147460
  61.8 0.7 copy-start.18
  65.4 0.9 %copy-start.12 = (f32[320,128]{1,0:T(8,128)S(1)}, f32[320,128]{1,0:T(8,128)}, u32[]{:S(2)}) copy-start(f32[320,128]{1,0:T(8,128)} %copy-done.9) | copy-start | bytes 491524
  66.4 0.9 %copy-start.15 = (f32[320,128]{1,0:T(8,128)S(1)}, f32[320,128]{1,0:T(8,128)}, u32[]{:S(2)}) copy-start(f32[320,128]{1,0:T(8,128)} %copy-done.13) | copy-start | bytes 491524
  67.3 0.9 %copy-start.19 = (f32[320,128]{1,0:T(8,128)S(1)}, f32[320,128]{1,0:T(8,128)}, u32[]{:S(2)}) copy-start(f32[320,128]{1,0:T(8,128)} %copy-done.18) | copy-start | bytes 491524

commit v3 on v2

--- a/solution.py
+++ b/solution.py
@@ -409,11 +409,12 @@
     row_copy.wait()
 
 
-def finish_product(recv_ref, slab_ref, loads, work_ref):
-    received = jnp.concatenate([unpack_received(recv_ref), slab_ref[...]], axis=1)
-    near = mm(two_pieces(received), loads[0][...])
+def finish_product(loads, work_ref):
+    recv, slab = loads[0], loads[1]
+    received = jnp.concatenate([unpack_received(recv), slab[...]], axis=1)
+    near = mm(two_pieces(received), loads[2][...])
     near = near[:TILE] + near[TILE:]
-    coupling, local = loads[1], loads[2]
+    coupling, local = loads[3], loads[4]
     elements = local.shape[1]
     work_ref[...] = local[...]
     for f in range(FACES):
@@ -422,19 +423,18 @@
             f,
             -coupling[f * TILE : (f + 1) * TILE, :] * near[:, f * elements : (f + 1) * elements],
         )
-    inner = mm3(loads[3][0], loads[3][1], work_ref[...])
-    return mm3(loads[5][0], loads[5][1], loads[4][...] * inner)
+    inner = mm3(loads[5][0], loads[5][1], work_ref[...])
+    return mm3(loads[7][0], loads[7][1], loads[6][...] * inner)
 
 
 def middle_kernel(*refs):
-    recv, slab_in = refs[:2]
-    loads = Loads(refs[2:11], refs[14:23], refs[27])
-    outs, stage, work, sems = refs[11:14], refs[23:26], refs[26], refs[28]
+    loads = Loads(refs[:11], refs[14:25], refs[29])
+    outs, stage, work, sems = refs[11:14], refs[25:28], refs[28], refs[30]
     copies = [pltpu.make_async_copy(s, o, sems.at[i]) for i, (s, o) in enumerate(zip(stage, outs))]
     field, send, slab = stage
-    field[...] = finish_product(recv, slab_in, loads, work)
+    field[...] = finish_product(loads, work)
     copies[0].start()
-    pack_send(field, loads[6], loads[7][0:1, :], loads[8], send, slab)
+    pack_send(field, loads[8], loads[9][0:1, :], loads[10], send, slab)
     copies[1].start()
     copies[2].start()
     for copy in copies:
@@ -442,22 +442,26 @@
 
 
 def last_kernel(*refs):
-    recv, slab_in = refs[:2]
-    loads = Loads(refs[2:11], refs[12:21], refs[22])
-    out, work = refs[11], refs[21]
-    k2 = K2_SCALE * finish_product(recv, slab_in, loads, work)
-    row = loads[8][...] + put(
+    loads = Loads(refs[:11], refs[12:23], refs[25])
+    out, stage, work, sems = refs[11], refs[23], refs[24], refs[26]
+    k2 = K2_SCALE * finish_product(loads, work)
+    row = loads[10][...] + put(
         [
-            (3, total_of(k2 * loads[6][...])),
-            (4, total_of(k2 * loads[7][...])),
+            (3, total_of(k2 * loads[8][...])),
+            (4, total_of(k2 * loads[9][...])),
             (5, total_of(k2 * k2)),
         ]
     )
-    out[...] = jnp.broadcast_to(row.reshape(1, 1, 128), out.shape)
-
-
-def combine_kernel(rows_ref, start_ref, field_ref, out_ref, sems):
-    del sems
+    stage[...] = jnp.broadcast_to(row.reshape(1, 1, 128), stage.shape)
+    copy = pltpu.make_async_copy(stage, out, sems.at[0])
+    copy.start()
+    copy.wait()
+
+
+def combine_kernel(*refs):
+    loads = Loads(refs[:3], refs[4:7], refs[8])
+    out, stage, sems = refs[3], refs[7], refs[9]
+    rows_ref = loads[0]
     totals = jnp.sum(rows_ref[:, 0, :], axis=0, keepdims=True)
     lane = lane_row(128)
     g00, g01, g11, g02, g12, g22 = [
@@ -493,32 +497,30 @@
     y0 = (target0 - upper * y1) / radius0
     along1 = y1 / unit
     along0 = y0 / beta - along1 * h00
-    out_ref[...] = along0 * start_ref[...] + along1 * field_ref[...]
-
-
-def call(kernel, outs, args, held=0, staged=True, scratch=()):
-    in_vmem, in_place = pl.BlockSpec(memory_space=pltpu.VMEM), pl.BlockSpec(memory_space=pl.ANY)
-    moved = args[held:]
-    buffers = [pltpu.VMEM(a.shape, a.dtype) for a in moved]
+    stage[...] = along0 * loads[1][...] + along1 * loads[2][...]
+    copy = pltpu.make_async_copy(stage, out, sems.at[0])
+    copy.start()
+    copy.wait()
+
+
+def call(kernel, outs, args, scratch=()):
+    in_place = pl.BlockSpec(memory_space=pl.ANY)
     out_list = jax.tree.leaves(outs)
-    if staged:
-        buffers += [pltpu.VMEM(o.shape, o.dtype) for o in out_list]
+    buffers = [pltpu.VMEM(a.shape, a.dtype) for a in list(args) + out_list]
     buffers += list(scratch)
-    buffers.append(pltpu.SemaphoreType.DMA((max(len(moved), 1),)))
-    if staged:
-        buffers.append(pltpu.SemaphoreType.DMA((len(out_list),)))
+    buffers += [pltpu.SemaphoreType.DMA((len(args),)), pltpu.SemaphoreType.DMA((len(out_list),))]
     return pl.pallas_call(
         kernel,
         out_shape=outs,
-        in_specs=[in_vmem] * held + [in_place] * len(moved),
-        out_specs=jax.tree.map(lambda _: in_place if staged else in_vmem, outs),
+        in_specs=[in_place] * len(args),
+        out_specs=jax.tree.map(lambda _: in_place, outs),
         scratch_shapes=buffers,
         cost_estimate=pl.CostEstimate(
             flops=10**9,
             bytes_accessed=sum(a.size * a.dtype.itemsize for a in args),
             transcendentals=0,
         ),
-        compiler_params=pltpu.CompilerParams(vmem_limit_bytes=40 * 2**20),
+        compiler_params=pltpu.CompilerParams(vmem_limit_bytes=67043328),
     )(*args)
 
 
@@ -591,7 +593,6 @@
         middle_kernel,
         (field, send, slab),
         (recv0, slab0, recv_hot) + solve_args + (send_hot, codes, tiles),
-        held=2,
         scratch=[work],
     )
     recv1, slab1 = exchange(send1, slab1)
@@ -605,12 +606,10 @@
         last_kernel,
         struct((gx_size * groups, 1, 128), F32),
         (recv1, slab1, recv_hot) + solve_args + (k0, k1, partial),
-        held=2,
-        staged=False,
         scratch=[work],
     )
     rows = lax.all_to_all(rows, ("gx", "yz"), 0, 0, tiled=True)
-    return call(combine_kernel, field, (rows, k0, k1), held=3, staged=False)
+    return call(combine_kernel, field, (rows, k0, k1))
 
 
 def solution(mesh):

time: 84.1 us -> 59.9 us (0.71)
  local copies, waits for them, and re-layouts: 32.9 us -> 0 us
  waiting for transfers between devices: 4.46 us -> 13.2 us
    unnamed x86 -> x0, local copies, waits for them, and re-layouts: 32.9 us -> none
    all_to_all x2, waiting for transfers between devices: 4.46 us -> 13.2 us  [exchange(): return (lax.all_to_all(send, 'yz', 0, 0, tiled=True), slab)]
    ppermute x2, starting transfers between devices: 2.19 us -> 3.11 us  [exchange(): slab = lax.ppermute(slab, 'gx', up + down)]
  transfers between devices with their start and end apart: 4 -> 4, of which waited for: 2 -> 2; matrix products, arithmetic and copies ran while one was open for 0% -> 0% of each run, Pallas kernels for 7% -> 10%
where the time goes in v3:
time: 59.9 us; the launch traced here: 59.5 us
  Pallas kernels  21.2 us (35%)
  starting transfers between devices  14.8 us (25%)
  waiting for transfers between devices  13.2 us (22%)
  blocking collectives  10.2 us (17%)
    pallas_call x6, Pallas kernels, call(): pl.pallas_call(kernel, out_shape=outs, in_specs=[in_place] * len(args), o...  21.2 us
    all_to_all x2, waiting for transfers between devices, exchange(): return (lax.all_to_all(send, 'yz', 0, 0, tiled=True), slab)  13.2 us
    all_to_all x2, starting transfers between devices, exchange(): return (lax.all_to_all(send, 'yz', 0, 0, tiled=True), slab)  11.7 us
    all_to_all x1, blocking collectives, on_device(): rows = lax.all_to_all(rows, ('gx', 'yz'), 0, 0, tiled=True)  10.2 us
    ppermute x2, starting transfers between devices, exchange(): slab = lax.ppermute(slab, 'gx', up + down)  3.11 us
  transfers between devices with their start and end apart: 4, of which 2 were waited for; matrix products, arithmetic and copies ran while one was open for 0% of the time, Pallas kernels for 10%

profile of v3, /device:TPU:0, one launch (start us, length us, event | category | flops | bytes accessed | tf_op | source)
XLA Modules:
  0.0 59.5 jit_solution(10672910228661225104)
XLA Ops:
  0.0 4.7 %shard_map.163 = (f32[320,128]{1,0:T(8,128)}, f32[16,40,128]{2,1,0:T(8,128)}, f32[80,128]{1,0:T(8,128)}, bf16[768,1152]{1,0:T(8,128)(2,1)}, s32[8,1024]{1,0:T(8,...) custom-call(s32[1,352]{1,0:T(1,128)} %refs_0_.2, s32[1,352]{1,0:T(1,128)} %refs_1_.2, ...), custom_call_target="tpu_custom_call" | custom-call | flops 1000000000 | bytes 1383488 | tf_op jit(solution)/shard_map/pallas_call | solution.py:512
  4.7 7.5 %all-to-all-start = ((f32[16,40,128]{2,1,0:T(8,128)}), f32[16,40,128]{2,1,0:T(8,128)}, u32[]{:S(2)}, u32[]{:S(2)}) async-start(f32[16,40,128]{2,1,0:T(8,128)} %get-tuple-element.20), calls=%async_computation | async-start | bytes 655360 | tf_op jit(solution)/shard_map/all_to_all | solution.py:582
  12.2 1.6 %collective-permute-start = (f32[80,128]{1,0:T(8,128)}, f32[80,128]{1,0:T(8,128)}, u32[]{:S(2)}, u32[]{:S(2)}) collective-permute-start(f32[80,128]{1,0:T(8,128)} %get-tuple-element.21), channel_id=1, source_target_pairs={{0,16},{16,0},{1,17},{17,1},{2,18},{18,2},{3,19},{19,3},{4,20},{20... | collective-permute-start | bytes 122888 | tf_op jit(solution)/shard_map/ppermute | solution.py:576
  13.8 3.1 %shard_map.164 = (f32[320,128]{1,0:T(8,128)}, bf16[1152,768]{1,0:T(8,128)(2,1)}) custom-call(s32[8,1152]{1,0:T(8,128)} %get-tuple-element.22.refs_0_, s32[6,128]{1,0:T(8,128)} %refs_0_.3, f32[320,128]{1,0:T(8,128)} %get-tuple-element.23.refs_2_.refs_6_.refs_8_.refs_1_, f32[320,128]{1,0:T(8,128)} %refs_2_.3, f32[480,128]{1,0:T(8,128)} %refs_3_.9, ...), custom_call_target="tpu_custom_call" | custom-call | flops 1000000000 | bytes 700928 | tf_op jit(solution)/shard_map/pallas_call | solution.py:512
  16.8 0.0 collective-permute-done.refs_1_
  16.8 6.5 %all-to-all-done.refs_0_ = f32[16,40,128]{2,1,0:T(8,128)} async-done(((f32[16,40,128]{2,1,0:T(8,128)}), f32[16,40,128]{2,1,0:T(8,128)}, u32[]{:S(2)}, u32[]{:S(2)}) %all-to-all-start) | async-done | bytes 327712 | tf_op jit(solution)/shard_map/all_to_all | solution.py:582
  23.3 5.0 %shard_map.165 = (f32[320,128]{1,0:T(8,128)}, f32[16,40,128]{2,1,0:T(8,128)}, f32[80,128]{1,0:T(8,128)}) custom-call(f32[16,40,128]{2,1,0:T(8,128)} %all-to-all-done.refs_0_, f32[80,128]{1,0:T(8,128)} %collective-permute-done.refs_1_, bf16[1152,768]{1,0:T(8,128)(2,1)} %get-tuple-element.24.refs_2_, f32[480,128]{1,0:T(8,128)} %refs_3_.9, ...), custom_call_target="tpu_custom_call" | custom-call | flops 1000000000 | bytes 5563392 | tf_op jit(solution)/shard_map/pallas_call | solution.py:512
  28.3 4.2 %all-to-all-start.1 = ((f32[16,40,128]{2,1,0:T(8,128)}), f32[16,40,128]{2,1,0:T(8,128)}, u32[]{:S(2)}, u32[]{:S(2)}) async-start(f32[16,40,128]{2,1,0:T(8,128)} %get-tuple-element.30), calls=%async_computation.1 | async-start | bytes 655360 | tf_op jit(solution)/shard_map/all_to_all | solution.py:582
  32.5 1.6 %collective-permute-start.1 = (f32[80,128]{1,0:T(8,128)}, f32[80,128]{1,0:T(8,128)}, u32[]{:S(2)}, u32[]{:S(2)}) collective-permute-start(f32[80,128]{1,0:T(8,128)} %get-tuple-element.31), channel_id=1, source_target_pairs={{0,16},{16,0},{1,17},{17,1},{2,18},{18,2},{3,19},{19,3},{4,20},{20... | collective-permute-start | bytes 122888 | tf_op jit(solution)/shard_map/ppermute | solution.py:576
  34.1 2.8 %shard_map.166 = (f32[320,128]{1,0:T(8,128)}, f32[1,128]{1,0:T(1,128)}) custom-call(s32[6,128]{1,0:T(8,128)} %refs_0_.3, f32[320,128]{1,0:T(8,128)} %get-tuple-element.32.refs_1_.refs_9_.refs_2_, f32[320,128]{1,0:T(8,128)} %refs_2_.3, f32[480,128]{1,0:T(8,128)} %refs_3_.9, f32[75,128]{1,0:T(8,128)} %refs_4_.5, ...), custom_call_target="tpu_custom_call" | custom-call | flops 1000000000 | bytes 827904 | tf_op jit(solution)/shard_map/pallas_call | solution.py:512
  36.9 0.0 collective-permute-done.1.refs_1_
  36.9 6.7 %all-to-all-done.1.refs_0_ = f32[16,40,128]{2,1,0:T(8,128)} async-done(((f32[16,40,128]{2,1,0:T(8,128)}), f32[16,40,128]{2,1,0:T(8,128)}, u32[]{:S(2)}, u32[]{:S(2)}) %all-to-all-start.1) | async-done | bytes 327712 | tf_op jit(solution)/shard_map/all_to_all | solution.py:582
  43.6 4.0 %shard_map.167 = f32[32,1,128]{2,1,0:T(1,128)} custom-call(f32[16,40,128]{2,1,0:T(8,128)} %all-to-all-done.1.refs_0_, f32[80,128]{1,0:T(8,128)} %collective-permute-done.1.refs_1_, bf16[1152,768]{1,0:T(8,128)(2,1)} %get-tuple-element.24.refs_2_, f32[480,128]{1,0:T(8,128)} %refs_3_.9, f32[320,128]{1,0:T(8,128)} %get-tuple-element.33.refs_4_, ...), custom_call_target="tpu_custom_call" | custom-call | flops 1000000000 | bytes 3858944 | tf_op jit(solution)/shard_map/pallas_call | solution.py:512
  47.6 10.2 %all_to_all.15.refs_0_ = f32[32,1,128]{2,1,0:T(1,128)} all-to-all(f32[32,1,128]{2,1,0:T(1,128)} %shard_map.167), channel_id=1, replica_groups=mesh['gx'=2,'yz'=16] {'gx','yz'}, dimensions={0} | all-to-all | bytes 32768 | tf_op jit(solution)/shard_map/all_to_all | solution.py:611
  57.8 1.7 %shard_map.168 = f32[320,128]{1,0:T(8,128)} custom-call(f32[32,1,128]{2,1,0:T(1,128)} %all_to_all.15.refs_0_, f32[320,128]{1,0:T(8,128)} %get-tuple-element.23.refs_2_.refs_6_.refs_8_.refs_1_, f32[320,128]{1,0:T(8,128)} %get-tuple-element.32.refs_1_.refs_9_.refs_2_), custom_call_target="tpu_custom_call" | custom-call | flops 1000000000 | bytes 344064 | tf_op jit(solution)/shard_map/pallas_call | solution.py:512
Async XLA Ops:
  4.7 18.6 %all-to-all-start = ((f32[16,40,128]{2,1,0:T(8,128)}), f32[16,40,128]{2,1,0:T(8,128)}, u32[]{:S(2)}, u32[]{:S(2)}) async-start(f32[16,40,128]{2,1,0:T(8,128)} %get-tuple-element.20), calls=%async_computation | async-start | bytes 655360 | tf_op jit(solution)/shard_map/all_to_all | solution.py:582
  12.2 4.6 %collective-permute-start = (f32[80,128]{1,0:T(8,128)}, f32[80,128]{1,0:T(8,128)}, u32[]{:S(2)}, u32[]{:S(2)}) collective-permute-start(f32[80,128]{1,0:T(8,128)} %get-tuple-element.21), channel_id=1, source_target_pairs={{0,16},{16,0},{1,17},{17,1},{2,18},{18,2},{3,19},{19,3},{4,20},{20... | collective-permute-start | bytes 122888 | tf_op jit(solution)/shard_map/ppermute | solution.py:576
  28.3 15.3 %all-to-all-start.1 = ((f32[16,40,128]{2,1,0:T(8,128)}), f32[16,40,128]{2,1,0:T(8,128)}, u32[]{:S(2)}, u32[]{:S(2)}) async-start(f32[16,40,128]{2,1,0:T(8,128)} %get-tuple-element.30), calls=%async_computation.1 | async-start | bytes 655360 | tf_op jit(solution)/shard_map/all_to_all | solution.py:582
  32.5 4.4 %collective-permute-start.1 = (f32[80,128]{1,0:T(8,128)}, f32[80,128]{1,0:T(8,128)}, u32[]{:S(2)}, u32[]{:S(2)}) collective-permute-start(f32[80,128]{1,0:T(8,128)} %get-tuple-element.31), channel_id=1, source_target_pairs={{0,16},{16,0},{1,17},{17,1},{2,18},{18,2},{3,19},{19,3},{4,20},{20... | collective-permute-start | bytes 122888 | tf_op jit(solution)/shard_map/ppermute | solution.py:576

commit v4 on v3

--- a/solution.py
+++ b/solution.py
@@ -16,6 +16,7 @@
 FACES = 6
 HALF = 32
 K2_SCALE = 2.0**-20
+VMEM_LIMIT = 40 * 2**20
 F32 = jnp.float32
 BF16 = jnp.bfloat16
 
@@ -271,32 +272,54 @@
     return send_id, codes, recv_id
 
 
-class Loads:
-    def __init__(self, sources, buffers, sems):
-        self.buffers = list(buffers)
-        self.copies = [
-            pltpu.make_async_copy(s, b, sems.at[i])
-            for i, (s, b) in enumerate(zip(sources, buffers))
+class Refs:
+    def __init__(self, plan, refs):
+        arg_vmem, out_vmem = plan
+        refs = list(refs)
+        take = lambda n: [refs.pop(0) for _ in range(n)]
+        args, outs = take(len(arg_vmem)), take(len(out_vmem))
+        self.args = [a if v else refs.pop(0) for a, v in zip(args, arg_vmem)]
+        self.outs = [o if v else refs.pop(0) for o, v in zip(outs, out_vmem)]
+        in_sems, out_sems = take(2)
+        self.work = refs
+        self.pending = [
+            None if v else pltpu.make_async_copy(a, b, in_sems.at[i])
+            for i, (a, b, v) in enumerate(zip(args, self.args, arg_vmem))
         ]
-        for copy in self.copies:
-            copy.start()
-
-    def __getitem__(self, i):
-        if self.copies[i] is not None:
-            self.copies[i].wait()
-            self.copies[i] = None
-        return self.buffers[i]
-
-
-def start_kernel(sizes, *refs):
-    loads = Loads(refs[:12], refs[20:32], refs[40])
-    tables = [loads[i] for i in range(7)]
-    outs, stage, sems = refs[12:20], refs[32:40], refs[41]
-    field, send, slab, send_hot, codes_ref, recv_id_ref, first2, final2 = stage
-    copies = [pltpu.make_async_copy(s, o, sems.at[i]) for i, (s, o) in enumerate(zip(stage, outs))]
+        self.ships = [
+            None if v else pltpu.make_async_copy(b, o, out_sems.at[i])
+            for i, (o, b, v) in enumerate(zip(outs, self.outs, out_vmem))
+        ]
+        self.sent = []
+
+    def start(self):
+        for copy in self.pending:
+            if copy is not None:
+                copy.start()
+
+    def get(self, i):
+        if self.pending[i] is not None:
+            self.pending[i].wait()
+            self.pending[i] = None
+        return self.args[i]
+
+    def ship(self, i):
+        if self.ships[i] is not None:
+            self.ships[i].start()
+            self.sent.append(self.ships[i])
+
+    def finish(self):
+        for copy in self.sent:
+            copy.wait()
+
+
+def start_kernel(sizes, plan, *refs):
+    r = Refs(plan, refs)
+    r.start()
+    field, send, slab, send_hot, codes_ref, recv_id_ref, first2, final2 = r.outs
     elements = field.shape[1]
     groups = send.shape[0]
-    small, outq, inc, inq, coarse, band, plane = tables
+    small, outq, inc, inq, coarse, band, plane = [r.get(i) for i in range(7)]
     send_id, codes, recv_id = index_tables(
         small.shape[1] // groups,
         small[...],
@@ -310,23 +333,21 @@
         sizes,
     )
     codes_ref[...] = jnp.broadcast_to(codes, codes_ref.shape)
-    copies[4].start()
+    r.ship(4)
     recv_id_ref[...] = jnp.broadcast_to(recv_id, recv_id_ref.shape)
-    copies[5].start()
-    columns = lax.broadcasted_iota(jnp.int32, (FACES * elements, send_id.shape[1]), 0)
-    send_hot[...] = one_hot(columns == send_id)
-    copies[3].start()
-    first2[0], first2[1] = split(loads[7][...])
-    copies[6].start()
-    final2[0], final2[1] = split(loads[8][...])
-    copies[7].start()
-    field[...] = solve_cells(loads[9][...], first2, final2, loads[10])
-    copies[0].start()
-    pack_send(field, send_hot, codes, loads[11], send, slab)
-    copies[1].start()
-    copies[2].start()
-    for copy in copies:
-        copy.wait()
+    r.ship(5)
+    fill_send_hot(send_id, send_hot)
+    r.ship(3)
+    first2[0], first2[1] = split(r.get(7)[...])
+    r.ship(6)
+    final2[0], final2[1] = split(r.get(8)[...])
+    r.ship(7)
+    field[...] = solve_cells(r.get(9)[...], first2, final2, r.get(10))
+    r.ship(0)
+    pack_send(field, send_hot, codes, r.get(11), send, slab)
+    r.ship(1)
+    r.ship(2)
+    r.finish()
 
 
 def local_part(
@@ -363,21 +384,44 @@
         )
 
 
-def first_local_kernel(*refs):
-    loads = Loads(refs[:7], refs[9:16], refs[18])
-    (local_out, hot_out), (local, recv_hot), sems = refs[7:9], refs[16:18], refs[19]
-    elements = local.shape[1]
-    ids = jnp.transpose(loads[0][...])[:, 0:1]
-    adjacent = loads[1]
+def hold(r, outs, args):
+    copies = [
+        pltpu.make_async_copy(r.args[arg], r.outs[out], r.work[0].at[n])
+        for n, (out, arg) in enumerate(zip(outs, args))
+    ]
+    for copy in copies:
+        copy.start()
+    return copies
+
+
+def fill_received_hot(ids, adjacent, hot_ref):
+    elements = adjacent.shape[1]
+    column = jnp.transpose(ids)[:, 0:1]
     for f in range(FACES):
-        recv_hot[:, f * elements : (f + 1) * elements] = one_hot(ids == adjacent[f : f + 1, :])
-    hot_copy = pltpu.make_async_copy(recv_hot, hot_out, sems.at[0])
-    hot_copy.start()
-    local_part(loads[2], loads[3], loads[4], loads[5], adjacent, loads[6], local)
-    copy = pltpu.make_async_copy(local, local_out, sems.at[1])
-    copy.start()
-    copy.wait()
-    hot_copy.wait()
+        hot_ref[:, f * elements : (f + 1) * elements] = one_hot(column == adjacent[f : f + 1, :])
+
+
+def prepare(r):
+    local, recv_hot, coupling, first2 = r.outs[:4]
+    copies = hold(r, (2, 3), (2, 7))
+    r.start()
+    fill_received_hot(r.get(6)[...], r.get(4), recv_hot)
+    for copy in copies:
+        copy.wait()
+    local_part(r.get(0), r.get(1), coupling, r.get(3), r.get(4), r.get(5), local)
+
+
+def first_local_kernel(plan, *refs):
+    prepare(Refs(plan, refs))
+
+
+def second_local_kernel(plan, *refs):
+    r = Refs(plan, refs)
+    prepare(r)
+    k0, k1 = r.get(8)[...], r.get(0)[...]
+    r.outs[4][...] = put(
+        [(0, total_of(k0 * k0)), (1, total_of(k0 * k1)), (2, total_of(k1 * k1))]
+    )
 
 
 def total_of(x):
@@ -392,29 +436,16 @@
     return row
 
 
-def second_local_kernel(*refs):
-    loads = Loads(refs[:7], refs[9:16], refs[18])
-    (local_out, partial_out), (local, partial), sems = refs[7:9], refs[16:18], refs[19]
-    adjacent = loads[0]
-    local_part(loads[1], loads[2], loads[3], loads[4], adjacent, loads[5], local)
-    copy = pltpu.make_async_copy(local, local_out, sems.at[0])
-    copy.start()
-    k0, k1 = loads[6][...], loads[1][...]
-    partial[...] = put(
-        [(0, total_of(k0 * k0)), (1, total_of(k0 * k1)), (2, total_of(k1 * k1))]
-    )
-    row_copy = pltpu.make_async_copy(partial, partial_out, sems.at[1])
-    row_copy.start()
-    copy.wait()
-    row_copy.wait()
-
-
-def finish_product(loads, work_ref):
-    recv, slab = loads[0], loads[1]
-    received = jnp.concatenate([unpack_received(recv), slab[...]], axis=1)
-    near = mm(two_pieces(received), loads[2][...])
+def fill_send_hot(send_id, hot_ref):
+    columns = lax.broadcasted_iota(jnp.int32, hot_ref.shape, 0)
+    hot_ref[...] = one_hot(columns == send_id)
+
+
+def finish_product(r, work_ref):
+    received = jnp.concatenate([unpack_received(r.get(0)), r.get(1)[...]], axis=1)
+    near = mm(two_pieces(received), r.get(2)[...])
     near = near[:TILE] + near[TILE:]
-    coupling, local = loads[3], loads[4]
+    coupling, local = r.get(3), r.get(4)
     elements = local.shape[1]
     work_ref[...] = local[...]
     for f in range(FACES):
@@ -423,45 +454,47 @@
             f,
             -coupling[f * TILE : (f + 1) * TILE, :] * near[:, f * elements : (f + 1) * elements],
         )
-    inner = mm3(loads[5][0], loads[5][1], work_ref[...])
-    return mm3(loads[7][0], loads[7][1], loads[6][...] * inner)
-
-
-def middle_kernel(*refs):
-    loads = Loads(refs[:11], refs[14:25], refs[29])
-    outs, stage, work, sems = refs[11:14], refs[25:28], refs[28], refs[30]
-    copies = [pltpu.make_async_copy(s, o, sems.at[i]) for i, (s, o) in enumerate(zip(stage, outs))]
-    field, send, slab = stage
-    field[...] = finish_product(loads, work)
-    copies[0].start()
-    pack_send(field, loads[8], loads[9][0:1, :], loads[10], send, slab)
-    copies[1].start()
-    copies[2].start()
-    for copy in copies:
-        copy.wait()
-
-
-def last_kernel(*refs):
-    loads = Loads(refs[:11], refs[12:23], refs[25])
-    out, stage, work, sems = refs[11], refs[23], refs[24], refs[26]
-    k2 = K2_SCALE * finish_product(loads, work)
-    row = loads[10][...] + put(
+    first = r.get(5)
+    inner = mm3(first[0], first[1], work_ref[...])
+    final = r.get(7)
+    return mm3(final[0], final[1], r.get(6)[...] * inner)
+
+
+def middle_kernel(plan, *refs):
+    r = Refs(plan, refs)
+    r.start()
+    field, send, slab = r.outs
+    field[...] = finish_product(r, r.work[0])
+    r.ship(0)
+    pack_send(field, r.get(8), r.get(9)[0:1, :], r.get(10), send, slab)
+    r.ship(1)
+    r.ship(2)
+    r.finish()
+
+
+def last_kernel(plan, *refs):
+    r = Refs(plan, refs)
+    work = r.work[1]
+    fills = hold(r, (1, 2), (8, 9))
+    r.start()
+    rows, k0, k1 = r.outs
+    k2 = K2_SCALE * finish_product(r, work)
+    for fill in fills:
+        fill.wait()
+    row = r.get(10)[...] + put(
         [
-            (3, total_of(k2 * loads[8][...])),
-            (4, total_of(k2 * loads[9][...])),
+            (3, total_of(k2 * k0[...])),
+            (4, total_of(k2 * k1[...])),
             (5, total_of(k2 * k2)),
         ]
     )
-    stage[...] = jnp.broadcast_to(row.reshape(1, 1, 128), stage.shape)
-    copy = pltpu.make_async_copy(stage, out, sems.at[0])
-    copy.start()
-    copy.wait()
-
-
-def combine_kernel(*refs):
-    loads = Loads(refs[:3], refs[4:7], refs[8])
-    out, stage, sems = refs[3], refs[7], refs[9]
-    rows_ref = loads[0]
+    rows[...] = jnp.broadcast_to(row.reshape(1, 1, 128), rows.shape)
+
+
+def combine_kernel(plan, *refs):
+    r = Refs(plan, refs)
+    r.start()
+    rows_ref = r.get(0)
     totals = jnp.sum(rows_ref[:, 0, :], axis=0, keepdims=True)
     lane = lane_row(128)
     g00, g01, g11, g02, g12, g22 = [
@@ -497,31 +530,35 @@
     y0 = (target0 - upper * y1) / radius0
     along1 = y1 / unit
     along0 = y0 / beta - along1 * h00
-    stage[...] = along0 * loads[1][...] + along1 * loads[2][...]
-    copy = pltpu.make_async_copy(stage, out, sems.at[0])
-    copy.start()
-    copy.wait()
-
-
-def call(kernel, outs, args, scratch=()):
-    in_place = pl.BlockSpec(memory_space=pl.ANY)
-    out_list = jax.tree.leaves(outs)
-    buffers = [pltpu.VMEM(a.shape, a.dtype) for a in list(args) + out_list]
-    buffers += list(scratch)
-    buffers += [pltpu.SemaphoreType.DMA((len(args),)), pltpu.SemaphoreType.DMA((len(out_list),))]
+    r.outs[0][...] = along0 * r.get(1)[...] + along1 * r.get(2)[...]
+    r.ship(0)
+    r.finish()
+
+
+def call(kernel, outs, args, arg_spaces=None, out_spaces=None, scratch=()):
+    arg_spaces = arg_spaces or "h" * len(args)
+    out_spaces = out_spaces or "h" * len(outs)
+    space = lambda c: pltpu.VMEM if c == "v" else pltpu.HBM
+    plan = (tuple(c != "h" for c in arg_spaces), tuple(c != "h" for c in out_spaces))
+    buffers = [
+        pltpu.VMEM(a.shape, a.dtype)
+        for a, c in zip(tuple(args) + tuple(outs), arg_spaces + out_spaces)
+        if c == "h"
+    ]
+    buffers += [pltpu.SemaphoreType.DMA((len(args),)), pltpu.SemaphoreType.DMA((len(outs),))]
     return pl.pallas_call(
-        kernel,
-        out_shape=outs,
-        in_specs=[in_place] * len(args),
-        out_specs=jax.tree.map(lambda _: in_place, outs),
-        scratch_shapes=buffers,
+        functools.partial(kernel, plan),
+        out_shape=tuple(space(c)(o.shape, o.dtype) for o, c in zip(outs, out_spaces)),
+        in_specs=[pl.BlockSpec(memory_space=space(c)) for c in arg_spaces],
+        out_specs=tuple(pl.BlockSpec(memory_space=space(c)) for c in out_spaces),
+        scratch_shapes=buffers + list(scratch),
         cost_estimate=pl.CostEstimate(
             flops=10**9,
             bytes_accessed=sum(a.size * a.dtype.itemsize for a in args),
             transcendentals=0,
         ),
-        compiler_params=pltpu.CompilerParams(vmem_limit_bytes=67043328),
-    )(*args)
+        compiler_params=pltpu.CompilerParams(vmem_limit_bytes=VMEM_LIMIT),
+    )(*[pltpu.with_memory_space_constraint(a, space(c)) for a, c in zip(args, arg_spaces)])
 
 
 def on_device(
@@ -582,34 +619,47 @@
         return lax.all_to_all(send, "yz", 0, 0, tiled=True), slab
 
     recv0, slab0 = exchange(send0, slab0)
-    local0, recv_hot = call(
-        first_local_kernel,
-        (field, struct((lanes + 128, traces), BF16)),
-        (recv_id, adjacent, k0, mass, coupling, flux, volume),
-    )
+    copy_sems = pltpu.SemaphoreType.DMA((2,))
     work = pltpu.VMEM((DOFS, elements), F32)
-    solve_args = (coupling, local0, first2, mid, final2)
+    held = (
+        field,
+        struct((lanes + 128, traces), BF16),
+        struct(coupling.shape, F32),
+        struct(first2.shape, BF16),
+    )
+    local_args = lambda u: (u, mass, coupling, flux, adjacent, volume, recv_id, first2)
+    local, recv_hot, near_coupling, near_first = call(
+        first_local_kernel, held, local_args(k0), "hhrhhhhr", "vvvv", scratch=[copy_sems]
+    )
     k1, send1, slab1 = call(
         middle_kernel,
         (field, send, slab),
-        (recv0, slab0, recv_hot) + solve_args + (send_hot, codes, tiles),
+        (recv0, slab0, recv_hot, near_coupling, local, near_first)
+        + (mid, final2, send_hot, codes, tiles),
+        "vvvvvvhhhhh",
         scratch=[work],
     )
     recv1, slab1 = exchange(send1, slab1)
-    local1, partial = call(
+    local, recv_hot, near_coupling, near_first, partial = call(
         second_local_kernel,
-        (field, struct((1, 128), F32)),
-        (adjacent, k1, mass, coupling, flux, volume, k0),
-    )
-    solve_args = (coupling, local1, first2, mid, final2)
-    rows = call(
+        held + (struct((1, 128), F32),),
+        local_args(k1) + (k0,),
+        "hhrhhhhrh",
+        "vvvvv",
+        scratch=[copy_sems],
+    )
+    rows, k0, k1 = call(
         last_kernel,
-        struct((gx_size * groups, 1, 128), F32),
-        (recv1, slab1, recv_hot) + solve_args + (k0, k1, partial),
-        scratch=[work],
+        (struct((gx_size * groups, 1, 128), F32), field, field),
+        (recv1, slab1, recv_hot, near_coupling, local, near_first)
+        + (mid, final2, k0, k1, partial),
+        "vvvvvvhhrrv",
+        "vvv",
+        scratch=[copy_sems, work],
     )
     rows = lax.all_to_all(rows, ("gx", "yz"), 0, 0, tiled=True)
-    return call(combine_kernel, field, (rows, k0, k1))
+    (update,) = call(combine_kernel, (field,), (rows, k0, k1), "vvv")
+    return update
 
 
 def solution(mesh):

time: 59.9 us -> 56 us (0.935)
  Pallas kernels: 21.2 us -> 18.2 us
  starting transfers between devices: 14.8 us -> 14.1 us
    pallas_call x6, Pallas kernels: 21.2 us -> 18.2 us  [call(): pl.pallas_call(functools.partial(kernel, plan), out_shape=tuple((space(c)...]
    all_to_all x2, starting transfers between devices: 11.7 us -> 11 us  [exchange(): return (lax.all_to_all(send, 'yz', 0, 0, tiled=True), slab)]
where the time goes in v4:
time: 56 us; the launch traced here: 55.6 us
  Pallas kernels  18.2 us (32%)
  starting transfers between devices  14.1 us (25%)
  waiting for transfers between devices  13.2 us (24%)
  blocking collectives  10.1 us (18%)
    pallas_call x6, Pallas kernels, call(): pl.pallas_call(functools.partial(kernel, plan), out_shape=tuple((space(c)...  18.2 us
    all_to_all x2, waiting for transfers between devices, exchange(): return (lax.all_to_all(send, 'yz', 0, 0, tiled=True), slab)  13.2 us
    all_to_all x2, starting transfers between devices, exchange(): return (lax.all_to_all(send, 'yz', 0, 0, tiled=True), slab)  11 us
    all_to_all x1, blocking collectives, on_device(): rows = lax.all_to_all(rows, ('gx', 'yz'), 0, 0, tiled=True)  10.1 us
    ppermute x2, starting transfers between devices, exchange(): slab = lax.ppermute(slab, 'gx', up + down)  3.12 us
  transfers between devices with their start and end apart: 4, of which 2 were waited for; matrix products, arithmetic and copies ran while one was open for 0% of the time, Pallas kernels for 10%

profile of v4, /device:TPU:0, one launch (start us, length us, event | category | flops | bytes accessed | tf_op | source)
XLA Modules:
  0.0 55.6 jit_solution(12550728256149933611)
XLA Ops:
  0.0 4.7 %shard_map.163 = (f32[320,128]{1,0:T(8,128)}, f32[16,40,128]{2,1,0:T(8,128)}, f32[80,128]{1,0:T(8,128)}, bf16[768,1152]{1,0:T(8,128)(2,1)}, s32[8,1024]{1,0:T(8,...) custom-call(s32[1,352]{1,0:T(1,128)} %refs_0_.1, s32[1,352]{1,0:T(1,128)} %refs_1_.3, ...), custom_call_target="tpu_custom_call" | custom-call | flops 1000000000 | bytes 1383488 | tf_op jit(solution)/shard_map/pallas_call | solution.py:549
  4.7 7.4 %all-to-all-start = ((f32[16,40,128]{2,1,0:T(8,128)}), f32[16,40,128]{2,1,0:T(8,128)S(1)}, u32[]{:S(2)}, u32[]{:S(2)}) async-start(f32[16,40,128]{2,1,0:T(8,128)} %get-tuple-element.28), calls=%async_computation | async-start | bytes 655360 | tf_op jit(solution)/shard_map/all_to_all | solution.py:619
  12.1 1.6 %collective-permute-start = (f32[80,128]{1,0:T(8,128)}, f32[80,128]{1,0:T(8,128)S(1)}, u32[]{:S(2)}, u32[]{:S(2)}) collective-permute-start(f32[80,128]{1,0:T(8,128)} %get-tuple-element.29), channel_id=1, source_target_pairs={{0,16},{16,0},{1,17},{17,1},{2,18},{18,2},{3,19},{19,3},{4,20},{20... | collective-permute-start | bytes 122888 | tf_op jit(solution)/shard_map/ppermute | solution.py:613
  13.7 2.9 %shard_map.164 = (f32[320,128]{1,0:T(8,128)S(1)}, bf16[1152,768]{1,0:T(8,128)(2,1)S(1)}, f32[480,128]{1,0:T(8,128)S(1)}, bf16[2,320,320]{2,1,0:T(8,128)(2,1)S(1)}) custom-call(f32[320,128]{1,0:T(8,128)} %get-tuple-element.30.refs_0_.refs_8_, f32[320,128]{1,0:T(8,128)} %refs_1_.5, f32[480,128]{1,0:T(8,128)} %refs_2_.5, f32[75,128]{1,0:T(8,128)} %refs_3_.5, ...), custom_call_target="tpu_custom_call" | custom-call | flops 1000000000 | bytes 1110528 | tf_op jit(solution)/shard_map/pallas_call | solution.py:549
  16.6 0.0 collective-permute-done.refs_1_
  16.6 6.6 %all-to-all-done.refs_0_ = f32[16,40,128]{2,1,0:T(8,128)S(1)} async-done(((f32[16,40,128]{2,1,0:T(8,128)}), f32[16,40,128]{2,1,0:T(8,128)S(1)}, u32[]{:S(2)}, u32[]{:S(2)}) %all-to-all-start) | async-done | bytes 327712 | tf_op jit(solution)/shard_map/all_to_all | solution.py:619
  23.2 4.6 %shard_map.165 = (f32[320,128]{1,0:T(8,128)}, f32[16,40,128]{2,1,0:T(8,128)}, f32[80,128]{1,0:T(8,128)}) custom-call(f32[16,40,128]{2,1,0:T(8,128)S(1)} %all-to-all-done.refs_0_, f32[80,128]{1,0:T(8,128)S(1)} %collective-permute-done.refs_1_, bf16[1152,768]{1,0:T(8,128)(2,1)S(1)} %get-tuple-element.33.refs_2_, f32[480,128]{1,0:T(8,128)S(1)} %get-tuple-element.34.refs_3_, ...), custom_call_target="tpu_custom_call" | custom-call | flops 1000000000 | bytes 5563392 | tf_op jit(solution)/shard_map/pallas_call | solution.py:549
  27.8 3.6 %all-to-all-start.1 = ((f32[16,40,128]{2,1,0:T(8,128)}), f32[16,40,128]{2,1,0:T(8,128)S(1)}, u32[]{:S(2)}, u32[]{:S(2)}) async-start(f32[16,40,128]{2,1,0:T(8,128)} %get-tuple-element.40), calls=%async_computation.1 | async-start | bytes 655360 | tf_op jit(solution)/shard_map/all_to_all | solution.py:619
  31.4 1.6 %collective-permute-start.1 = (f32[80,128]{1,0:T(8,128)}, f32[80,128]{1,0:T(8,128)S(1)}, u32[]{:S(2)}, u32[]{:S(2)}) collective-permute-start(f32[80,128]{1,0:T(8,128)} %get-tuple-element.41), channel_id=1, source_target_pairs={{0,16},{16,0},{1,17},{17,1},{2,18},{18,2},{3,19},{19,3},{4,20},{20... | collective-permute-start | bytes 122888 | tf_op jit(solution)/shard_map/ppermute | solution.py:613
  33.0 2.9 %shard_map.166 = (f32[320,128]{1,0:T(8,128)S(1)}, bf16[1152,768]{1,0:T(8,128)(2,1)S(1)}, f32[480,128]{1,0:T(8,128)S(1)}, bf16[2,320,320]{2,1,0:T(8,128)(2,1)S(1)}, f32[1,128]{1,0:T(1,128)S(1)}) custom-call(f32[320,128]{1,0:T(8,128)} %get-tuple-element.42.refs_0_.refs_9_, f32[320,128]{1,0:T(8,128)} %refs_1_.5, f32[480,128]{1,0:T(8,128)} %refs_2_.5, ...), custom_call_target="tpu_custom_call" | custom-call | flops 1000000000 | bytes 1274368 | tf_op jit(solution)/shard_map/pallas_call | solution.py:549
  35.9 0.0 collective-permute-done.1.refs_1_
  35.9 6.6 %all-to-all-done.1.refs_0_ = f32[16,40,128]{2,1,0:T(8,128)S(1)} async-done(((f32[16,40,128]{2,1,0:T(8,128)}), f32[16,40,128]{2,1,0:T(8,128)S(1)}, u32[]{:S(2)}, u32[]{:S(2)}) %all-to-all-start.1) | async-done | bytes 327712 | tf_op jit(solution)/shard_map/all_to_all | solution.py:619
  42.4 2.2 %shard_map.167 = (f32[32,1,128]{2,1,0:T(1,128)S(1)}, f32[320,128]{1,0:T(8,128)S(1)}, f32[320,128]{1,0:T(8,128)S(1)}) custom-call(f32[16,40,128]{2,1,0:T(8,128)S(1)} %all-to-all-done.1.refs_0_, f32[80,128]{1,0:T(8,128)S(1)} %collective-permute-done.1.refs_1_, bf16[1152,768]{1,0:T(8,128)(2,1)S(1)} %get-tuple-element.43.refs_2_, ...), custom_call_target="tpu_custom_call" | custom-call | flops 1000000000 | bytes 3858944 | tf_op jit(solution)/shard_map/pallas_call | solution.py:549
  44.6 10.1 %all_to_all.15.refs_0_ = f32[32,1,128]{2,1,0:T(1,128)S(1)} all-to-all(f32[32,1,128]{2,1,0:T(1,128)S(1)} %get-tuple-element.48), channel_id=1, replica_groups=mesh['gx'=2,'yz'=16] {'gx','yz'}, dimensions={0} | all-to-all | bytes 32768 | tf_op jit(solution)/shard_map/all_to_all | solution.py:660
  54.7 0.9 %shard_map.168 = f32[320,128]{1,0:T(8,128)} custom-call(f32[32,1,128]{2,1,0:T(1,128)S(1)} %all_to_all.15.refs_0_, f32[320,128]{1,0:T(8,128)S(1)} %get-tuple-element.49.refs_1_, f32[320,128]{1,0:T(8,128)S(1)} %get-tuple-element.50.refs_2_), custom_call_target="tpu_custom_call" | custom-call | flops 1000000000 | bytes 344064 | tf_op jit(solution)/shard_map/pallas_call | solution.py:549
Async XLA Ops:
  4.7 18.5 %all-to-all-start = ((f32[16,40,128]{2,1,0:T(8,128)}), f32[16,40,128]{2,1,0:T(8,128)S(1)}, u32[]{:S(2)}, u32[]{:S(2)}) async-start(f32[16,40,128]{2,1,0:T(8,128)} %get-tuple-element.28), calls=%async_computation | async-start | bytes 655360 | tf_op jit(solution)/shard_map/all_to_all | solution.py:619
  12.1 4.4 %collective-permute-start = (f32[80,128]{1,0:T(8,128)}, f32[80,128]{1,0:T(8,128)S(1)}, u32[]{:S(2)}, u32[]{:S(2)}) collective-permute-start(f32[80,128]{1,0:T(8,128)} %get-tuple-element.29), channel_id=1, source_target_pairs={{0,16},{16,0},{1,17},{17,1},{2,18},{18,2},{3,19},{19,3},{4,20},{20... | collective-permute-start | bytes 122888 | tf_op jit(solution)/shard_map/ppermute | solution.py:613
  27.8 14.6 %all-to-all-start.1 = ((f32[16,40,128]{2,1,0:T(8,128)}), f32[16,40,128]{2,1,0:T(8,128)S(1)}, u32[]{:S(2)}, u32[]{:S(2)}) async-start(f32[16,40,128]{2,1,0:T(8,128)} %get-tuple-element.40), calls=%async_computation.1 | async-start | bytes 655360 | tf_op jit(solution)/shard_map/all_to_all | solution.py:619
  31.4 4.5 %collective-permute-start.1 = (f32[80,128]{1,0:T(8,128)}, f32[80,128]{1,0:T(8,128)S(1)}, u32[]{:S(2)}, u32[]{:S(2)}) collective-permute-start(f32[80,128]{1,0:T(8,128)} %get-tuple-element.41), channel_id=1, source_target_pairs={{0,16},{16,0},{1,17},{17,1},{2,18},{18,2},{3,19},{19,3},{4,20},{20... | collective-permute-start | bytes 122888 | tf_op jit(solution)/shard_map/ppermute | solution.py:613

commit v5 on v4

--- a/solution.py
+++ b/solution.py
@@ -14,7 +14,7 @@
 TILE = VARS * NODES * NODES
 DOFS = TILE * NODES
 FACES = 6
-HALF = 32
+STRIDE = 64
 K2_SCALE = 2.0**-20
 VMEM_LIMIT = 40 * 2**20
 F32 = jnp.float32
@@ -63,7 +63,7 @@
 def constant_matrices():
     derivative, interpolate, project = gll_tables()
     eye_vars = np.eye(VARS)
-    blocks = [np.kron(eye_vars, m) for m in project + interpolate] + [np.eye(TILE)]
+    blocks = [np.kron(eye_vars, m) for m in project + interpolate]
     tiles = np.concatenate(pieces(np.concatenate(blocks, axis=1)), axis=0)
     eye = np.eye(4)
     volume = np.concatenate(
@@ -142,49 +142,95 @@
     return lax.broadcasted_iota(jnp.int32, (1, length), 1)
 
 
-def pack_send(field_ref, send_hot_ref, codes, tiles_ref, send_ref, slab_ref):
+def fold_plan(columns):
+    for rows in range(8, TILE + 1, 8):
+        full, rest = TILE // rows, TILE % rows
+        parts = rows // rest if rest else 1
+        width = -(-columns // parts) if rest else 0
+        if full * columns + width <= 128:
+            break
+    plan = [(g * rows, rows, 0, columns, 0, g * columns) for g in range(full)]
+    if rest:
+        for part in range(parts):
+            count = min(width, columns - part * width)
+            if count > 0:
+                plan.append(
+                    (full * rows, rest, part * width, count, part * rest, full * columns)
+                )
+    return rows, plan
+
+
+def roll_lanes(x, shift):
+    return pltpu.roll(x, shift % 128, 1) if shift % 128 else x
+
+
+def in_lanes(start, count):
+    lane = lane_row(128)
+    return (lane >= start) & (lane < start + count)
+
+
+def fold_halves(block):
+    middle = TILE // 2
+    return jnp.where(
+        lane_row(128) < STRIDE, block[:middle], roll_lanes(block[middle:], STRIDE)
+    )
+
+
+def unfold_halves(block):
+    return jnp.concatenate([block, roll_lanes(block, STRIDE)], axis=0)
+
+
+def pack_send(field_ref, send_hot_ref, codes, tiles_ref, send_ref, halo_ref, cap):
     groups = send_ref.shape[0]
-    lanes = groups * 2 * HALF
+    lanes = groups * STRIDE
     gathered = mm(two_pieces(all_traces(field_ref)), send_hot_ref[...])
     high, low = gathered[:TILE], gathered[TILE:]
-    slab_ref[...] = high[:, lanes:] + low[:, lanes:]
+    halo_ref[...] = fold_halves(high[:, lanes:] + low[:, lanes:])
     high, low = high[:, :lanes].astype(BF16), low[:, :lanes].astype(BF16)
-    masks = [one_hot(codes == q) for q in range(9)]
+    masks = [one_hot(codes == q) for q in range(8)]
     high_stack = jnp.concatenate([high * m for m in masks], axis=0)
     low_stack = jnp.concatenate([low * m for m in masks], axis=0)
     result = mm(tiles_ref[...], high_stack)
     result = result[:TILE] + (result[TILE:] + mm(tiles_ref[:TILE], low_stack))
-    left = lane_row(128) < 2 * HALF
-    middle = TILE // 2
-    for pair in range(groups // 2):
-        block = result[:, pair * 128 : pair * 128 + 128]
-        top, bottom = block[:middle], block[middle:]
-        send_ref[2 * pair] = jnp.where(left, top, pltpu.roll(bottom, 64, 1))
-        send_ref[2 * pair + 1] = jnp.where(left, pltpu.roll(top, 64, 1), bottom)
-
-
-def unpack_received(recv_ref):
-    left = lane_row(128) < 2 * HALF
+    rows, plan = fold_plan(2 * cap)
+    for group in range(groups):
+        block = result[:, group // 2 * 128 : group // 2 * 128 + 128]
+        base = group % 2 * STRIDE
+        folded = [None] * (rows // 8)
+        for row, count, column, width, to_row, to_lane in plan:
+            for k in range(count // 8):
+                part = roll_lanes(block[row + 8 * k : row + 8 * k + 8], to_lane - base - column)
+                at = to_row // 8 + k
+                if folded[at] is not None:
+                    part = jnp.where(in_lanes(to_lane, width), part, folded[at])
+                folded[at] = part
+        send_ref[group] = jnp.concatenate(folded, axis=0)
+
+
+def unpack_received(recv_ref, cap):
+    rows, plan = fold_plan(2 * cap)
     blocks = []
     for pair in range(recv_ref.shape[0] // 2):
-        even, odd = recv_ref[2 * pair], recv_ref[2 * pair + 1]
-        top = jnp.where(left, even, pltpu.roll(odd, 64, 1))
-        bottom = jnp.where(left, pltpu.roll(even, 64, 1), odd)
-        blocks.append(jnp.concatenate([top, bottom], axis=0))
+        wide = [None] * (TILE // 8)
+        for side in range(2):
+            block = recv_ref[2 * pair + side]
+            base = side * STRIDE
+            for row, count, column, width, to_row, to_lane in plan:
+                for k in range(count // 8):
+                    part = roll_lanes(
+                        block[to_row + 8 * k : to_row + 8 * k + 8], base + column - to_lane
+                    )
+                    at = row // 8 + k
+                    if wide[at] is not None:
+                        part = jnp.where(in_lanes(base + column, width), part, wide[at])
+                    wide[at] = part
+        blocks.append(jnp.concatenate(wide, axis=0))
     return jnp.concatenate(blocks, axis=1)
-
-
-def place_lanes(rows, groups, cap):
-    lane = lane_row(groups * 2 * HALF)
-    within = lane % HALF
-    target = jnp.where(within < cap, (lane // (2 * HALF)) * cap + within, -1)
-    slots = lax.broadcasted_iota(jnp.int32, (rows.shape[1], lane.shape[1]), 0)
-    return mm(rows, one_hot(slots == target))
 
 
 def index_tables(cap, small, outq, inc, inq, coarse, band, plane, elements, sizes):
     gx_size, groups = sizes
-    gx_index, yz_index = lax.axis_index("gx"), lax.axis_index("yz")
+    gx_index = lax.axis_index("gx")
     hang, halo = coarse.shape[1], band.shape[1]
     traces = FACES * elements
     as_f = lambda x: x.astype(F32)
@@ -209,66 +255,41 @@
         ],
         axis=0,
     ).astype(BF16)
-    placed = place_lanes(rows, groups, cap).astype(jnp.int32)
-    lane = lane_row(groups * 2 * HALF)
-    group, within, second = lane // (2 * HALF), lane % HALF, (lane // HALF) % 2
-    is_slot = within < cap
-    step = halo // 2
-    side = (within >= cap) & (within < cap + step)
-    position = within - cap + step * second
-    up = lax.rem(yz_index + 1, groups)
-    down = lax.rem(yz_index + groups - 1, groups)
-    slab_lane = lane_row(128)
-    target = jnp.concatenate(
-        [
-            jnp.where(side, position, -1),
-            jnp.where(slab_lane < 2 * halo, slab_lane % halo, -1),
-        ],
-        axis=1,
-    )
-    slots = lax.broadcasted_iota(jnp.int32, (halo, target.shape[1]), 0)
-    halo_rows = jnp.concatenate([as_f(band), as_f(plane), jnp.zeros((4, halo), F32)], axis=0)
+    lane = lane_row(groups * STRIDE)
+    group, within = lane // STRIDE, lane % STRIDE
+    is_fine, is_used = within < cap, within < 2 * cap
+    slot = group * cap + jnp.where(is_fine, within, within - cap)
+    slots = lax.broadcasted_iota(jnp.int32, (rows.shape[1], lane.shape[1]), 0)
+    placed = mm(rows, one_hot(slots == jnp.where(is_used, slot, -1))).astype(jnp.int32)
+    send_id = jnp.where(
+        is_fine, placed[0:1] * 8 + placed[1:2], placed[2:3] * 8 + placed[3:4]
+    )
+    send_id = jnp.where(is_used, send_id, traces)
+    codes = jnp.where(is_fine, placed[4:5], 4 + placed[5:6])
+    first_hang = traces + 4 * halo
+    mortar = placed[6:7]
+    recv_id = jnp.where(
+        is_fine, jnp.where(mortar < hang, first_hang + mortar, -1), first_hang + hang + slot
+    )
+    recv_id = jnp.where(is_used, recv_id, -1)
+
+    edge_lane = lane_row(128)
+    target = jnp.where(edge_lane < 4 * halo, edge_lane % halo, -1)
+    slots = lax.broadcasted_iota(jnp.int32, (halo, 128), 0)
+    halo_rows = jnp.concatenate([as_f(plane), as_f(band), jnp.zeros((4, halo), F32)], axis=0)
     edge = mm(halo_rows.astype(BF16), one_hot(slots == target)).astype(jnp.int32)
-    lanes = lane.shape[1]
-    side_send = jnp.where(
-        group == up,
-        3 * elements + edge[1:2, :lanes],
-        jnp.where(group == down, 2 * elements + edge[0:1, :lanes], traces),
-    )
-    slot_id = jnp.where(
-        second == 0, placed[0:1] * 8 + placed[1:2], placed[2:3] * 8 + placed[3:4]
-    )
-    send_id = jnp.where(is_slot, slot_id, jnp.where(side, side_send, traces))
-    codes = jnp.where(
-        is_slot, jnp.where(second == 0, placed[4:5], 4 + placed[5:6]), 8
-    )
-    slab_id = jnp.where(
-        slab_lane < halo,
-        edge[2:3, lanes:],
-        jnp.where(slab_lane < 2 * halo, elements + edge[3:4, lanes:], traces),
-    )
-    send_id = jnp.concatenate([send_id, slab_id], axis=1)
-
-    first_hang = traces + 4 * halo
-    side_recv = jnp.where(
-        group == down,
-        traces + 2 * halo + position,
-        jnp.where(group == up, traces + 3 * halo + position, -1),
-    )
-    mortar = placed[6:7]
-    fine_recv = jnp.where(mortar < hang, first_hang + mortar, -1)
-    reply_recv = first_hang + hang + group * cap + within
-    recv_id = jnp.where(
-        is_slot, jnp.where(second == 0, fine_recv, reply_recv), jnp.where(side, side_recv, -1)
-    )
-    from_upper = (slab_lane < halo) & (gx_index < gx_size - 1)
-    from_lower = (slab_lane >= halo) & (slab_lane < 2 * halo) & (gx_index > 0)
-    slab_recv = jnp.where(
-        from_upper,
-        traces + halo + slab_lane,
-        jnp.where(from_lower, traces + slab_lane - halo, -1),
-    )
-    recv_id = jnp.concatenate([recv_id, slab_recv], axis=1)
+    halo_id = jnp.zeros_like(edge_lane) + traces
+    halo_recv = jnp.zeros_like(edge_lane) - 1
+    present = (gx_index < gx_size - 1, gx_index > 0, True, True)
+    starts = (traces + halo, traces, traces + 3 * halo, traces + 2 * halo)
+    for face in range(4):
+        here = edge_lane // halo == face
+        halo_id = jnp.where(here, face * elements + edge[face : face + 1], halo_id)
+        halo_recv = jnp.where(
+            here & present[face], starts[face] + edge_lane - face * halo, halo_recv
+        )
+    send_id = jnp.concatenate([send_id, halo_id], axis=1)
+    recv_id = jnp.concatenate([recv_id, halo_recv], axis=1)
     return send_id, codes, recv_id
 
 
@@ -316,7 +337,7 @@
 def start_kernel(sizes, plan, *refs):
     r = Refs(plan, refs)
     r.start()
-    field, send, slab, send_hot, codes_ref, recv_id_ref, first2, final2 = r.outs
+    field, send, edge, send_hot, codes_ref, recv_id_ref, first2, final2 = r.outs
     elements = field.shape[1]
     groups = send.shape[0]
     small, outq, inc, inq, coarse, band, plane = [r.get(i) for i in range(7)]
@@ -344,7 +365,7 @@
     r.ship(7)
     field[...] = solve_cells(r.get(9)[...], first2, final2, r.get(10))
     r.ship(0)
-    pack_send(field, send_hot, codes, r.get(11), send, slab)
+    pack_send(field, send_hot, codes, r.get(11), send, edge, small.shape[1] // groups)
     r.ship(1)
     r.ship(2)
     r.finish()
@@ -441,11 +462,17 @@
     hot_ref[...] = one_hot(columns == send_id)
 
 
-def finish_product(r, work_ref):
-    received = jnp.concatenate([unpack_received(r.get(0)), r.get(1)[...]], axis=1)
-    near = mm(two_pieces(received), r.get(2)[...])
+def finish_product(sizes, r, work_ref):
+    cap, halo = sizes
+    upper, lower, after, before = [r.get(i)[...] for i in range(1, 5)]
+    face = lane_row(128) % STRIDE // halo
+    edge = jnp.where(
+        face < 2, jnp.where(face < 1, upper, lower), jnp.where(face < 3, after, before)
+    )
+    received = jnp.concatenate([unpack_received(r.get(0), cap), unfold_halves(edge)], axis=1)
+    near = mm(two_pieces(received), r.get(5)[...])
     near = near[:TILE] + near[TILE:]
-    coupling, local = r.get(3), r.get(4)
+    coupling, local = r.get(6), r.get(7)
     elements = local.shape[1]
     work_ref[...] = local[...]
     for f in range(FACES):
@@ -454,34 +481,34 @@
             f,
             -coupling[f * TILE : (f + 1) * TILE, :] * near[:, f * elements : (f + 1) * elements],
         )
-    first = r.get(5)
+    first = r.get(8)
     inner = mm3(first[0], first[1], work_ref[...])
-    final = r.get(7)
-    return mm3(final[0], final[1], r.get(6)[...] * inner)
-
-
-def middle_kernel(plan, *refs):
+    final = r.get(10)
+    return mm3(final[0], final[1], r.get(9)[...] * inner)
+
+
+def middle_kernel(sizes, plan, *refs):
     r = Refs(plan, refs)
     r.start()
-    field, send, slab = r.outs
-    field[...] = finish_product(r, r.work[0])
+    field, send, edge = r.outs
+    field[...] = finish_product(sizes, r, r.work[0])
     r.ship(0)
-    pack_send(field, r.get(8), r.get(9)[0:1, :], r.get(10), send, slab)
+    pack_send(field, r.get(11), r.get(12)[0:1, :], r.get(13), send, edge, sizes[0])
     r.ship(1)
     r.ship(2)
     r.finish()
 
 
-def last_kernel(plan, *refs):
+def last_kernel(sizes, plan, *refs):
     r = Refs(plan, refs)
     work = r.work[1]
-    fills = hold(r, (1, 2), (8, 9))
+    fills = hold(r, (1, 2), (11, 12))
     r.start()
     rows, k0, k1 = r.outs
-    k2 = K2_SCALE * finish_product(r, work)
+    k2 = K2_SCALE * finish_product(sizes, r, work)
     for fill in fills:
         fill.wait()
-    row = r.get(10)[...] + put(
+    row = r.get(13)[...] + put(
         [
             (3, total_of(k2 * k0[...])),
             (4, total_of(k2 * k1[...])),
@@ -584,18 +611,19 @@
     gx_size, groups = lax.axis_size("gx"), lax.axis_size("yz")
     elements = source.shape[1]
     traces = FACES * elements
-    lanes = groups * 2 * HALF
+    lanes = groups * STRIDE
+    cap, halo = small.shape[1] // groups, plane.shape[2]
     struct = jax.ShapeDtypeStruct
     field = struct((DOFS, elements), F32)
-    send = struct((groups, TILE // 2, 128), F32)
-    slab = struct((TILE, 128), F32)
-
-    k0, send0, slab0, send_hot, codes, recv_id, first2, final2 = call(
+    send = struct((groups, fold_plan(2 * cap)[0], 128), F32)
+    edge = struct((TILE // 2, 128), F32)
+
+    k0, send0, edge0, send_hot, codes, recv_id, first2, final2 = call(
         functools.partial(start_kernel, (gx_size, groups)),
         (
             field,
             send,
-            slab,
+            edge,
             struct((traces, lanes + 128), BF16),
             struct((8, lanes), jnp.int32),
             struct((8, lanes + 128), jnp.int32),
@@ -603,22 +631,23 @@
             struct((2, DOFS, DOFS), BF16),
         ),
         (small, outq, inc, inq, coarse, band, plane, first, final, source, mid, tiles),
+        out_spaces="hhvhhhhh",
     )
 
     up = [(i, i + 1) for i in range(gx_size - 1)]
     down = [(j, i) for i, j in up]
-
-    def exchange(send, slab):
+    ring = [(i, (i + 1) % groups) for i in range(groups)]
+    back = [(j, i) for i, j in ring]
+
+    def exchange(send, edge):
         if gx_size == 2:
-            slab = lax.ppermute(slab, "gx", up + down)
+            upper = lower = lax.ppermute(edge, "gx", up + down)
         else:
-            halo = plane.shape[2]
-            lower = lax.ppermute(slab, "gx", up)
-            upper = lax.ppermute(slab, "gx", down)
-            slab = jnp.where(lane_row(128) < halo, upper, lower)
-        return lax.all_to_all(send, "yz", 0, 0, tiled=True), slab
-
-    recv0, slab0 = exchange(send0, slab0)
+            upper, lower = lax.ppermute(edge, "gx", down), lax.ppermute(edge, "gx", up)
+        before, after = lax.ppermute(edge, "yz", ring), lax.ppermute(edge, "yz", back)
+        return lax.all_to_all(send, "yz", 0, 0, tiled=True), upper, lower, after, before
+
+    came = exchange(send0, edge0)
     copy_sems = pltpu.SemaphoreType.DMA((2,))
     work = pltpu.VMEM((DOFS, elements), F32)
     held = (
@@ -631,15 +660,17 @@
     local, recv_hot, near_coupling, near_first = call(
         first_local_kernel, held, local_args(k0), "hhrhhhhr", "vvvv", scratch=[copy_sems]
     )
-    k1, send1, slab1 = call(
-        middle_kernel,
-        (field, send, slab),
-        (recv0, slab0, recv_hot, near_coupling, local, near_first)
+    k1, send1, edge1 = call(
+        functools.partial(middle_kernel, (cap, halo)),
+        (field, send, edge),
+        came
+        + (recv_hot, near_coupling, local, near_first)
         + (mid, final2, send_hot, codes, tiles),
-        "vvvvvvhhhhh",
+        "vvvvvvvvvhhhhh",
+        "hhv",
         scratch=[work],
     )
-    recv1, slab1 = exchange(send1, slab1)
+    came = exchange(send1, edge1)
     local, recv_hot, near_coupling, near_first, partial = call(
         second_local_kernel,
         held + (struct((1, 128), F32),),
@@ -649,11 +680,12 @@
         scratch=[copy_sems],
     )
     rows, k0, k1 = call(
-        last_kernel,
+        functools.partial(last_kernel, (cap, halo)),
         (struct((gx_size * groups, 1, 128), F32), field, field),
-        (recv1, slab1, recv_hot, near_coupling, local, near_first)
+        came
+        + (recv_hot, near_coupling, local, near_first)
         + (mid, final2, k0, k1, partial),
-        "vvvvvvhhrrv",
+        "vvvvvvvvvhhrrv",
         "vvv",
         scratch=[copy_sems, work],
     )

time: 56 us -> 53.8 us (0.961)
  waiting for transfers between devices: 13.2 us -> 2.68 us
  starting transfers between devices: 14.1 us -> 23 us
    all_to_all x2, waiting for transfers between devices: 13.2 us -> 0.69 us  [exchange(): lax.all_to_all(send, 'yz', 0, 0, tiled=True)]
    ppermute x2 -> x6, starting transfers between devices: 3.12 us -> 12 us  [the longest x2 8.29 us: exchange(): lax.ppermute(edge, 'yz', back)]
    ppermute x2 -> x6, waiting for transfers between devices: 0.01 us -> 1.99 us  [the longest x2 1.98 us: exchange(): lax.ppermute(edge, 'yz', ring)]
  transfers between devices with their start and end apart: 4 -> 8, of which waited for: 2 -> 4; matrix products, arithmetic and copies ran while one was open for 0% -> 0% of each run, Pallas kernels for 10% -> 11%
where the time goes in v5:
time: 53.8 us; the launch traced here: 53.4 us
  starting transfers between devices  23 us (43%)
  Pallas kernels  17.9 us (33%)
  blocking collectives  9.79 us (18%)
  waiting for transfers between devices  2.68 us (5%)
    pallas_call x6, Pallas kernels, call(): pl.pallas_call(functools.partial(kernel, plan), out_shape=tuple((space(c)...  17.9 us
    all_to_all x2, starting transfers between devices, exchange(): lax.all_to_all(send, 'yz', 0, 0, tiled=True)  11 us
    all_to_all x1, blocking collectives, on_device(): rows = lax.all_to_all(rows, ('gx', 'yz'), 0, 0, tiled=True)  9.79 us
    ppermute x2, starting transfers between devices, exchange(): lax.ppermute(edge, 'yz', back)  8.29 us
    ppermute x2, starting transfers between devices, exchange(): upper = lower = lax.ppermute(edge, 'gx', up + down)  2.99 us
    ppermute x2, waiting for transfers between devices, exchange(): lax.ppermute(edge, 'yz', ring)  1.98 us
  transfers between devices with their start and end apart: 8, of which 4 were waited for; matrix products, arithmetic and copies ran while one was open for 0% of the time, Pallas kernels for 11%

profile of v5, /device:TPU:0, one launch (start us, length us, event | category | flops | bytes accessed | tf_op | source)
XLA Modules:
  0.0 53.4 jit_solution(15508438549007462836)
XLA Ops:
  0.0 4.6 %shard_map.163 = (f32[320,128]{1,0:T(8,128)}, f32[16,32,128]{2,1,0:T(8,128)}, f32[40,128]{1,0:T(8,128)S(1)}, bf16[768,1152]{1,0:T(8,128)(2,1)}, s32[8,1024]{1,0:...) custom-call(s32[1,352]{1,0:T(1,128)} %refs_0_.1, s32[1,352]{1,0:T(1,128)} %refs_1_.3, ...), custom_call_target="tpu_custom_call" | custom-call | flops 1000000000 | bytes 1357888 | tf_op jit(solution)/shard_map/pallas_call | solution.py:576
  4.6 7.4 %all-to-all-start = ((f32[16,32,128]{2,1,0:T(8,128)}), f32[16,32,128]{2,1,0:T(8,128)S(1)}, u32[]{:S(2)}, u32[]{:S(2)}) async-start(f32[16,32,128]{2,1,0:T(8,128)} %get-tuple-element.28), calls=%async_computation | async-start | bytes 524288 | tf_op jit(solution)/shard_map/all_to_all | solution.py:648
  12.0 0.4 collective-permute-start.2
  12.4 4.1 %collective-permute-start.1 = (f32[40,128]{1,0:T(8,128)S(1)}, f32[40,128]{1,0:T(8,128)S(1)}, u32[]{:S(2)}, u32[]{:S(2)}) collective-permute-start(f32[40,128]{1,0:T(8,128)S(1)} %get-tuple-element.29), channel_id=1, source_target_pairs={{1,0},{2,1},{3,2},{4,3},{5,4},{6,5},{7,6},{8,7},{9,8},{10,9},{11,1... | collective-permute-start | bytes 61448 | tf_op jit(solution)/shard_map/ppermute | solution.py:647
  16.5 1.5 %collective-permute-start = (f32[40,128]{1,0:T(8,128)S(1)}, f32[40,128]{1,0:T(8,128)S(1)}, u32[]{:S(2)}, u32[]{:S(2)}) collective-permute-start(f32[40,128]{1,0:T(8,128)S(1)} %get-tuple-element.29), channel_id=1, source_target_pairs={{0,16},{16,0},{1,17},{17,1},{2,18},{18,2},{3,19},{19,3},{4,20},{20... | collective-permute-start | bytes 61448 | tf_op jit(solution)/shard_map/ppermute | solution.py:644
  18.0 2.9 %shard_map.164 = (f32[320,128]{1,0:T(8,128)S(1)}, bf16[1152,768]{1,0:T(8,128)(2,1)S(1)}, f32[480,128]{1,0:T(8,128)S(1)}, bf16[2,320,320]{2,1,0:T(8,128)(2,1)S(1)}) custom-call(f32[320,128]{1,0:T(8,128)} %get-tuple-element.30.refs_0_.refs_8_.refs_11_, f32[320,128]{1,0:T(8,128)} %refs_1_.5, f32[480,128]{1,0:T(8,128)} %refs_2_.5, f32[75,128]{1,0:T(8,128)} %refs_3_.5, ...), custom_call_target="tpu_custom_call" | custom-call | flops 1000000000 | bytes 1110528 | tf_op jit(solution)/shard_map/pallas_call | solution.py:576
  20.9 1.0 %collective-permute-done.2.refs_4_ = f32[40,128]{1,0:T(8,128)S(1)} collective-permute-done((f32[40,128]{1,0:T(8,128)S(1)}, f32[40,128]{1,0:T(8,128)S(1)}, u32[]{:S(2)}, u32[]{:S(2)}) %collective-permute-start.2) | collective-permute-done | bytes 20512 | tf_op jit(solution)/shard_map/ppermute | solution.py:647
  21.9 0.0 collective-permute-done.1.refs_3_
  21.9 0.0 collective-permute-done.refs_1_.refs_2_
  21.9 0.3 all-to-all-done.refs_0_
  22.2 4.6 %shard_map.165 = (f32[320,128]{1,0:T(8,128)}, f32[16,32,128]{2,1,0:T(8,128)}, f32[40,128]{1,0:T(8,128)S(1)}) custom-call(f32[16,32,128]{2,1,0:T(8,128)S(1)} %all-to-all-done.refs_0_, f32[40,128]{1,0:T(8,128)S(1)} %collective-permute-done.refs_1_.refs_2_, f32[40,128]{1,0:T(8,128)S(1)} %collective-permute-done.refs_1_.refs_2_, ...), custom_call_target="tpu_custom_call" | custom-call | flops 1000000000 | bytes 5513216 | tf_op jit(solution)/shard_map/pallas_call | solution.py:576
  26.9 3.5 %all-to-all-start.1 = ((f32[16,32,128]{2,1,0:T(8,128)}), f32[16,32,128]{2,1,0:T(8,128)S(1)}, u32[]{:S(2)}, u32[]{:S(2)}) async-start(f32[16,32,128]{2,1,0:T(8,128)} %get-tuple-element.40), calls=%async_computation.1 | async-start | bytes 524288 | tf_op jit(solution)/shard_map/all_to_all | solution.py:648
  30.4 0.3 collective-permute-start.5
  30.7 4.2 %collective-permute-start.4 = (f32[40,128]{1,0:T(8,128)S(1)}, f32[40,128]{1,0:T(8,128)S(1)}, u32[]{:S(2)}, u32[]{:S(2)}) collective-permute-start(f32[40,128]{1,0:T(8,128)S(1)} %get-tuple-element.41), channel_id=1, source_target_pairs={{1,0},{2,1},{3,2},{4,3},{5,4},{6,5},{7,6},{8,7},{9,8},{10,9},{11,1... | collective-permute-start | bytes 61448 | tf_op jit(solution)/shard_map/ppermute | solution.py:647
  34.9 1.5 %collective-permute-start.3 = (f32[40,128]{1,0:T(8,128)S(1)}, f32[40,128]{1,0:T(8,128)S(1)}, u32[]{:S(2)}, u32[]{:S(2)}) collective-permute-start(f32[40,128]{1,0:T(8,128)S(1)} %get-tuple-element.41), channel_id=1, source_target_pairs={{0,16},{16,0},{1,17},{17,1},{2,18},{18,2},{3,19},{19,3},{4,20},{20... | collective-permute-start | bytes 61448 | tf_op jit(solution)/shard_map/ppermute | solution.py:644
  36.4 2.9 %shard_map.166 = (f32[320,128]{1,0:T(8,128)S(1)}, bf16[1152,768]{1,0:T(8,128)(2,1)S(1)}, f32[480,128]{1,0:T(8,128)S(1)}, bf16[2,320,320]{2,1,0:T(8,128)(2,1)S(1)}, f32[1,128]{1,0:T(1,128)S(1)}) custom-call(f32[320,128]{1,0:T(8,128)} %get-tuple-element.42.refs_0_.refs_12_, f32[320,128]{1,0:T(8,128)} %refs_1_.5, f32[480,128]{1,0:T(8,128)} %refs_2_.5, ...), custom_call_target="tpu_custom_call" | custom-call | flops 1000000000 | bytes 1274368 | tf_op jit(solution)/shard_map/pallas_call | solution.py:576
  39.3 1.0 %collective-permute-done.5.refs_4_ = f32[40,128]{1,0:T(8,128)S(1)} collective-permute-done((f32[40,128]{1,0:T(8,128)S(1)}, f32[40,128]{1,0:T(8,128)S(1)}, u32[]{:S(2)}, u32[]{:S(2)}) %collective-permute-start.5) | collective-permute-done | bytes 20512 | tf_op jit(solution)/shard_map/ppermute | solution.py:647
  40.3 0.0 collective-permute-done.4.refs_3_
  40.3 0.0 collective-permute-done.3.refs_1_.refs_2_
  40.3 0.3 all-to-all-done.1.refs_0_
  40.6 2.1 %shard_map.167 = (f32[32,1,128]{2,1,0:T(1,128)S(1)}, f32[320,128]{1,0:T(8,128)S(1)}, f32[320,128]{1,0:T(8,128)S(1)}) custom-call(f32[16,32,128]{2,1,0:T(8,128)S(1)} %all-to-all-done.1.refs_0_, f32[40,128]{1,0:T(8,128)S(1)} %collective-permute-done.3.refs_1_.refs_2_, f32[40,128]{1,0:T(8,128)S(1)} %collective-permute-done.3.refs_1_.refs_2_, ...), custom_call_target="tpu_custom_call" | custom-call | flops 1000000000 | bytes 3834368 | tf_op jit(solution)/shard_map/pallas_call | solution.py:576
  42.7 9.8 %all_to_all.15.refs_0_ = f32[32,1,128]{2,1,0:T(1,128)S(1)} all-to-all(f32[32,1,128]{2,1,0:T(1,128)S(1)} %get-tuple-element.48), channel_id=1, replica_groups=mesh['gx'=2,'yz'=16] {'gx','yz'}, dimensions={0} | all-to-all | bytes 32768 | tf_op jit(solution)/shard_map/all_to_all | solution.py:692
  52.5 0.9 %shard_map.168 = f32[320,128]{1,0:T(8,128)} custom-call(f32[32,1,128]{2,1,0:T(1,128)S(1)} %all_to_all.15.refs_0_, f32[320,128]{1,0:T(8,128)S(1)} %get-tuple-element.49.refs_1_, f32[320,128]{1,0:T(8,128)S(1)} %get-tuple-element.50.refs_2_), custom_call_target="tpu_custom_call" | custom-call | flops 1000000000 | bytes 344064 | tf_op jit(solution)/shard_map/pallas_call | solution.py:576
Async XLA Ops:
  4.6 17.7 %all-to-all-start = ((f32[16,32,128]{2,1,0:T(8,128)}), f32[16,32,128]{2,1,0:T(8,128)S(1)}, u32[]{:S(2)}, u32[]{:S(2)}) async-start(f32[16,32,128]{2,1,0:T(8,128)} %get-tuple-element.28), calls=%async_computation | async-start | bytes 524288 | tf_op jit(solution)/shard_map/all_to_all | solution.py:648
  12.0 9.9 %collective-permute-start.2 = (f32[40,128]{1,0:T(8,128)S(1)}, f32[40,128]{1,0:T(8,128)S(1)}, u32[]{:S(2)}, u32[]{:S(2)}) collective-permute-start(f32[40,128]{1,0:T(8,128)S(1)} %get-tuple-element.29), channel_id=1, source_target_pairs={{0,1},{1,2},{2,3},{3,4},{4,5},{5,6},{6,7},{7,8},{8,9},{9,10},{10,1... | collective-permute-start | bytes 61448 | tf_op jit(solution)/shard_map/ppermute | solution.py:647
  12.4 9.5 %collective-permute-start.1 = (f32[40,128]{1,0:T(8,128)S(1)}, f32[40,128]{1,0:T(8,128)S(1)}, u32[]{:S(2)}, u32[]{:S(2)}) collective-permute-start(f32[40,128]{1,0:T(8,128)S(1)} %get-tuple-element.29), channel_id=1, source_target_pairs={{1,0},{2,1},{3,2},{4,3},{5,4},{6,5},{7,6},{8,7},{9,8},{10,9},{11,1... | collective-permute-start | bytes 61448 | tf_op jit(solution)/shard_map/ppermute | solution.py:647
  16.5 5.4 %collective-permute-start = (f32[40,128]{1,0:T(8,128)S(1)}, f32[40,128]{1,0:T(8,128)S(1)}, u32[]{:S(2)}, u32[]{:S(2)}) collective-permute-start(f32[40,128]{1,0:T(8,128)S(1)} %get-tuple-element.29), channel_id=1, source_target_pairs={{0,16},{16,0},{1,17},{17,1},{2,18},{18,2},{3,19},{19,3},{4,20},{20... | collective-permute-start | bytes 61448 | tf_op jit(solution)/shard_map/ppermute | solution.py:644
  26.9 13.7 %all-to-all-start.1 = ((f32[16,32,128]{2,1,0:T(8,128)}), f32[16,32,128]{2,1,0:T(8,128)S(1)}, u32[]{:S(2)}, u32[]{:S(2)}) async-start(f32[16,32,128]{2,1,0:T(8,128)} %get-tuple-element.40), calls=%async_computation.1 | async-start | bytes 524288 | tf_op jit(solution)/shard_map/all_to_all | solution.py:648
  30.4 9.8 %collective-permute-start.5 = (f32[40,128]{1,0:T(8,128)S(1)}, f32[40,128]{1,0:T(8,128)S(1)}, u32[]{:S(2)}, u32[]{:S(2)}) collective-permute-start(f32[40,128]{1,0:T(8,128)S(1)} %get-tuple-element.41), channel_id=1, source_target_pairs={{0,1},{1,2},{2,3},{3,4},{4,5},{5,6},{6,7},{7,8},{8,9},{9,10},{10,1... | collective-permute-start | bytes 61448 | tf_op jit(solution)/shard_map/ppermute | solution.py:647
  30.7 9.6 %collective-permute-start.4 = (f32[40,128]{1,0:T(8,128)S(1)}, f32[40,128]{1,0:T(8,128)S(1)}, u32[]{:S(2)}, u32[]{:S(2)}) collective-permute-start(f32[40,128]{1,0:T(8,128)S(1)} %get-tuple-element.41), channel_id=1, source_target_pairs={{1,0},{2,1},{3,2},{4,3},{5,4},{6,5},{7,6},{8,7},{9,8},{10,9},{11,1... | collective-permute-start | bytes 61448 | tf_op jit(solution)/shard_map/ppermute | solution.py:647
  34.9 5.4 %collective-permute-start.3 = (f32[40,128]{1,0:T(8,128)S(1)}, f32[40,128]{1,0:T(8,128)S(1)}, u32[]{:S(2)}, u32[]{:S(2)}) collective-permute-start(f32[40,128]{1,0:T(8,128)S(1)} %get-tuple-element.41), channel_id=1, source_target_pairs={{0,16},{16,0},{1,17},{17,1},{2,18},{18,2},{3,19},{19,3},{4,20},{20... | collective-permute-start | bytes 61448 | tf_op jit(solution)/shard_map/ppermute | solution.py:644

commit v6 on v5

--- a/solution.py
+++ b/solution.py
@@ -14,7 +14,7 @@
 TILE = VARS * NODES * NODES
 DOFS = TILE * NODES
 FACES = 6
-STRIDE = 64
+FOLD = 64
 K2_SCALE = 2.0**-20
 VMEM_LIMIT = 40 * 2**20
 F32 = jnp.float32
@@ -160,6 +160,10 @@
     return rows, plan
 
 
+def table_lanes(groups, cap, halo):
+    return -(-(groups * 2 * cap + 4 * halo) // 128) * 128
+
+
 def roll_lanes(x, shift):
     return pltpu.roll(x, shift % 128, 1) if shift % 128 else x
 
@@ -169,24 +173,36 @@
     return (lane >= start) & (lane < start + count)
 
 
+def window(x, start, width, to):
+    block, offset = start // 128, start % 128
+    value = roll_lanes(x[:, block * 128 : block * 128 + 128], to - offset)
+    if offset + width > 128:
+        after = roll_lanes(x[:, block * 128 + 128 : block * 128 + 256], to - offset)
+        value = jnp.where(lane_row(128) < to + 128 - offset, value, after)
+    return value
+
+
 def fold_halves(block):
     middle = TILE // 2
     return jnp.where(
-        lane_row(128) < STRIDE, block[:middle], roll_lanes(block[middle:], STRIDE)
+        lane_row(128) < FOLD, block[:middle], roll_lanes(block[middle:], FOLD)
     )
 
 
 def unfold_halves(block):
-    return jnp.concatenate([block, roll_lanes(block, STRIDE)], axis=0)
-
-
-def pack_send(field_ref, send_hot_ref, codes, tiles_ref, send_ref, halo_ref, cap):
+    return jnp.concatenate([block, roll_lanes(block, FOLD)], axis=0)
+
+
+def pack_send(field_ref, send_hot_ref, codes, tiles_ref, send_ref, edge_ref, sizes):
+    cap, halo = sizes
     groups = send_ref.shape[0]
-    lanes = groups * STRIDE
     gathered = mm(two_pieces(all_traces(field_ref)), send_hot_ref[...])
     high, low = gathered[:TILE], gathered[TILE:]
-    halo_ref[...] = fold_halves(high[:, lanes:] + low[:, lanes:])
-    high, low = high[:, :lanes].astype(BF16), low[:, :lanes].astype(BF16)
+    first_edge = groups * 2 * cap
+    from_block = first_edge // 128 * 128
+    edges = high[:, from_block:] + low[:, from_block:]
+    edge_ref[...] = fold_halves(window(edges, first_edge - from_block, 4 * halo, 0))
+    high, low = high.astype(BF16), low.astype(BF16)
     masks = [one_hot(codes == q) for q in range(8)]
     high_stack = jnp.concatenate([high * m for m in masks], axis=0)
     low_stack = jnp.concatenate([low * m for m in masks], axis=0)
@@ -194,38 +210,45 @@
     result = result[:TILE] + (result[TILE:] + mm(tiles_ref[:TILE], low_stack))
     rows, plan = fold_plan(2 * cap)
     for group in range(groups):
-        block = result[:, group // 2 * 128 : group // 2 * 128 + 128]
-        base = group % 2 * STRIDE
         folded = [None] * (rows // 8)
         for row, count, column, width, to_row, to_lane in plan:
+            part = window(
+                result[row : row + count], group * 2 * cap + column, width, to_lane
+            )
             for k in range(count // 8):
-                part = roll_lanes(block[row + 8 * k : row + 8 * k + 8], to_lane - base - column)
-                at = to_row // 8 + k
+                at, value = to_row // 8 + k, part[8 * k : 8 * k + 8]
                 if folded[at] is not None:
-                    part = jnp.where(in_lanes(to_lane, width), part, folded[at])
-                folded[at] = part
+                    value = jnp.where(in_lanes(to_lane, width), value, folded[at])
+                folded[at] = value
         send_ref[group] = jnp.concatenate(folded, axis=0)
 
 
-def unpack_received(recv_ref, cap):
-    rows, plan = fold_plan(2 * cap)
-    blocks = []
-    for pair in range(recv_ref.shape[0] // 2):
-        wide = [None] * (TILE // 8)
-        for side in range(2):
-            block = recv_ref[2 * pair + side]
-            base = side * STRIDE
-            for row, count, column, width, to_row, to_lane in plan:
-                for k in range(count // 8):
-                    part = roll_lanes(
-                        block[to_row + 8 * k : to_row + 8 * k + 8], base + column - to_lane
-                    )
-                    at = row // 8 + k
-                    if wide[at] is not None:
-                        part = jnp.where(in_lanes(base + column, width), part, wide[at])
-                    wide[at] = part
-        blocks.append(jnp.concatenate(wide, axis=0))
-    return jnp.concatenate(blocks, axis=1)
+def unpack_received(recv_ref, edge, sizes):
+    cap, halo = sizes
+    groups = recv_ref.shape[0]
+    plan = fold_plan(2 * cap)[1]
+    wide = [[None] * (TILE // 8) for _ in range(table_lanes(groups, cap, halo) // 128)]
+
+    def lay(value, row, count, start, width, from_lane):
+        offset = start % 128
+        value = roll_lanes(value, offset - from_lane)
+        for block, low, high in (
+            (start // 128, offset, min(128, offset + width)),
+            (start // 128 + 1, 0, offset + width - 128),
+        ):
+            for k in range(count // 8 if high > low else 0):
+                part, held = value[8 * k : 8 * k + 8], wide[block][row // 8 + k]
+                if held is not None:
+                    part = jnp.where(in_lanes(low, high - low), part, held)
+                wide[block][row // 8 + k] = part
+
+    for group in range(groups):
+        block = recv_ref[group]
+        for row, count, column, width, to_row, to_lane in plan:
+            start = group * 2 * cap + column
+            lay(block[to_row : to_row + count], row, count, start, width, to_lane)
+    lay(unfold_halves(edge), 0, TILE, groups * 2 * cap, 4 * halo, 0)
+    return jnp.concatenate([jnp.concatenate(w, axis=0) for w in wide], axis=1)
 
 
 def index_tables(cap, small, outq, inc, inq, coarse, band, plane, elements, sizes):
@@ -255,41 +278,37 @@
         ],
         axis=0,
     ).astype(BF16)
-    lane = lane_row(groups * STRIDE)
-    group, within = lane // STRIDE, lane % STRIDE
-    is_fine, is_used = within < cap, within < 2 * cap
+    lane = lane_row(table_lanes(groups, cap, halo))
+    group, within = lane // (2 * cap), lane % (2 * cap)
+    is_tile, is_fine = lane < groups * 2 * cap, within < cap
     slot = group * cap + jnp.where(is_fine, within, within - cap)
     slots = lax.broadcasted_iota(jnp.int32, (rows.shape[1], lane.shape[1]), 0)
-    placed = mm(rows, one_hot(slots == jnp.where(is_used, slot, -1))).astype(jnp.int32)
-    send_id = jnp.where(
+    placed = mm(rows, one_hot(slots == jnp.where(is_tile, slot, -1))).astype(jnp.int32)
+    edge_lane = lane - groups * 2 * cap
+    is_edge = (edge_lane >= 0) & (edge_lane < 4 * halo)
+    face = edge_lane // halo
+    slots = lax.broadcasted_iota(jnp.int32, (halo, lane.shape[1]), 0)
+    edge_rows = jnp.concatenate([as_f(plane), as_f(band), jnp.zeros((4, halo), F32)], axis=0)
+    edge = mm(
+        edge_rows.astype(BF16), one_hot(slots == jnp.where(is_edge, edge_lane % halo, -1))
+    ).astype(jnp.int32)
+    tile_id = jnp.where(
         is_fine, placed[0:1] * 8 + placed[1:2], placed[2:3] * 8 + placed[3:4]
     )
-    send_id = jnp.where(is_used, send_id, traces)
-    codes = jnp.where(is_fine, placed[4:5], 4 + placed[5:6])
+    send_id = jnp.where(is_tile, tile_id, traces)
+    codes = jnp.where(is_tile, jnp.where(is_fine, placed[4:5], 4 + placed[5:6]), 8)
     first_hang = traces + 4 * halo
     mortar = placed[6:7]
-    recv_id = jnp.where(
+    tile_recv = jnp.where(
         is_fine, jnp.where(mortar < hang, first_hang + mortar, -1), first_hang + hang + slot
     )
-    recv_id = jnp.where(is_used, recv_id, -1)
-
-    edge_lane = lane_row(128)
-    target = jnp.where(edge_lane < 4 * halo, edge_lane % halo, -1)
-    slots = lax.broadcasted_iota(jnp.int32, (halo, 128), 0)
-    halo_rows = jnp.concatenate([as_f(plane), as_f(band), jnp.zeros((4, halo), F32)], axis=0)
-    edge = mm(halo_rows.astype(BF16), one_hot(slots == target)).astype(jnp.int32)
-    halo_id = jnp.zeros_like(edge_lane) + traces
-    halo_recv = jnp.zeros_like(edge_lane) - 1
+    recv_id = jnp.where(is_tile, tile_recv, -1)
     present = (gx_index < gx_size - 1, gx_index > 0, True, True)
     starts = (traces + halo, traces, traces + 3 * halo, traces + 2 * halo)
-    for face in range(4):
-        here = edge_lane // halo == face
-        halo_id = jnp.where(here, face * elements + edge[face : face + 1], halo_id)
-        halo_recv = jnp.where(
-            here & present[face], starts[face] + edge_lane - face * halo, halo_recv
-        )
-    send_id = jnp.concatenate([send_id, halo_id], axis=1)
-    recv_id = jnp.concatenate([recv_id, halo_recv], axis=1)
+    for f in range(4):
+        here = is_edge & (face == f)
+        send_id = jnp.where(here, f * elements + edge[f : f + 1], send_id)
+        recv_id = jnp.where(here & present[f], starts[f] + edge_lane - f * halo, recv_id)
     return send_id, codes, recv_id
 
 
@@ -365,7 +384,8 @@
     r.ship(7)
     field[...] = solve_cells(r.get(9)[...], first2, final2, r.get(10))
     r.ship(0)
-    pack_send(field, send_hot, codes, r.get(11), send, edge, small.shape[1] // groups)
+    tile_sizes = (small.shape[1] // groups, plane.shape[2])
+    pack_send(field, send_hot, codes, r.get(11), send, edge, tile_sizes)
     r.ship(1)
     r.ship(2)
     r.finish()
@@ -463,13 +483,13 @@
 
 
 def finish_product(sizes, r, work_ref):
-    cap, halo = sizes
+    halo = sizes[1]
     upper, lower, after, before = [r.get(i)[...] for i in range(1, 5)]
-    face = lane_row(128) % STRIDE // halo
+    face = lane_row(128) % FOLD // halo
     edge = jnp.where(
         face < 2, jnp.where(face < 1, upper, lower), jnp.where(face < 3, after, before)
     )
-    received = jnp.concatenate([unpack_received(r.get(0), cap), unfold_halves(edge)], axis=1)
+    received = unpack_received(r.get(0), edge, sizes)
     near = mm(two_pieces(received), r.get(5)[...])
     near = near[:TILE] + near[TILE:]
     coupling, local = r.get(6), r.get(7)
@@ -493,7 +513,7 @@
     field, send, edge = r.outs
     field[...] = finish_product(sizes, r, r.work[0])
     r.ship(0)
-    pack_send(field, r.get(11), r.get(12)[0:1, :], r.get(13), send, edge, sizes[0])
+    pack_send(field, r.get(11), r.get(12)[0:1, :], r.get(13), send, edge, sizes)
     r.ship(1)
     r.ship(2)
     r.finish()
@@ -611,8 +631,8 @@
     gx_size, groups = lax.axis_size("gx"), lax.axis_size("yz")
     elements = source.shape[1]
     traces = FACES * elements
-    lanes = groups * STRIDE
     cap, halo = small.shape[1] // groups, plane.shape[2]
+    lanes = table_lanes(groups, cap, halo)
     struct = jax.ShapeDtypeStruct
     field = struct((DOFS, elements), F32)
     send = struct((groups, fold_plan(2 * cap)[0], 128), F32)
@@ -624,9 +644,9 @@
             field,
             send,
             edge,
-            struct((traces, lanes + 128), BF16),
+            struct((traces, lanes), BF16),
             struct((8, lanes), jnp.int32),
-            struct((8, lanes + 128), jnp.int32),
+            struct((8, lanes), jnp.int32),
             struct((2, DOFS, DOFS), BF16),
             struct((2, DOFS, DOFS), BF16),
         ),
@@ -652,7 +672,7 @@
     work = pltpu.VMEM((DOFS, elements), F32)
     held = (
         field,
-        struct((lanes + 128, traces), BF16),
+        struct((lanes, traces), BF16),
         struct(coupling.shape, F32),
         struct(first2.shape, BF16),
     )

time: 53.8 us -> 53 us (0.985)
  Pallas kernels: 17.9 us -> 16.6 us
    pallas_call x6, Pallas kernels: 17.9 us -> 16.6 us  [call(): pl.pallas_call(functools.partial(kernel, plan), out_shape=tuple((space(c)...]
  transfers between devices with their start and end apart: 8 -> 8, of which waited for: 4 -> 4; matrix products, arithmetic and copies ran while one was open for 0% -> 0% of each run, Pallas kernels for 11% -> 10%
where the time goes in v6:
time: 53 us; the launch traced here: 52.5 us
  starting transfers between devices  22.9 us (43%)
  Pallas kernels  16.6 us (31%)
  blocking collectives  9.78 us (18%)
  waiting for transfers between devices  3.12 us (6%)
    pallas_call x6, Pallas kernels, call(): pl.pallas_call(functools.partial(kernel, plan), out_shape=tuple((space(c)...  16.6 us
    all_to_all x2, starting transfers between devices, exchange(): lax.all_to_all(send, 'yz', 0, 0, tiled=True)  11 us
    all_to_all x1, blocking collectives, on_device(): rows = lax.all_to_all(rows, ('gx', 'yz'), 0, 0, tiled=True)  9.78 us
    ppermute x2, starting transfers between devices, exchange(): lax.ppermute(edge, 'yz', back)  8.29 us
    ppermute x2, starting transfers between devices, exchange(): upper = lower = lax.ppermute(edge, 'gx', up + down)  2.98 us
    ppermute x2, waiting for transfers between devices, exchange(): lax.ppermute(edge, 'yz', ring)  2.41 us
  transfers between devices with their start and end apart: 8, of which 4 were waited for; matrix products, arithmetic and copies ran while one was open for 0% of the time, Pallas kernels for 10%

profile of v6, /device:TPU:0, one launch (start us, length us, event | category | flops | bytes accessed | tf_op | source)
XLA Modules:
  0.0 52.5 jit_solution(17694699822118061856)
XLA Ops:
  0.0 4.2 %shard_map.163 = (f32[320,128]{1,0:T(8,128)}, f32[16,32,128]{2,1,0:T(8,128)}, f32[40,128]{1,0:T(8,128)S(1)}, bf16[768,768]{1,0:T(8,128)(2,1)}, s32[8,768]{1,0:T(...) custom-call(s32[1,352]{1,0:T(1,128)} %refs_0_.1, s32[1,352]{1,0:T(1,128)} %refs_1_.3, ...), custom_call_target="tpu_custom_call" | custom-call | flops 1000000000 | bytes 1357888 | tf_op jit(solution)/shard_map/pallas_call | solution.py:596
  4.2 7.4 %all-to-all-start = ((f32[16,32,128]{2,1,0:T(8,128)}), f32[16,32,128]{2,1,0:T(8,128)S(1)}, u32[]{:S(2)}, u32[]{:S(2)}) async-start(f32[16,32,128]{2,1,0:T(8,128)} %get-tuple-element.28), calls=%async_computation | async-start | bytes 524288 | tf_op jit(solution)/shard_map/all_to_all | solution.py:668
  11.7 0.4 collective-permute-start.2
  12.1 4.1 %collective-permute-start.1 = (f32[40,128]{1,0:T(8,128)S(1)}, f32[40,128]{1,0:T(8,128)S(1)}, u32[]{:S(2)}, u32[]{:S(2)}) collective-permute-start(f32[40,128]{1,0:T(8,128)S(1)} %get-tuple-element.29), channel_id=1, source_target_pairs={{1,0},{2,1},{3,2},{4,3},{5,4},{6,5},{7,6},{8,7},{9,8},{10,9},{11,1... | collective-permute-start | bytes 61448 | tf_op jit(solution)/shard_map/ppermute | solution.py:667
  16.2 1.5 %collective-permute-start = (f32[40,128]{1,0:T(8,128)S(1)}, f32[40,128]{1,0:T(8,128)S(1)}, u32[]{:S(2)}, u32[]{:S(2)}) collective-permute-start(f32[40,128]{1,0:T(8,128)S(1)} %get-tuple-element.29), channel_id=1, source_target_pairs={{0,16},{16,0},{1,17},{17,1},{2,18},{18,2},{3,19},{19,3},{4,20},{20... | collective-permute-start | bytes 61448 | tf_op jit(solution)/shard_map/ppermute | solution.py:664
  17.7 2.7 %shard_map.164 = (f32[320,128]{1,0:T(8,128)S(1)}, bf16[768,768]{1,0:T(8,128)(2,1)S(1)}, f32[480,128]{1,0:T(8,128)S(1)}, bf16[2,320,320]{2,1,0:T(8,128)(2,1)S(1)}) custom-call(f32[320,128]{1,0:T(8,128)} %get-tuple-element.30.refs_0_.refs_8_.refs_11_, f32[320,128]{1,0:T(8,128)} %refs_1_.5, f32[480,128]{1,0:T(8,128)} %refs_2_.5, f32[75,128]{1,0:T(8,128)} %refs_3_.5, ...), custom_call_target="tpu_custom_call" | custom-call | flops 1000000000 | bytes 1098240 | tf_op jit(solution)/shard_map/pallas_call | solution.py:596
  20.3 1.2 %collective-permute-done.2.refs_4_ = f32[40,128]{1,0:T(8,128)S(1)} collective-permute-done((f32[40,128]{1,0:T(8,128)S(1)}, f32[40,128]{1,0:T(8,128)S(1)}, u32[]{:S(2)}, u32[]{:S(2)}) %collective-permute-start.2) | collective-permute-done | bytes 20512 | tf_op jit(solution)/shard_map/ppermute | solution.py:667
  21.5 0.0 collective-permute-done.1.refs_3_
  21.6 0.0 collective-permute-done.refs_1_.refs_2_
  21.6 0.3 all-to-all-done.refs_0_
  21.9 4.2 %shard_map.165 = (f32[320,128]{1,0:T(8,128)}, f32[16,32,128]{2,1,0:T(8,128)}, f32[40,128]{1,0:T(8,128)S(1)}) custom-call(f32[16,32,128]{2,1,0:T(8,128)S(1)} %all-to-all-done.refs_0_, f32[40,128]{1,0:T(8,128)S(1)} %collective-permute-done.refs_1_.refs_2_, f32[40,128]{1,0:T(8,128)S(1)} %collective-permute-done.refs_1_.refs_2_, ...), custom_call_target="tpu_custom_call" | custom-call | flops 1000000000 | bytes 4325376 | tf_op jit(solution)/shard_map/pallas_call | solution.py:596
  26.1 3.5 %all-to-all-start.1 = ((f32[16,32,128]{2,1,0:T(8,128)}), f32[16,32,128]{2,1,0:T(8,128)S(1)}, u32[]{:S(2)}, u32[]{:S(2)}) async-start(f32[16,32,128]{2,1,0:T(8,128)} %get-tuple-element.40), calls=%async_computation.1 | async-start | bytes 524288 | tf_op jit(solution)/shard_map/all_to_all | solution.py:668
  29.7 0.3 collective-permute-start.5
  29.9 4.2 %collective-permute-start.4 = (f32[40,128]{1,0:T(8,128)S(1)}, f32[40,128]{1,0:T(8,128)S(1)}, u32[]{:S(2)}, u32[]{:S(2)}) collective-permute-start(f32[40,128]{1,0:T(8,128)S(1)} %get-tuple-element.41), channel_id=1, source_target_pairs={{1,0},{2,1},{3,2},{4,3},{5,4},{6,5},{7,6},{8,7},{9,8},{10,9},{11,1... | collective-permute-start | bytes 61448 | tf_op jit(solution)/shard_map/ppermute | solution.py:667
  34.2 1.5 %collective-permute-start.3 = (f32[40,128]{1,0:T(8,128)S(1)}, f32[40,128]{1,0:T(8,128)S(1)}, u32[]{:S(2)}, u32[]{:S(2)}) collective-permute-start(f32[40,128]{1,0:T(8,128)S(1)} %get-tuple-element.41), channel_id=1, source_target_pairs={{0,16},{16,0},{1,17},{17,1},{2,18},{18,2},{3,19},{19,3},{4,20},{20... | collective-permute-start | bytes 61448 | tf_op jit(solution)/shard_map/ppermute | solution.py:664
  35.6 2.7 %shard_map.166 = (f32[320,128]{1,0:T(8,128)S(1)}, bf16[768,768]{1,0:T(8,128)(2,1)S(1)}, f32[480,128]{1,0:T(8,128)S(1)}, bf16[2,320,320]{2,1,0:T(8,128)(2,1)S(1)}, f32[1,128]{1,0:T(1,128)S(1)}) custom-call(f32[320,128]{1,0:T(8,128)} %get-tuple-element.42.refs_0_.refs_12_, f32[320,128]{1,0:T(8,128)} %refs_1_.5, f32[480,128]{1,0:T(8,128)} %refs_2_.5, ...), custom_call_target="tpu_custom_call" | custom-call | flops 1000000000 | bytes 1262080 | tf_op jit(solution)/shard_map/pallas_call | solution.py:596
  38.3 1.2 %collective-permute-done.5.refs_4_ = f32[40,128]{1,0:T(8,128)S(1)} collective-permute-done((f32[40,128]{1,0:T(8,128)S(1)}, f32[40,128]{1,0:T(8,128)S(1)}, u32[]{:S(2)}, u32[]{:S(2)}) %collective-permute-start.5) | collective-permute-done | bytes 20512 | tf_op jit(solution)/shard_map/ppermute | solution.py:667
  39.5 0.0 collective-permute-done.4.refs_3_
  39.5 0.0 collective-permute-done.3.refs_1_.refs_2_
  39.5 0.3 all-to-all-done.1.refs_0_
  39.9 2.0 %shard_map.167 = (f32[32,1,128]{2,1,0:T(1,128)S(1)}, f32[320,128]{1,0:T(8,128)S(1)}, f32[320,128]{1,0:T(8,128)S(1)}) custom-call(f32[16,32,128]{2,1,0:T(8,128)S(1)} %all-to-all-done.1.refs_0_, f32[40,128]{1,0:T(8,128)S(1)} %collective-permute-done.3.refs_1_.refs_2_, f32[40,128]{1,0:T(8,128)S(1)} %collective-permute-done.3.refs_1_.refs_2_, ...), custom_call_target="tpu_custom_call" | custom-call | flops 1000000000 | bytes 3244544 | tf_op jit(solution)/shard_map/pallas_call | solution.py:596
  41.9 9.8 %all_to_all.15.refs_0_ = f32[32,1,128]{2,1,0:T(1,128)S(1)} all-to-all(f32[32,1,128]{2,1,0:T(1,128)S(1)} %get-tuple-element.48), channel_id=1, replica_groups=mesh['gx'=2,'yz'=16] {'gx','yz'}, dimensions={0} | all-to-all | bytes 32768 | tf_op jit(solution)/shard_map/all_to_all | solution.py:712
  51.6 0.9 %shard_map.168 = f32[320,128]{1,0:T(8,128)} custom-call(f32[32,1,128]{2,1,0:T(1,128)S(1)} %all_to_all.15.refs_0_, f32[320,128]{1,0:T(8,128)S(1)} %get-tuple-element.49.refs_1_, f32[320,128]{1,0:T(8,128)S(1)} %get-tuple-element.50.refs_2_), custom_call_target="tpu_custom_call" | custom-call | flops 1000000000 | bytes 344064 | tf_op jit(solution)/shard_map/pallas_call | solution.py:596
Async XLA Ops:
  4.2 17.7 %all-to-all-start = ((f32[16,32,128]{2,1,0:T(8,128)}), f32[16,32,128]{2,1,0:T(8,128)S(1)}, u32[]{:S(2)}, u32[]{:S(2)}) async-start(f32[16,32,128]{2,1,0:T(8,128)} %get-tuple-element.28), calls=%async_computation | async-start | bytes 524288 | tf_op jit(solution)/shard_map/all_to_all | solution.py:668
  11.7 9.9 %collective-permute-start.2 = (f32[40,128]{1,0:T(8,128)S(1)}, f32[40,128]{1,0:T(8,128)S(1)}, u32[]{:S(2)}, u32[]{:S(2)}) collective-permute-start(f32[40,128]{1,0:T(8,128)S(1)} %get-tuple-element.29), channel_id=1, source_target_pairs={{0,1},{1,2},{2,3},{3,4},{4,5},{5,6},{6,7},{7,8},{8,9},{9,10},{10,1... | collective-permute-start | bytes 61448 | tf_op jit(solution)/shard_map/ppermute | solution.py:667
  12.1 9.5 %collective-permute-start.1 = (f32[40,128]{1,0:T(8,128)S(1)}, f32[40,128]{1,0:T(8,128)S(1)}, u32[]{:S(2)}, u32[]{:S(2)}) collective-permute-start(f32[40,128]{1,0:T(8,128)S(1)} %get-tuple-element.29), channel_id=1, source_target_pairs={{1,0},{2,1},{3,2},{4,3},{5,4},{6,5},{7,6},{8,7},{9,8},{10,9},{11,1... | collective-permute-start | bytes 61448 | tf_op jit(solution)/shard_map/ppermute | solution.py:667
  16.2 5.4 %collective-permute-start = (f32[40,128]{1,0:T(8,128)S(1)}, f32[40,128]{1,0:T(8,128)S(1)}, u32[]{:S(2)}, u32[]{:S(2)}) collective-permute-start(f32[40,128]{1,0:T(8,128)S(1)} %get-tuple-element.29), channel_id=1, source_target_pairs={{0,16},{16,0},{1,17},{17,1},{2,18},{18,2},{3,19},{19,3},{4,20},{20... | collective-permute-start | bytes 61448 | tf_op jit(solution)/shard_map/ppermute | solution.py:664
  26.1 13.7 %all-to-all-start.1 = ((f32[16,32,128]{2,1,0:T(8,128)}), f32[16,32,128]{2,1,0:T(8,128)S(1)}, u32[]{:S(2)}, u32[]{:S(2)}) async-start(f32[16,32,128]{2,1,0:T(8,128)} %get-tuple-element.40), calls=%async_computation.1 | async-start | bytes 524288 | tf_op jit(solution)/shard_map/all_to_all | solution.py:668
  29.7 9.8 %collective-permute-start.5 = (f32[40,128]{1,0:T(8,128)S(1)}, f32[40,128]{1,0:T(8,128)S(1)}, u32[]{:S(2)}, u32[]{:S(2)}) collective-permute-start(f32[40,128]{1,0:T(8,128)S(1)} %get-tuple-element.41), channel_id=1, source_target_pairs={{0,1},{1,2},{2,3},{3,4},{4,5},{5,6},{6,7},{7,8},{8,9},{9,10},{10,1... | collective-permute-start | bytes 61448 | tf_op jit(solution)/shard_map/ppermute | solution.py:667
  29.9 9.6 %collective-permute-start.4 = (f32[40,128]{1,0:T(8,128)S(1)}, f32[40,128]{1,0:T(8,128)S(1)}, u32[]{:S(2)}, u32[]{:S(2)}) collective-permute-start(f32[40,128]{1,0:T(8,128)S(1)} %get-tuple-element.41), channel_id=1, source_target_pairs={{1,0},{2,1},{3,2},{4,3},{5,4},{6,5},{7,6},{8,7},{9,8},{10,9},{11,1... | collective-permute-start | bytes 61448 | tf_op jit(solution)/shard_map/ppermute | solution.py:667
  34.2 5.4 %collective-permute-start.3 = (f32[40,128]{1,0:T(8,128)S(1)}, f32[40,128]{1,0:T(8,128)S(1)}, u32[]{:S(2)}, u32[]{:S(2)}) collective-permute-start(f32[40,128]{1,0:T(8,128)S(1)} %get-tuple-element.41), channel_id=1, source_target_pairs={{0,16},{16,0},{1,17},{17,1},{2,18},{18,2},{3,19},{19,3},{4,20},{20... | collective-permute-start | bytes 61448 | tf_op jit(solution)/shard_map/ppermute | solution.py:664

commit v7 on v6

--- a/solution.py
+++ b/solution.py
@@ -15,6 +15,7 @@
 DOFS = TILE * NODES
 FACES = 6
 FOLD = 64
+CHUNK = 1
 K2_SCALE = 2.0**-20
 VMEM_LIMIT = 40 * 2**20
 F32 = jnp.float32
@@ -173,11 +174,11 @@
     return (lane >= start) & (lane < start + count)
 
 
-def window(x, start, width, to):
+def window(blocks, rows, start, width, to):
     block, offset = start // 128, start % 128
-    value = roll_lanes(x[:, block * 128 : block * 128 + 128], to - offset)
+    value = roll_lanes(blocks[block][rows], to - offset)
     if offset + width > 128:
-        after = roll_lanes(x[:, block * 128 + 128 : block * 128 + 256], to - offset)
+        after = roll_lanes(blocks[block + 1][rows], to - offset)
         value = jnp.where(lane_row(128) < to + 128 - offset, value, after)
     return value
 
@@ -193,34 +194,53 @@
     return jnp.concatenate([block, roll_lanes(block, FOLD)], axis=0)
 
 
-def pack_send(field_ref, send_hot_ref, codes, tiles_ref, send_ref, edge_ref, sizes):
+def pick_columns(table, ids):
+    lane = jnp.broadcast_to(ids % 128, (TILE, 128))
+    block = ids // 128
+    value = jnp.zeros((TILE, 128), F32)
+    for b, part in enumerate(table):
+        part = jnp.take_along_axis(part, lane, axis=1, mode="promise_in_bounds")
+        value = jnp.where(block == b, part, value)
+    return value
+
+
+def pack_send(field_ref, send_id, codes, tiles_ref, send_ref, edge_ref, sizes, ship):
     cap, halo = sizes
     groups = send_ref.shape[0]
-    gathered = mm(two_pieces(all_traces(field_ref)), send_hot_ref[...])
-    high, low = gathered[:TILE], gathered[TILE:]
-    first_edge = groups * 2 * cap
-    from_block = first_edge // 128 * 128
-    edges = high[:, from_block:] + low[:, from_block:]
-    edge_ref[...] = fold_halves(window(edges, first_edge - from_block, 4 * halo, 0))
-    high, low = high.astype(BF16), low.astype(BF16)
-    masks = [one_hot(codes == q) for q in range(8)]
-    high_stack = jnp.concatenate([high * m for m in masks], axis=0)
-    low_stack = jnp.concatenate([low * m for m in masks], axis=0)
-    result = mm(tiles_ref[...], high_stack)
-    result = result[:TILE] + (result[TILE:] + mm(tiles_ref[:TILE], low_stack))
+    traces = all_traces(field_ref)
+    table = [traces[:, b : b + 128] for b in range(0, traces.shape[1], 128)]
     rows, plan = fold_plan(2 * cap)
-    for group in range(groups):
-        folded = [None] * (rows // 8)
-        for row, count, column, width, to_row, to_lane in plan:
-            part = window(
-                result[row : row + count], group * 2 * cap + column, width, to_lane
-            )
-            for k in range(count // 8):
-                at, value = to_row // 8 + k, part[8 * k : 8 * k + 8]
-                if folded[at] is not None:
-                    value = jnp.where(in_lanes(to_lane, width), value, folded[at])
-                folded[at] = value
-        send_ref[group] = jnp.concatenate(folded, axis=0)
+    picked, done, sent = [], [], 0
+    count = send_id.shape[1] // 128
+    for part, start in enumerate(range(0, count, CHUNK)):
+        lanes = slice(start * 128, min(start + CHUNK, count) * 128)
+        for b in range(lanes.start, lanes.stop, 128):
+            picked.append(pick_columns(table, send_id[:, b : b + 128]))
+        high, low = split(jnp.concatenate(picked[start:], axis=1))
+        masks = [one_hot(codes[:, lanes] == q) for q in range(8)]
+        high_stack = jnp.concatenate([high * m for m in masks], axis=0)
+        low_stack = jnp.concatenate([low * m for m in masks], axis=0)
+        result = mm(tiles_ref[...], high_stack)
+        result = result[:TILE] + (result[TILE:] + mm(tiles_ref[:TILE], low_stack))
+        done += [result[:, b : b + 128] for b in range(0, result.shape[1], 128)]
+        ready = min(groups, lanes.stop // (2 * cap))
+        for group in range(sent, ready):
+            folded = [None] * (rows // 8)
+            for row, height, column, width, to_row, to_lane in plan:
+                piece = window(
+                    done, slice(row, row + height), group * 2 * cap + column, width, to_lane
+                )
+                for k in range(height // 8):
+                    at, value = to_row // 8 + k, piece[8 * k : 8 * k + 8]
+                    if folded[at] is not None:
+                        value = jnp.where(in_lanes(to_lane, width), value, folded[at])
+                    folded[at] = value
+            send_ref[group] = jnp.concatenate(folded, axis=0)
+        if ready > sent:
+            ship(part, sent, ready)
+        sent = ready
+    edges = window(picked, slice(None), groups * 2 * cap, 4 * halo, 0)
+    edge_ref[...] = fold_halves(edges)
 
 
 def unpack_received(recv_ref, edge, sizes):
@@ -251,54 +271,53 @@
     return jnp.concatenate([jnp.concatenate(w, axis=0) for w in wide], axis=1)
 
 
+def pick_lanes(rows, ids):
+    length = rows[0].shape[1]
+    table = jnp.concatenate(rows + [jnp.zeros((8 - len(rows), length), jnp.int32)], axis=0)
+    wide = -(-length // 128) * 128
+    if wide > length:
+        table = jnp.concatenate([table, jnp.zeros((8, wide - length), jnp.int32)], axis=1)
+    count = ids.shape[1]
+    full = -(-count // 128) * 128
+    if full > count:
+        ids = jnp.concatenate([ids, jnp.zeros((1, full - count), jnp.int32)], axis=1)
+    picked = []
+    for start in range(0, full, 128):
+        wanted = ids[:, start : start + 128]
+        lane = jnp.broadcast_to(wanted % 128, (8, 128))
+        value = jnp.zeros((8, 128), jnp.int32)
+        for b in range(wide // 128):
+            part = jnp.take_along_axis(
+                table[:, b * 128 : b * 128 + 128], lane, axis=1, mode="promise_in_bounds"
+            )
+            value = jnp.where(wanted // 128 == b, part, value)
+        picked.append(value)
+    return jnp.concatenate(picked, axis=1)[:, :count]
+
+
 def index_tables(cap, small, outq, inc, inq, coarse, band, plane, elements, sizes):
     gx_size, groups = sizes
     gx_index = lax.axis_index("gx")
     hang, halo = coarse.shape[1], band.shape[1]
     traces = FACES * elements
-    as_f = lambda x: x.astype(F32)
-    coarse_hot = one_hot(
-        lax.broadcasted_iota(jnp.int32, (hang, inc.shape[1]), 0) == inc
-    )
-    pad = jnp.zeros((6, hang), F32)
-    pick = mm(
-        jnp.concatenate([as_f(coarse // 8), as_f(coarse % 8), pad], axis=0).astype(BF16),
-        coarse_hot,
-    )
-    rows = jnp.concatenate(
-        [
-            as_f(small // 8),
-            as_f(small % 8),
-            jnp.where(inc < hang, pick[0:1], float(traces // 8)),
-            jnp.where(inc < hang, pick[1:2], 0.0),
-            as_f(outq),
-            as_f(inq),
-            as_f(inc),
-            jnp.zeros_like(pick[0:1]),
-        ],
-        axis=0,
-    ).astype(BF16)
     lane = lane_row(table_lanes(groups, cap, halo))
     group, within = lane // (2 * cap), lane % (2 * cap)
     is_tile, is_fine = lane < groups * 2 * cap, within < cap
     slot = group * cap + jnp.where(is_fine, within, within - cap)
-    slots = lax.broadcasted_iota(jnp.int32, (rows.shape[1], lane.shape[1]), 0)
-    placed = mm(rows, one_hot(slots == jnp.where(is_tile, slot, -1))).astype(jnp.int32)
     edge_lane = lane - groups * 2 * cap
     is_edge = (edge_lane >= 0) & (edge_lane < 4 * halo)
     face = edge_lane // halo
-    slots = lax.broadcasted_iota(jnp.int32, (halo, lane.shape[1]), 0)
-    edge_rows = jnp.concatenate([as_f(plane), as_f(band), jnp.zeros((4, halo), F32)], axis=0)
-    edge = mm(
-        edge_rows.astype(BF16), one_hot(slots == jnp.where(is_edge, edge_lane % halo, -1))
-    ).astype(jnp.int32)
-    tile_id = jnp.where(
-        is_fine, placed[0:1] * 8 + placed[1:2], placed[2:3] * 8 + placed[3:4]
-    )
+    owned = pick_lanes([coarse], jnp.minimum(inc, hang - 1))[0:1]
+    owned = jnp.where(inc < hang, owned, traces)
+    placed = pick_lanes([small, owned, outq, inq, inc], jnp.where(is_tile, slot, 0))
+    edge = pick_lanes(
+        [plane[0:1], plane[1:2], band[0:1], band[1:2]], jnp.where(is_edge, edge_lane % halo, 0)
+    )
+    tile_id = jnp.where(is_fine, placed[0:1], placed[1:2])
     send_id = jnp.where(is_tile, tile_id, traces)
-    codes = jnp.where(is_tile, jnp.where(is_fine, placed[4:5], 4 + placed[5:6]), 8)
+    codes = jnp.where(is_tile, jnp.where(is_fine, placed[2:3], 4 + placed[3:4]), 8)
     first_hang = traces + 4 * halo
-    mortar = placed[6:7]
+    mortar = placed[4:5]
     tile_recv = jnp.where(
         is_fine, jnp.where(mortar < hang, first_hang + mortar, -1), first_hang + hang + slot
     )
@@ -330,6 +349,7 @@
             None if v else pltpu.make_async_copy(b, o, out_sems.at[i])
             for i, (o, b, v) in enumerate(zip(outs, self.outs, out_vmem))
         ]
+        self.places = outs
         self.sent = []
 
     def start(self):
@@ -348,6 +368,17 @@
             self.ships[i].start()
             self.sent.append(self.ships[i])
 
+    def ship_rows(self, i, sems):
+        def ship(part, start, stop):
+            rows = pl.ds(start, stop - start)
+            copy = pltpu.make_async_copy(
+                self.outs[i].at[rows], self.places[i].at[rows], sems.at[part]
+            )
+            copy.start()
+            self.sent.append(copy)
+
+        return ship
+
     def finish(self):
         for copy in self.sent:
             copy.wait()
@@ -356,7 +387,8 @@
 def start_kernel(sizes, plan, *refs):
     r = Refs(plan, refs)
     r.start()
-    field, send, edge, send_hot, codes_ref, recv_id_ref, first2, final2 = r.outs
+    field, send, edge, ids = r.outs
+    first2, final2, part_sems = r.work
     elements = field.shape[1]
     groups = send.shape[0]
     small, outq, inc, inq, coarse, band, plane = [r.get(i) for i in range(7)]
@@ -372,22 +404,17 @@
         elements,
         sizes,
     )
-    codes_ref[...] = jnp.broadcast_to(codes, codes_ref.shape)
-    r.ship(4)
-    recv_id_ref[...] = jnp.broadcast_to(recv_id, recv_id_ref.shape)
-    r.ship(5)
-    fill_send_hot(send_id, send_hot)
+    ids[...] = jnp.concatenate(
+        [send_id, codes, recv_id, jnp.zeros((5, ids.shape[1]), jnp.int32)], axis=0
+    )
     r.ship(3)
     first2[0], first2[1] = split(r.get(7)[...])
-    r.ship(6)
     final2[0], final2[1] = split(r.get(8)[...])
-    r.ship(7)
     field[...] = solve_cells(r.get(9)[...], first2, final2, r.get(10))
     r.ship(0)
     tile_sizes = (small.shape[1] // groups, plane.shape[2])
-    pack_send(field, send_hot, codes, r.get(11), send, edge, tile_sizes)
-    r.ship(1)
-    r.ship(2)
+    ship = r.ship_rows(1, part_sems)
+    pack_send(field, send_id, codes, r.get(11), send, edge, tile_sizes, ship)
     r.finish()
 
 
@@ -437,32 +464,28 @@
 
 def fill_received_hot(ids, adjacent, hot_ref):
     elements = adjacent.shape[1]
-    column = jnp.transpose(ids)[:, 0:1]
+    column = jnp.transpose(ids)[:, 2:3]
     for f in range(FACES):
         hot_ref[:, f * elements : (f + 1) * elements] = one_hot(column == adjacent[f : f + 1, :])
 
 
-def prepare(r):
-    local, recv_hot, coupling, first2 = r.outs[:4]
-    copies = hold(r, (2, 3), (2, 7))
+def local_kernel(plan, *refs):
+    r = Refs(plan, refs)
+    local, recv_hot, coupling, mid, first2, final2, ids = r.outs[:7]
+    copies = hold(r, (2, 3), (8, 9))
     r.start()
-    fill_received_hot(r.get(6)[...], r.get(4), recv_hot)
-    for copy in copies:
-        copy.wait()
-    local_part(r.get(0), r.get(1), coupling, r.get(3), r.get(4), r.get(5), local)
-
-
-def first_local_kernel(plan, *refs):
-    prepare(Refs(plan, refs))
-
-
-def second_local_kernel(plan, *refs):
-    r = Refs(plan, refs)
-    prepare(r)
-    k0, k1 = r.get(8)[...], r.get(0)[...]
-    r.outs[4][...] = put(
-        [(0, total_of(k0 * k0)), (1, total_of(k0 * k1)), (2, total_of(k1 * k1))]
-    )
+    ids[...] = r.get(5)[...]
+    fill_received_hot(ids[...], r.get(3), recv_hot)
+    copies[0].wait()
+    local_part(r.get(0), r.get(1), coupling, r.get(2), r.get(3), r.get(4), local)
+    first2[0], first2[1] = split(r.get(6)[...])
+    final2[0], final2[1] = split(r.get(7)[...])
+    if len(r.outs) > 7:
+        k0, k1 = r.get(10)[...], r.get(0)[...]
+        r.outs[7][...] = put(
+            [(0, total_of(k0 * k0)), (1, total_of(k0 * k1)), (2, total_of(k1 * k1))]
+        )
+    copies[1].wait()
 
 
 def total_of(x):
@@ -475,11 +498,6 @@
     for position, value in values:
         row = jnp.where(lane == position, value, row)
     return row
-
-
-def fill_send_hot(send_id, hot_ref):
-    columns = lax.broadcasted_iota(jnp.int32, hot_ref.shape, 0)
-    hot_ref[...] = one_hot(columns == send_id)
 
 
 def finish_product(sizes, r, work_ref):
@@ -501,21 +519,20 @@
             f,
             -coupling[f * TILE : (f + 1) * TILE, :] * near[:, f * elements : (f + 1) * elements],
         )
-    first = r.get(8)
+    mid, first, final = r.get(8), r.get(9), r.get(10)
     inner = mm3(first[0], first[1], work_ref[...])
-    final = r.get(10)
-    return mm3(final[0], final[1], r.get(9)[...] * inner)
+    return mm3(final[0], final[1], mid[...] * inner)
 
 
 def middle_kernel(sizes, plan, *refs):
     r = Refs(plan, refs)
     r.start()
     field, send, edge = r.outs
-    field[...] = finish_product(sizes, r, r.work[0])
+    work, ids = r.work[0], r.get(11)
+    ship = r.ship_rows(1, r.work[1])
+    field[...] = finish_product(sizes, r, work)
     r.ship(0)
-    pack_send(field, r.get(11), r.get(12)[0:1, :], r.get(13), send, edge, sizes)
-    r.ship(1)
-    r.ship(2)
+    pack_send(field, ids[0:1, :], ids[1:2, :], r.get(12), send, edge, sizes, ship)
     r.finish()
 
 
@@ -638,20 +655,19 @@
     send = struct((groups, fold_plan(2 * cap)[0], 128), F32)
     edge = struct((TILE // 2, 128), F32)
 
-    k0, send0, edge0, send_hot, codes, recv_id, first2, final2 = call(
+    part_sems = pltpu.SemaphoreType.DMA((-(-lanes // (128 * CHUNK)),))
+    pieces2 = pltpu.VMEM((2, DOFS, DOFS), BF16)
+    k0, send0, edge0, ids = call(
         functools.partial(start_kernel, (gx_size, groups)),
         (
             field,
             send,
             edge,
-            struct((traces, lanes), BF16),
             struct((8, lanes), jnp.int32),
-            struct((8, lanes), jnp.int32),
-            struct((2, DOFS, DOFS), BF16),
-            struct((2, DOFS, DOFS), BF16),
         ),
         (small, outq, inc, inq, coarse, band, plane, first, final, source, mid, tiles),
-        out_spaces="hhvhhhhh",
+        out_spaces="hhvh",
+        scratch=[pieces2, pieces2, part_sems],
     )
 
     up = [(i, i + 1) for i in range(gx_size - 1)]
@@ -670,42 +686,37 @@
     came = exchange(send0, edge0)
     copy_sems = pltpu.SemaphoreType.DMA((2,))
     work = pltpu.VMEM((DOFS, elements), F32)
-    held = (
-        field,
-        struct((lanes, traces), BF16),
-        struct(coupling.shape, F32),
-        struct(first2.shape, BF16),
-    )
-    local_args = lambda u: (u, mass, coupling, flux, adjacent, volume, recv_id, first2)
-    local, recv_hot, near_coupling, near_first = call(
-        first_local_kernel, held, local_args(k0), "hhrhhhhr", "vvvv", scratch=[copy_sems]
-    )
+
+    def local_step(u, start=()):
+        factor = struct((2, DOFS, DOFS), BF16)
+        outs = (field, struct((lanes, traces), BF16), struct(coupling.shape, F32), field)
+        outs += (factor, factor, struct(ids.shape, jnp.int32))
+        outs += (struct((1, 128), F32),) * len(start)
+        return call(
+            local_kernel,
+            outs,
+            (u, mass, flux, adjacent, volume, ids, first, final, coupling, mid) + start,
+            "hhhhhhhhrr" + "h" * len(start),
+            "v" * len(outs),
+            scratch=[copy_sems],
+        )
+
+    local, recv_hot, near, *factors, near_ids = local_step(k0)
     k1, send1, edge1 = call(
         functools.partial(middle_kernel, (cap, halo)),
         (field, send, edge),
-        came
-        + (recv_hot, near_coupling, local, near_first)
-        + (mid, final2, send_hot, codes, tiles),
-        "vvvvvvvvvhhhhh",
+        came + (recv_hot, near, local, *factors, near_ids, tiles),
+        "v" * 12 + "h",
         "hhv",
-        scratch=[work],
+        scratch=[work, part_sems],
     )
     came = exchange(send1, edge1)
-    local, recv_hot, near_coupling, near_first, partial = call(
-        second_local_kernel,
-        held + (struct((1, 128), F32),),
-        local_args(k1) + (k0,),
-        "hhrhhhhrh",
-        "vvvvv",
-        scratch=[copy_sems],
-    )
+    local, recv_hot, near, *factors, near_ids, partial = local_step(k1, (k0,))
     rows, k0, k1 = call(
         functools.partial(last_kernel, (cap, halo)),
         (struct((gx_size * groups, 1, 128), F32), field, field),
-        came
-        + (recv_hot, near_coupling, local, near_first)
-        + (mid, final2, k0, k1, partial),
-        "vvvvvvvvvhhrrv",
+        came + (recv_hot, near, local, *factors, k0, k1, partial),
+        "v" * 11 + "rrv",
         "vvv",
         scratch=[copy_sems, work],
     )

time: 53 us -> 51.9 us (0.979)
  waiting for transfers between devices: 3.12 us -> 2.32 us
    ppermute x2, waiting for transfers between devices: 2.41 us -> 1.61 us  [exchange(): lax.ppermute(edge, 'yz', ring)]
  transfers between devices with their start and end apart: 8 -> 8, of which waited for: 4 -> 4; matrix products, arithmetic and copies ran while one was open for 0% -> 0% of each run, Pallas kernels for 10% -> 12%
where the time goes in v7:
time: 51.9 us; the launch traced here: 51.5 us
  starting transfers between devices  22.9 us (44%)
  Pallas kernels  16.4 us (32%)
  blocking collectives  9.78 us (19%)
  waiting for transfers between devices  2.32 us (4%)
    pallas_call x6, Pallas kernels, call(): pl.pallas_call(functools.partial(kernel, plan), out_shape=tuple((space(c)...  16.4 us
    all_to_all x2, starting transfers between devices, exchange(): lax.all_to_all(send, 'yz', 0, 0, tiled=True)  11 us
    all_to_all x1, blocking collectives, on_device(): rows = lax.all_to_all(rows, ('gx', 'yz'), 0, 0, tiled=True)  9.78 us
    ppermute x2, starting transfers between devices, exchange(): lax.ppermute(edge, 'yz', back)  8.29 us
    ppermute x2, starting transfers between devices, exchange(): upper = lower = lax.ppermute(edge, 'gx', up + down)  2.98 us
    ppermute x2, waiting for transfers between devices, exchange(): lax.ppermute(edge, 'yz', ring)  1.61 us
  transfers between devices with their start and end apart: 8, of which 4 were waited for; matrix products, arithmetic and copies ran while one was open for 0% of the time, Pallas kernels for 12%

profile of v7, /device:TPU:0, one launch (start us, length us, event | category | flops | bytes accessed | tf_op | source)
XLA Modules:
  0.0 51.5 jit_solution(12803330786094379379)
XLA Ops:
  0.0 3.8 %shard_map.163 = (f32[320,128]{1,0:T(8,128)}, f32[16,32,128]{2,1,0:T(8,128)}, f32[40,128]{1,0:T(8,128)S(1)}, s32[8,768]{1,0:T(8,128)}) custom-call(s32[1,352]{1,0:T(1,128)} %refs_0_.1, s32[1,352]{1,0:T(1,128)} %refs_1_.3, s32[1,352]{1,0:T(1,128)} %refs_2_.3, s32[1,352]{1,0:T(1,128)} %refs_3_.3, s32[1,80]{1,0:T(1,128)} %refs_4_.3, s32[1,2,16]{2,1,0:T(2,128)} %refs_5_.1, ...), custom_call_target="tpu_custom_call" | custom-call | flops 1000000000 | bytes 1357888 | tf_op jit(solution)/shard_map/pallas_call | solution.py:613
  3.9 7.4 %all-to-all-start = ((f32[16,32,128]{2,1,0:T(8,128)}), f32[16,32,128]{2,1,0:T(8,128)S(1)}, u32[]{:S(2)}, u32[]{:S(2)}) async-start(f32[16,32,128]{2,1,0:T(8,128)} %get-tuple-element.29), calls=%async_computation | async-start | bytes 524288 | tf_op jit(solution)/shard_map/all_to_all | solution.py:684
  11.3 0.4 collective-permute-start.2
  11.7 4.1 %collective-permute-start.1 = (f32[40,128]{1,0:T(8,128)S(1)}, f32[40,128]{1,0:T(8,128)S(1)}, u32[]{:S(2)}, u32[]{:S(2)}) collective-permute-start(f32[40,128]{1,0:T(8,128)S(1)} %get-tuple-element.30), channel_id=1, source_target_pairs={{1,0},{2,1},{3,2},{4,3},{5,4},{6,5},{7,6},{8,7},{9,8},{10,9},{11,1... | collective-permute-start | bytes 61448 | tf_op jit(solution)/shard_map/ppermute | solution.py:683
  15.8 1.5 %collective-permute-start = (f32[40,128]{1,0:T(8,128)S(1)}, f32[40,128]{1,0:T(8,128)S(1)}, u32[]{:S(2)}, u32[]{:S(2)}) collective-permute-start(f32[40,128]{1,0:T(8,128)S(1)} %get-tuple-element.30), channel_id=1, source_target_pairs={{0,16},{16,0},{1,17},{17,1},{2,18},{18,2},{3,19},{19,3},{4,20},{20... | collective-permute-start | bytes 61448 | tf_op jit(solution)/shard_map/ppermute | solution.py:680
  17.3 2.7 %shard_map.164 = (f32[320,128]{1,0:T(8,128)S(1)}, bf16[768,768]{1,0:T(8,128)(2,1)S(1)}, f32[480,128]{1,0:T(8,128)S(1)}, f32[320,128]{1,0:T(8,128)S(1)}, bf16[2,3...) custom-call(f32[320,128]{1,0:T(8,128)} %get-tuple-element.31.refs_0_.refs_10_.refs_11_, ...), custom_call_target="tpu_custom_call" | custom-call | flops 1000000000 | bytes 1671680 | tf_op jit(solution)/shard_map/pallas_call | solution.py:613
  20.0 1.2 %collective-permute-done.2.refs_4_ = f32[40,128]{1,0:T(8,128)S(1)} collective-permute-done((f32[40,128]{1,0:T(8,128)S(1)}, f32[40,128]{1,0:T(8,128)S(1)}, u32[]{:S(2)}, u32[]{:S(2)}) %collective-permute-start.2) | collective-permute-done | bytes 20512 | tf_op jit(solution)/shard_map/ppermute | solution.py:683
  21.2 0.0 collective-permute-done.1.refs_3_
  21.2 0.0 collective-permute-done.refs_1_.refs_2_
  21.2 0.3 all-to-all-done.refs_0_
  21.5 3.9 %shard_map.165 = (f32[320,128]{1,0:T(8,128)}, f32[16,32,128]{2,1,0:T(8,128)}, f32[40,128]{1,0:T(8,128)S(1)}) custom-call(f32[16,32,128]{2,1,0:T(8,128)S(1)} %all-to-all-done.refs_0_, f32[40,128]{1,0:T(8,128)S(1)} %collective-permute-done.refs_1_.refs_2_, f32[40,128]{1,0:T(8,128)S(1)} %collective-permute-done.refs_1_.refs_2_, ...), custom_call_target="tpu_custom_call" | custom-call | flops 1000000000 | bytes 3145728 | tf_op jit(solution)/shard_map/pallas_call | solution.py:613
  25.4 3.5 %all-to-all-start.1 = ((f32[16,32,128]{2,1,0:T(8,128)}), f32[16,32,128]{2,1,0:T(8,128)S(1)}, u32[]{:S(2)}, u32[]{:S(2)}) async-start(f32[16,32,128]{2,1,0:T(8,128)} %get-tuple-element.40), calls=%async_computation.1 | async-start | bytes 524288 | tf_op jit(solution)/shard_map/all_to_all | solution.py:684
  28.9 0.3 collective-permute-start.5
  29.2 4.2 %collective-permute-start.4 = (f32[40,128]{1,0:T(8,128)S(1)}, f32[40,128]{1,0:T(8,128)S(1)}, u32[]{:S(2)}, u32[]{:S(2)}) collective-permute-start(f32[40,128]{1,0:T(8,128)S(1)} %get-tuple-element.41), channel_id=1, source_target_pairs={{1,0},{2,1},{3,2},{4,3},{5,4},{6,5},{7,6},{8,7},{9,8},{10,9},{11,1... | collective-permute-start | bytes 61448 | tf_op jit(solution)/shard_map/ppermute | solution.py:683
  33.4 1.5 %collective-permute-start.3 = (f32[40,128]{1,0:T(8,128)S(1)}, f32[40,128]{1,0:T(8,128)S(1)}, u32[]{:S(2)}, u32[]{:S(2)}) collective-permute-start(f32[40,128]{1,0:T(8,128)S(1)} %get-tuple-element.41), channel_id=1, source_target_pairs={{0,16},{16,0},{1,17},{17,1},{2,18},{18,2},{3,19},{19,3},{4,20},{20... | collective-permute-start | bytes 61448 | tf_op jit(solution)/shard_map/ppermute | solution.py:680
  34.9 3.4 %shard_map.166 = (f32[320,128]{1,0:T(8,128)S(1)}, bf16[768,768]{1,0:T(8,128)(2,1)S(1)}, f32[480,128]{1,0:T(8,128)S(1)}, f32[320,128]{1,0:T(8,128)S(1)}, bf16[2,3...) custom-call(f32[320,128]{1,0:T(8,128)} %get-tuple-element.42.refs_0_.refs_, ...), custom_call_target="tpu_custom_call" | custom-call | flops 1000000000 | bytes 1835520 | tf_op jit(solution)/shard_map/pallas_call | solution.py:613
  38.3 0.5 collective-permute-done.5.refs_4_
  38.8 0.0 collective-permute-done.4.refs_3_
  38.8 0.0 collective-permute-done.3.refs_1_.refs_2_
  38.8 0.3 all-to-all-done.1.refs_0_
  39.1 1.6 %shard_map.167 = (f32[32,1,128]{2,1,0:T(1,128)S(1)}, f32[320,128]{1,0:T(8,128)S(1)}, f32[320,128]{1,0:T(8,128)S(1)}) custom-call(f32[16,32,128]{2,1,0:T(8,128)S(1)} %all-to-all-done.1.refs_0_, f32[40,128]{1,0:T(8,128)S(1)} %collective-permute-done.3.refs_1_.refs_2_, f32[40,128]{1,0:T(8,128)S(1)} %collective-permute-done.3.refs_1_.refs_2_, ...), custom_call_target="tpu_custom_call" | custom-call | flops 1000000000 | bytes 3244544 | tf_op jit(solution)/shard_map/pallas_call | solution.py:613
  40.8 9.8 %all_to_all.15.refs_0_ = f32[32,1,128]{2,1,0:T(1,128)S(1)} all-to-all(f32[32,1,128]{2,1,0:T(1,128)S(1)} %get-tuple-element.50), channel_id=1, replica_groups=mesh['gx'=2,'yz'=16] {'gx','yz'}, dimensions={0} | all-to-all | bytes 32768 | tf_op jit(solution)/shard_map/all_to_all | solution.py:723
  50.6 0.9 %shard_map.168 = f32[320,128]{1,0:T(8,128)} custom-call(f32[32,1,128]{2,1,0:T(1,128)S(1)} %all_to_all.15.refs_0_, f32[320,128]{1,0:T(8,128)S(1)} %get-tuple-element.51.refs_1_, f32[320,128]{1,0:T(8,128)S(1)} %get-tuple-element.52.refs_2_), custom_call_target="tpu_custom_call" | custom-call | flops 1000000000 | bytes 344064 | tf_op jit(solution)/shard_map/pallas_call | solution.py:613
Async XLA Ops:
  3.9 17.7 %all-to-all-start = ((f32[16,32,128]{2,1,0:T(8,128)}), f32[16,32,128]{2,1,0:T(8,128)S(1)}, u32[]{:S(2)}, u32[]{:S(2)}) async-start(f32[16,32,128]{2,1,0:T(8,128)} %get-tuple-element.29), calls=%async_computation | async-start | bytes 524288 | tf_op jit(solution)/shard_map/all_to_all | solution.py:684
  11.3 9.9 %collective-permute-start.2 = (f32[40,128]{1,0:T(8,128)S(1)}, f32[40,128]{1,0:T(8,128)S(1)}, u32[]{:S(2)}, u32[]{:S(2)}) collective-permute-start(f32[40,128]{1,0:T(8,128)S(1)} %get-tuple-element.30), channel_id=1, source_target_pairs={{0,1},{1,2},{2,3},{3,4},{4,5},{5,6},{6,7},{7,8},{8,9},{9,10},{10,1... | collective-permute-start | bytes 61448 | tf_op jit(solution)/shard_map/ppermute | solution.py:683
  11.7 9.5 %collective-permute-start.1 = (f32[40,128]{1,0:T(8,128)S(1)}, f32[40,128]{1,0:T(8,128)S(1)}, u32[]{:S(2)}, u32[]{:S(2)}) collective-permute-start(f32[40,128]{1,0:T(8,128)S(1)} %get-tuple-element.30), channel_id=1, source_target_pairs={{1,0},{2,1},{3,2},{4,3},{5,4},{6,5},{7,6},{8,7},{9,8},{10,9},{11,1... | collective-permute-start | bytes 61448 | tf_op jit(solution)/shard_map/ppermute | solution.py:683
  15.8 5.4 %collective-permute-start = (f32[40,128]{1,0:T(8,128)S(1)}, f32[40,128]{1,0:T(8,128)S(1)}, u32[]{:S(2)}, u32[]{:S(2)}) collective-permute-start(f32[40,128]{1,0:T(8,128)S(1)} %get-tuple-element.30), channel_id=1, source_target_pairs={{0,16},{16,0},{1,17},{17,1},{2,18},{18,2},{3,19},{19,3},{4,20},{20... | collective-permute-start | bytes 61448 | tf_op jit(solution)/shard_map/ppermute | solution.py:680
  25.4 13.7 %all-to-all-start.1 = ((f32[16,32,128]{2,1,0:T(8,128)}), f32[16,32,128]{2,1,0:T(8,128)S(1)}, u32[]{:S(2)}, u32[]{:S(2)}) async-start(f32[16,32,128]{2,1,0:T(8,128)} %get-tuple-element.40), calls=%async_computation.1 | async-start | bytes 524288 | tf_op jit(solution)/shard_map/all_to_all | solution.py:684
  28.9 9.8 %collective-permute-start.5 = (f32[40,128]{1,0:T(8,128)S(1)}, f32[40,128]{1,0:T(8,128)S(1)}, u32[]{:S(2)}, u32[]{:S(2)}) collective-permute-start(f32[40,128]{1,0:T(8,128)S(1)} %get-tuple-element.41), channel_id=1, source_target_pairs={{0,1},{1,2},{2,3},{3,4},{4,5},{5,6},{6,7},{7,8},{8,9},{9,10},{10,1... | collective-permute-start | bytes 61448 | tf_op jit(solution)/shard_map/ppermute | solution.py:683
  29.2 9.6 %collective-permute-start.4 = (f32[40,128]{1,0:T(8,128)S(1)}, f32[40,128]{1,0:T(8,128)S(1)}, u32[]{:S(2)}, u32[]{:S(2)}) collective-permute-start(f32[40,128]{1,0:T(8,128)S(1)} %get-tuple-element.41), channel_id=1, source_target_pairs={{1,0},{2,1},{3,2},{4,3},{5,4},{6,5},{7,6},{8,7},{9,8},{10,9},{11,1... | collective-permute-start | bytes 61448 | tf_op jit(solution)/shard_map/ppermute | solution.py:683
  33.4 5.4 %collective-permute-start.3 = (f32[40,128]{1,0:T(8,128)S(1)}, f32[40,128]{1,0:T(8,128)S(1)}, u32[]{:S(2)}, u32[]{:S(2)}) collective-permute-start(f32[40,128]{1,0:T(8,128)S(1)} %get-tuple-element.41), channel_id=1, source_target_pairs={{0,16},{16,0},{1,17},{17,1},{2,18},{18,2},{3,19},{19,3},{4,20},{20... | collective-permute-start | bytes 61448 | tf_op jit(solution)/shard_map/ppermute | solution.py:680

commit v8 on v7

--- a/solution.py
+++ b/solution.py
@@ -96,11 +96,6 @@
     return first[:, :columns] + (first[:, columns:] + mm(a_low, b_high))
 
 
-def solve_cells(x, first_ref, final_ref, mid_ref):
-    inner = mm3(first_ref[0], first_ref[1], x)
-    return mm3(final_ref[0], final_ref[1], mid_ref[...] * inner)
-
-
 def face_rows(ref, face):
     end = NODES - 1 if face % 2 else 0
     if face // 2 == 0:
@@ -176,11 +171,10 @@
 
 def window(blocks, rows, start, width, to):
     block, offset = start // 128, start % 128
-    value = roll_lanes(blocks[block][rows], to - offset)
+    value = blocks[block][rows]
     if offset + width > 128:
-        after = roll_lanes(blocks[block + 1][rows], to - offset)
-        value = jnp.where(lane_row(128) < to + 128 - offset, value, after)
-    return value
+        value = jnp.where(lane_row(128) >= offset, value, blocks[block + 1][rows])
+    return roll_lanes(value, to - offset)
 
 
 def fold_halves(block):
@@ -220,8 +214,9 @@
         masks = [one_hot(codes[:, lanes] == q) for q in range(8)]
         high_stack = jnp.concatenate([high * m for m in masks], axis=0)
         low_stack = jnp.concatenate([low * m for m in masks], axis=0)
-        result = mm(tiles_ref[...], high_stack)
-        result = result[:TILE] + (result[TILE:] + mm(tiles_ref[:TILE], low_stack))
+        width = high.shape[1]
+        result = mm(tiles_ref[:TILE], jnp.concatenate([high_stack, low_stack], axis=1))
+        result = result[:, :width] + (result[:, width:] + mm(tiles_ref[TILE:], high_stack))
         done += [result[:, b : b + 128] for b in range(0, result.shape[1], 128)]
         ready = min(groups, lanes.stop // (2 * cap))
         for group in range(sent, ready):
@@ -408,9 +403,11 @@
         [send_id, codes, recv_id, jnp.zeros((5, ids.shape[1]), jnp.int32)], axis=0
     )
     r.ship(3)
-    first2[0], first2[1] = split(r.get(7)[...])
-    final2[0], final2[1] = split(r.get(8)[...])
-    field[...] = solve_cells(r.get(9)[...], first2, final2, r.get(10))
+    first, final, source, mid = [r.get(i) for i in range(7, 11)]
+    first2[0], first2[1] = split(first[...])
+    inner = mm3(first2[0], first2[1], source[...])
+    final2[0], final2[1] = split(final[...])
+    field[...] = mm3(final2[0], final2[1], mid[...] * inner)
     r.ship(0)
     tile_sizes = (small.shape[1] // groups, plane.shape[2])
     ship = r.ship_rows(1, part_sems)

time: 51.9 us -> 51.7 us (level)
  no operation moved by 1% of the time
where the time goes in v8:
time: 51.7 us; the launch traced here: 51.3 us
  starting transfers between devices  22.9 us (44%)
  Pallas kernels  16.2 us (31%)
  blocking collectives  9.78 us (19%)
  waiting for transfers between devices  2.32 us (4%)
    pallas_call x6, Pallas kernels, call(): pl.pallas_call(functools.partial(kernel, plan), out_shape=tuple((space(c)...  16.2 us
    all_to_all x2, starting transfers between devices, exchange(): lax.all_to_all(send, 'yz', 0, 0, tiled=True)  11 us
    all_to_all x1, blocking collectives, on_device(): rows = lax.all_to_all(rows, ('gx', 'yz'), 0, 0, tiled=True)  9.78 us
    ppermute x2, starting transfers between devices, exchange(): lax.ppermute(edge, 'yz', back)  8.29 us
    ppermute x2, starting transfers between devices, exchange(): upper = lower = lax.ppermute(edge, 'gx', up + down)  2.98 us
    ppermute x2, waiting for transfers between devices, exchange(): lax.ppermute(edge, 'yz', ring)  1.61 us
  transfers between devices with their start and end apart: 8, of which 4 were waited for; matrix products, arithmetic and copies ran while one was open for 0% of the time, Pallas kernels for 12%

profile of v8, /device:TPU:0, one launch (start us, length us, event | category | flops | bytes accessed | tf_op | source)
XLA Modules:
  0.0 51.3 jit_solution(14180141285654055232)
XLA Ops:
  0.0 3.8 %shard_map.163 = (f32[320,128]{1,0:T(8,128)}, f32[16,32,128]{2,1,0:T(8,128)}, f32[40,128]{1,0:T(8,128)S(1)}, s32[8,768]{1,0:T(8,128)}) custom-call(s32[1,352]{1,0:T(1,128)} %refs_0_.1, s32[1,352]{1,0:T(1,128)} %refs_1_.3, s32[1,352]{1,0:T(1,128)} %refs_2_.3, s32[1,352]{1,0:T(1,128)} %refs_3_.3, s32[1,80]{1,0:T(1,128)} %refs_4_.3, s32[1,2,16]{2,1,0:T(2,128)} %refs_5_.1, ...), custom_call_target="tpu_custom_call" | custom-call | flops 1000000000 | bytes 1357888 | tf_op jit(solution)/shard_map/pallas_call | solution.py:610
  3.8 7.4 %all-to-all-start = ((f32[16,32,128]{2,1,0:T(8,128)}), f32[16,32,128]{2,1,0:T(8,128)S(1)}, u32[]{:S(2)}, u32[]{:S(2)}) async-start(f32[16,32,128]{2,1,0:T(8,128)} %get-tuple-element.29), calls=%async_computation | async-start | bytes 524288 | tf_op jit(solution)/shard_map/all_to_all | solution.py:681
  11.2 0.4 collective-permute-start.2
  11.6 4.1 %collective-permute-start.1 = (f32[40,128]{1,0:T(8,128)S(1)}, f32[40,128]{1,0:T(8,128)S(1)}, u32[]{:S(2)}, u32[]{:S(2)}) collective-permute-start(f32[40,128]{1,0:T(8,128)S(1)} %get-tuple-element.30), channel_id=1, source_target_pairs={{1,0},{2,1},{3,2},{4,3},{5,4},{6,5},{7,6},{8,7},{9,8},{10,9},{11,1... | collective-permute-start | bytes 61448 | tf_op jit(solution)/shard_map/ppermute | solution.py:680
  15.7 1.5 %collective-permute-start = (f32[40,128]{1,0:T(8,128)S(1)}, f32[40,128]{1,0:T(8,128)S(1)}, u32[]{:S(2)}, u32[]{:S(2)}) collective-permute-start(f32[40,128]{1,0:T(8,128)S(1)} %get-tuple-element.30), channel_id=1, source_target_pairs={{0,16},{16,0},{1,17},{17,1},{2,18},{18,2},{3,19},{19,3},{4,20},{20... | collective-permute-start | bytes 61448 | tf_op jit(solution)/shard_map/ppermute | solution.py:677
  17.2 2.7 %shard_map.164 = (f32[320,128]{1,0:T(8,128)S(1)}, bf16[768,768]{1,0:T(8,128)(2,1)S(1)}, f32[480,128]{1,0:T(8,128)S(1)}, f32[320,128]{1,0:T(8,128)S(1)}, bf16[2,3...) custom-call(f32[320,128]{1,0:T(8,128)} %get-tuple-element.31.refs_0_.refs_10_.refs_11_, ...), custom_call_target="tpu_custom_call" | custom-call | flops 1000000000 | bytes 1671680 | tf_op jit(solution)/shard_map/pallas_call | solution.py:610
  19.9 1.1 %collective-permute-done.2.refs_4_ = f32[40,128]{1,0:T(8,128)S(1)} collective-permute-done((f32[40,128]{1,0:T(8,128)S(1)}, f32[40,128]{1,0:T(8,128)S(1)}, u32[]{:S(2)}, u32[]{:S(2)}) %collective-permute-start.2) | collective-permute-done | bytes 20512 | tf_op jit(solution)/shard_map/ppermute | solution.py:680
  21.1 0.0 collective-permute-done.1.refs_3_
  21.1 0.0 collective-permute-done.refs_1_.refs_2_
  21.1 0.3 all-to-all-done.refs_0_
  21.4 3.8 %shard_map.165 = (f32[320,128]{1,0:T(8,128)}, f32[16,32,128]{2,1,0:T(8,128)}, f32[40,128]{1,0:T(8,128)S(1)}) custom-call(f32[16,32,128]{2,1,0:T(8,128)S(1)} %all-to-all-done.refs_0_, f32[40,128]{1,0:T(8,128)S(1)} %collective-permute-done.refs_1_.refs_2_, f32[40,128]{1,0:T(8,128)S(1)} %collective-permute-done.refs_1_.refs_2_, ...), custom_call_target="tpu_custom_call" | custom-call | flops 1000000000 | bytes 3145728 | tf_op jit(solution)/shard_map/pallas_call | solution.py:610
  25.2 3.5 %all-to-all-start.1 = ((f32[16,32,128]{2,1,0:T(8,128)}), f32[16,32,128]{2,1,0:T(8,128)S(1)}, u32[]{:S(2)}, u32[]{:S(2)}) async-start(f32[16,32,128]{2,1,0:T(8,128)} %get-tuple-element.40), calls=%async_computation.1 | async-start | bytes 524288 | tf_op jit(solution)/shard_map/all_to_all | solution.py:681
  28.8 0.3 collective-permute-start.5
  29.0 4.2 %collective-permute-start.4 = (f32[40,128]{1,0:T(8,128)S(1)}, f32[40,128]{1,0:T(8,128)S(1)}, u32[]{:S(2)}, u32[]{:S(2)}) collective-permute-start(f32[40,128]{1,0:T(8,128)S(1)} %get-tuple-element.41), channel_id=1, source_target_pairs={{1,0},{2,1},{3,2},{4,3},{5,4},{6,5},{7,6},{8,7},{9,8},{10,9},{11,1... | collective-permute-start | bytes 61448 | tf_op jit(solution)/shard_map/ppermute | solution.py:680
  33.3 1.5 %collective-permute-start.3 = (f32[40,128]{1,0:T(8,128)S(1)}, f32[40,128]{1,0:T(8,128)S(1)}, u32[]{:S(2)}, u32[]{:S(2)}) collective-permute-start(f32[40,128]{1,0:T(8,128)S(1)} %get-tuple-element.41), channel_id=1, source_target_pairs={{0,16},{16,0},{1,17},{17,1},{2,18},{18,2},{3,19},{19,3},{4,20},{20... | collective-permute-start | bytes 61448 | tf_op jit(solution)/shard_map/ppermute | solution.py:677
  34.7 3.4 %shard_map.166 = (f32[320,128]{1,0:T(8,128)S(1)}, bf16[768,768]{1,0:T(8,128)(2,1)S(1)}, f32[480,128]{1,0:T(8,128)S(1)}, f32[320,128]{1,0:T(8,128)S(1)}, bf16[2,3...) custom-call(f32[320,128]{1,0:T(8,128)} %get-tuple-element.42.refs_0_.refs_, ...), custom_call_target="tpu_custom_call" | custom-call | flops 1000000000 | bytes 1835520 | tf_op jit(solution)/shard_map/pallas_call | solution.py:610
  38.1 0.5 collective-permute-done.5.refs_4_
  38.6 0.0 collective-permute-done.4.refs_3_
  38.6 0.0 collective-permute-done.3.refs_1_.refs_2_
  38.6 0.3 all-to-all-done.1.refs_0_
  39.0 1.6 %shard_map.167 = (f32[32,1,128]{2,1,0:T(1,128)S(1)}, f32[320,128]{1,0:T(8,128)S(1)}, f32[320,128]{1,0:T(8,128)S(1)}) custom-call(f32[16,32,128]{2,1,0:T(8,128)S(1)} %all-to-all-done.1.refs_0_, f32[40,128]{1,0:T(8,128)S(1)} %collective-permute-done.3.refs_1_.refs_2_, f32[40,128]{1,0:T(8,128)S(1)} %collective-permute-done.3.refs_1_.refs_2_, ...), custom_call_target="tpu_custom_call" | custom-call | flops 1000000000 | bytes 3244544 | tf_op jit(solution)/shard_map/pallas_call | solution.py:610
  40.6 9.8 %all_to_all.15.refs_0_ = f32[32,1,128]{2,1,0:T(1,128)S(1)} all-to-all(f32[32,1,128]{2,1,0:T(1,128)S(1)} %get-tuple-element.50), channel_id=1, replica_groups=mesh['gx'=2,'yz'=16] {'gx','yz'}, dimensions={0} | all-to-all | bytes 32768 | tf_op jit(solution)/shard_map/all_to_all | solution.py:720
  50.4 0.9 %shard_map.168 = f32[320,128]{1,0:T(8,128)} custom-call(f32[32,1,128]{2,1,0:T(1,128)S(1)} %all_to_all.15.refs_0_, f32[320,128]{1,0:T(8,128)S(1)} %get-tuple-element.51.refs_1_, f32[320,128]{1,0:T(8,128)S(1)} %get-tuple-element.52.refs_2_), custom_call_target="tpu_custom_call" | custom-call | flops 1000000000 | bytes 344064 | tf_op jit(solution)/shard_map/pallas_call | solution.py:610
Async XLA Ops:
  3.8 17.7 %all-to-all-start = ((f32[16,32,128]{2,1,0:T(8,128)}), f32[16,32,128]{2,1,0:T(8,128)S(1)}, u32[]{:S(2)}, u32[]{:S(2)}) async-start(f32[16,32,128]{2,1,0:T(8,128)} %get-tuple-element.29), calls=%async_computation | async-start | bytes 524288 | tf_op jit(solution)/shard_map/all_to_all | solution.py:681
  11.2 9.9 %collective-permute-start.2 = (f32[40,128]{1,0:T(8,128)S(1)}, f32[40,128]{1,0:T(8,128)S(1)}, u32[]{:S(2)}, u32[]{:S(2)}) collective-permute-start(f32[40,128]{1,0:T(8,128)S(1)} %get-tuple-element.30), channel_id=1, source_target_pairs={{0,1},{1,2},{2,3},{3,4},{4,5},{5,6},{6,7},{7,8},{8,9},{9,10},{10,1... | collective-permute-start | bytes 61448 | tf_op jit(solution)/shard_map/ppermute | solution.py:680
  11.6 9.5 %collective-permute-start.1 = (f32[40,128]{1,0:T(8,128)S(1)}, f32[40,128]{1,0:T(8,128)S(1)}, u32[]{:S(2)}, u32[]{:S(2)}) collective-permute-start(f32[40,128]{1,0:T(8,128)S(1)} %get-tuple-element.30), channel_id=1, source_target_pairs={{1,0},{2,1},{3,2},{4,3},{5,4},{6,5},{7,6},{8,7},{9,8},{10,9},{11,1... | collective-permute-start | bytes 61448 | tf_op jit(solution)/shard_map/ppermute | solution.py:680
  15.7 5.4 %collective-permute-start = (f32[40,128]{1,0:T(8,128)S(1)}, f32[40,128]{1,0:T(8,128)S(1)}, u32[]{:S(2)}, u32[]{:S(2)}) collective-permute-start(f32[40,128]{1,0:T(8,128)S(1)} %get-tuple-element.30), channel_id=1, source_target_pairs={{0,16},{16,0},{1,17},{17,1},{2,18},{18,2},{3,19},{19,3},{4,20},{20... | collective-permute-start | bytes 61448 | tf_op jit(solution)/shard_map/ppermute | solution.py:677
  25.2 13.7 %all-to-all-start.1 = ((f32[16,32,128]{2,1,0:T(8,128)}), f32[16,32,128]{2,1,0:T(8,128)S(1)}, u32[]{:S(2)}, u32[]{:S(2)}) async-start(f32[16,32,128]{2,1,0:T(8,128)} %get-tuple-element.40), calls=%async_computation.1 | async-start | bytes 524288 | tf_op jit(solution)/shard_map/all_to_all | solution.py:681
  28.8 9.8 %collective-permute-start.5 = (f32[40,128]{1,0:T(8,128)S(1)}, f32[40,128]{1,0:T(8,128)S(1)}, u32[]{:S(2)}, u32[]{:S(2)}) collective-permute-start(f32[40,128]{1,0:T(8,128)S(1)} %get-tuple-element.41), channel_id=1, source_target_pairs={{0,1},{1,2},{2,3},{3,4},{4,5},{5,6},{6,7},{7,8},{8,9},{9,10},{10,1... | collective-permute-start | bytes 61448 | tf_op jit(solution)/shard_map/ppermute | solution.py:680
  29.0 9.6 %collective-permute-start.4 = (f32[40,128]{1,0:T(8,128)S(1)}, f32[40,128]{1,0:T(8,128)S(1)}, u32[]{:S(2)}, u32[]{:S(2)}) collective-permute-start(f32[40,128]{1,0:T(8,128)S(1)} %get-tuple-element.41), channel_id=1, source_target_pairs={{1,0},{2,1},{3,2},{4,3},{5,4},{6,5},{7,6},{8,7},{9,8},{10,9},{11,1... | collective-permute-start | bytes 61448 | tf_op jit(solution)/shard_map/ppermute | solution.py:680
  33.3 5.4 %collective-permute-start.3 = (f32[40,128]{1,0:T(8,128)S(1)}, f32[40,128]{1,0:T(8,128)S(1)}, u32[]{:S(2)}, u32[]{:S(2)}) collective-permute-start(f32[40,128]{1,0:T(8,128)S(1)} %get-tuple-element.41), channel_id=1, source_target_pairs={{0,16},{16,0},{1,17},{17,1},{2,18},{18,2},{3,19},{19,3},{4,20},{20... | collective-permute-start | bytes 61448 | tf_op jit(solution)/shard_map/ppermute | solution.py:677

commit v9 on v8

--- a/solution.py
+++ b/solution.py
@@ -403,9 +403,10 @@
         [send_id, codes, recv_id, jnp.zeros((5, ids.shape[1]), jnp.int32)], axis=0
     )
     r.ship(3)
-    first, final, source, mid = [r.get(i) for i in range(7, 11)]
+    first, source = r.get(7), r.get(8)
     first2[0], first2[1] = split(first[...])
     inner = mm3(first2[0], first2[1], source[...])
+    final, mid = r.get(9), r.get(10)
     final2[0], final2[1] = split(final[...])
     field[...] = mm3(final2[0], final2[1], mid[...] * inner)
     r.ship(0)
@@ -662,7 +663,7 @@
             edge,
             struct((8, lanes), jnp.int32),
         ),
-        (small, outq, inc, inq, coarse, band, plane, first, final, source, mid, tiles),
+        (small, outq, inc, inq, coarse, band, plane, first, source, final, mid, tiles),
         out_spaces="hhvh",
         scratch=[pieces2, pieces2, part_sems],
     )

time: 51.7 us -> 51.6 us (level)
  no operation moved by 1% of the time
where the time goes in v9:
time: 51.6 us; the launch traced here: 51.1 us
  starting transfers between devices  22.9 us (44%)
  Pallas kernels  16 us (31%)
  blocking collectives  9.78 us (19%)
  waiting for transfers between devices  2.32 us (4%)
    pallas_call x6, Pallas kernels, call(): pl.pallas_call(functools.partial(kernel, plan), out_shape=tuple((space(c)...  16 us
    all_to_all x2, starting transfers between devices, exchange(): lax.all_to_all(send, 'yz', 0, 0, tiled=True)  11 us
    all_to_all x1, blocking collectives, on_device(): rows = lax.all_to_all(rows, ('gx', 'yz'), 0, 0, tiled=True)  9.78 us
    ppermute x2, starting transfers between devices, exchange(): lax.ppermute(edge, 'yz', back)  8.29 us
    ppermute x2, starting transfers between devices, exchange(): upper = lower = lax.ppermute(edge, 'gx', up + down)  2.98 us
    ppermute x2, waiting for transfers between devices, exchange(): lax.ppermute(edge, 'yz', ring)  1.61 us
  transfers between devices with their start and end apart: 8, of which 4 were waited for; matrix products, arithmetic and copies ran while one was open for 0% of the time, Pallas kernels for 12%

profile of v9, /device:TPU:0, one launch (start us, length us, event | category | flops | bytes accessed | tf_op | source)
XLA Modules:
  0.0 51.1 jit_solution(13904363503594990840)
XLA Ops:
  0.0 3.6 %shard_map.163 = (f32[320,128]{1,0:T(8,128)}, f32[16,32,128]{2,1,0:T(8,128)}, f32[40,128]{1,0:T(8,128)S(1)}, s32[8,768]{1,0:T(8,128)}) custom-call(s32[1,352]{1,0:T(1,128)} %refs_0_.1, s32[1,352]{1,0:T(1,128)} %refs_1_.3, s32[1,352]{1,0:T(1,128)} %refs_2_.3, s32[1,352]{1,0:T(1,128)} %refs_3_.3, s32[1,80]{1,0:T(1,128)} %refs_4_.3, s32[1,2,16]{2,1,0:T(2,128)} %refs_5_.1, ...), custom_call_target="tpu_custom_call" | custom-call | flops 1000000000 | bytes 1357888 | tf_op jit(solution)/shard_map/pallas_call | solution.py:611
  3.6 7.4 %all-to-all-start = ((f32[16,32,128]{2,1,0:T(8,128)}), f32[16,32,128]{2,1,0:T(8,128)S(1)}, u32[]{:S(2)}, u32[]{:S(2)}) async-start(f32[16,32,128]{2,1,0:T(8,128)} %get-tuple-element.29), calls=%async_computation | async-start | bytes 524288 | tf_op jit(solution)/shard_map/all_to_all | solution.py:682
  11.1 0.4 collective-permute-start.2
  11.5 4.1 %collective-permute-start.1 = (f32[40,128]{1,0:T(8,128)S(1)}, f32[40,128]{1,0:T(8,128)S(1)}, u32[]{:S(2)}, u32[]{:S(2)}) collective-permute-start(f32[40,128]{1,0:T(8,128)S(1)} %get-tuple-element.30), channel_id=1, source_target_pairs={{1,0},{2,1},{3,2},{4,3},{5,4},{6,5},{7,6},{8,7},{9,8},{10,9},{11,1... | collective-permute-start | bytes 61448 | tf_op jit(solution)/shard_map/ppermute | solution.py:681
  15.6 1.5 %collective-permute-start = (f32[40,128]{1,0:T(8,128)S(1)}, f32[40,128]{1,0:T(8,128)S(1)}, u32[]{:S(2)}, u32[]{:S(2)}) collective-permute-start(f32[40,128]{1,0:T(8,128)S(1)} %get-tuple-element.30), channel_id=1, source_target_pairs={{0,16},{16,0},{1,17},{17,1},{2,18},{18,2},{3,19},{19,3},{4,20},{20... | collective-permute-start | bytes 61448 | tf_op jit(solution)/shard_map/ppermute | solution.py:678
  17.0 2.7 %shard_map.164 = (f32[320,128]{1,0:T(8,128)S(1)}, bf16[768,768]{1,0:T(8,128)(2,1)S(1)}, f32[480,128]{1,0:T(8,128)S(1)}, f32[320,128]{1,0:T(8,128)S(1)}, bf16[2,3...) custom-call(f32[320,128]{1,0:T(8,128)} %get-tuple-element.31.refs_0_.refs_10_.refs_11_, ...), custom_call_target="tpu_custom_call" | custom-call | flops 1000000000 | bytes 1671680 | tf_op jit(solution)/shard_map/pallas_call | solution.py:611
  19.8 1.2 %collective-permute-done.2.refs_4_ = f32[40,128]{1,0:T(8,128)S(1)} collective-permute-done((f32[40,128]{1,0:T(8,128)S(1)}, f32[40,128]{1,0:T(8,128)S(1)}, u32[]{:S(2)}, u32[]{:S(2)}) %collective-permute-start.2) | collective-permute-done | bytes 20512 | tf_op jit(solution)/shard_map/ppermute | solution.py:681
  20.9 0.0 collective-permute-done.1.refs_3_
  20.9 0.0 collective-permute-done.refs_1_.refs_2_
  20.9 0.3 all-to-all-done.refs_0_
  21.3 3.8 %shard_map.165 = (f32[320,128]{1,0:T(8,128)}, f32[16,32,128]{2,1,0:T(8,128)}, f32[40,128]{1,0:T(8,128)S(1)}) custom-call(f32[16,32,128]{2,1,0:T(8,128)S(1)} %all-to-all-done.refs_0_, f32[40,128]{1,0:T(8,128)S(1)} %collective-permute-done.refs_1_.refs_2_, f32[40,128]{1,0:T(8,128)S(1)} %collective-permute-done.refs_1_.refs_2_, ...), custom_call_target="tpu_custom_call" | custom-call | flops 1000000000 | bytes 3145728 | tf_op jit(solution)/shard_map/pallas_call | solution.py:611
  25.1 3.5 %all-to-all-start.1 = ((f32[16,32,128]{2,1,0:T(8,128)}), f32[16,32,128]{2,1,0:T(8,128)S(1)}, u32[]{:S(2)}, u32[]{:S(2)}) async-start(f32[16,32,128]{2,1,0:T(8,128)} %get-tuple-element.40), calls=%async_computation.1 | async-start | bytes 524288 | tf_op jit(solution)/shard_map/all_to_all | solution.py:682
  28.6 0.3 collective-permute-start.5
  28.9 4.2 %collective-permute-start.4 = (f32[40,128]{1,0:T(8,128)S(1)}, f32[40,128]{1,0:T(8,128)S(1)}, u32[]{:S(2)}, u32[]{:S(2)}) collective-permute-start(f32[40,128]{1,0:T(8,128)S(1)} %get-tuple-element.41), channel_id=1, source_target_pairs={{1,0},{2,1},{3,2},{4,3},{5,4},{6,5},{7,6},{8,7},{9,8},{10,9},{11,1... | collective-permute-start | bytes 61448 | tf_op jit(solution)/shard_map/ppermute | solution.py:681
  33.1 1.5 %collective-permute-start.3 = (f32[40,128]{1,0:T(8,128)S(1)}, f32[40,128]{1,0:T(8,128)S(1)}, u32[]{:S(2)}, u32[]{:S(2)}) collective-permute-start(f32[40,128]{1,0:T(8,128)S(1)} %get-tuple-element.41), channel_id=1, source_target_pairs={{0,16},{16,0},{1,17},{17,1},{2,18},{18,2},{3,19},{19,3},{4,20},{20... | collective-permute-start | bytes 61448 | tf_op jit(solution)/shard_map/ppermute | solution.py:678
  34.6 3.4 %shard_map.166 = (f32[320,128]{1,0:T(8,128)S(1)}, bf16[768,768]{1,0:T(8,128)(2,1)S(1)}, f32[480,128]{1,0:T(8,128)S(1)}, f32[320,128]{1,0:T(8,128)S(1)}, bf16[2,3...) custom-call(f32[320,128]{1,0:T(8,128)} %get-tuple-element.42.refs_0_.refs_, ...), custom_call_target="tpu_custom_call" | custom-call | flops 1000000000 | bytes 1835520 | tf_op jit(solution)/shard_map/pallas_call | solution.py:611
  38.0 0.5 collective-permute-done.5.refs_4_
  38.5 0.0 collective-permute-done.4.refs_3_
  38.5 0.0 collective-permute-done.3.refs_1_.refs_2_
  38.5 0.3 all-to-all-done.1.refs_0_
  38.8 1.6 %shard_map.167 = (f32[32,1,128]{2,1,0:T(1,128)S(1)}, f32[320,128]{1,0:T(8,128)S(1)}, f32[320,128]{1,0:T(8,128)S(1)}) custom-call(f32[16,32,128]{2,1,0:T(8,128)S(1)} %all-to-all-done.1.refs_0_, f32[40,128]{1,0:T(8,128)S(1)} %collective-permute-done.3.refs_1_.refs_2_, f32[40,128]{1,0:T(8,128)S(1)} %collective-permute-done.3.refs_1_.refs_2_, ...), custom_call_target="tpu_custom_call" | custom-call | flops 1000000000 | bytes 3244544 | tf_op jit(solution)/shard_map/pallas_call | solution.py:611
  40.5 9.8 %all_to_all.15.refs_0_ = f32[32,1,128]{2,1,0:T(1,128)S(1)} all-to-all(f32[32,1,128]{2,1,0:T(1,128)S(1)} %get-tuple-element.50), channel_id=1, replica_groups=mesh['gx'=2,'yz'=16] {'gx','yz'}, dimensions={0} | all-to-all | bytes 32768 | tf_op jit(solution)/shard_map/all_to_all | solution.py:721
  50.2 0.9 %shard_map.168 = f32[320,128]{1,0:T(8,128)} custom-call(f32[32,1,128]{2,1,0:T(1,128)S(1)} %all_to_all.15.refs_0_, f32[320,128]{1,0:T(8,128)S(1)} %get-tuple-element.51.refs_1_, f32[320,128]{1,0:T(8,128)S(1)} %get-tuple-element.52.refs_2_), custom_call_target="tpu_custom_call" | custom-call | flops 1000000000 | bytes 344064 | tf_op jit(solution)/shard_map/pallas_call | solution.py:611
Async XLA Ops:
  3.6 17.7 %all-to-all-start = ((f32[16,32,128]{2,1,0:T(8,128)}), f32[16,32,128]{2,1,0:T(8,128)S(1)}, u32[]{:S(2)}, u32[]{:S(2)}) async-start(f32[16,32,128]{2,1,0:T(8,128)} %get-tuple-element.29), calls=%async_computation | async-start | bytes 524288 | tf_op jit(solution)/shard_map/all_to_all | solution.py:682
  11.1 9.9 %collective-permute-start.2 = (f32[40,128]{1,0:T(8,128)S(1)}, f32[40,128]{1,0:T(8,128)S(1)}, u32[]{:S(2)}, u32[]{:S(2)}) collective-permute-start(f32[40,128]{1,0:T(8,128)S(1)} %get-tuple-element.30), channel_id=1, source_target_pairs={{0,1},{1,2},{2,3},{3,4},{4,5},{5,6},{6,7},{7,8},{8,9},{9,10},{10,1... | collective-permute-start | bytes 61448 | tf_op jit(solution)/shard_map/ppermute | solution.py:681
  11.5 9.5 %collective-permute-start.1 = (f32[40,128]{1,0:T(8,128)S(1)}, f32[40,128]{1,0:T(8,128)S(1)}, u32[]{:S(2)}, u32[]{:S(2)}) collective-permute-start(f32[40,128]{1,0:T(8,128)S(1)} %get-tuple-element.30), channel_id=1, source_target_pairs={{1,0},{2,1},{3,2},{4,3},{5,4},{6,5},{7,6},{8,7},{9,8},{10,9},{11,1... | collective-permute-start | bytes 61448 | tf_op jit(solution)/shard_map/ppermute | solution.py:681
  15.6 5.4 %collective-permute-start = (f32[40,128]{1,0:T(8,128)S(1)}, f32[40,128]{1,0:T(8,128)S(1)}, u32[]{:S(2)}, u32[]{:S(2)}) collective-permute-start(f32[40,128]{1,0:T(8,128)S(1)} %get-tuple-element.30), channel_id=1, source_target_pairs={{0,16},{16,0},{1,17},{17,1},{2,18},{18,2},{3,19},{19,3},{4,20},{20... | collective-permute-start | bytes 61448 | tf_op jit(solution)/shard_map/ppermute | solution.py:678
  25.1 13.7 %all-to-all-start.1 = ((f32[16,32,128]{2,1,0:T(8,128)}), f32[16,32,128]{2,1,0:T(8,128)S(1)}, u32[]{:S(2)}, u32[]{:S(2)}) async-start(f32[16,32,128]{2,1,0:T(8,128)} %get-tuple-element.40), calls=%async_computation.1 | async-start | bytes 524288 | tf_op jit(solution)/shard_map/all_to_all | solution.py:682
  28.6 9.8 %collective-permute-start.5 = (f32[40,128]{1,0:T(8,128)S(1)}, f32[40,128]{1,0:T(8,128)S(1)}, u32[]{:S(2)}, u32[]{:S(2)}) collective-permute-start(f32[40,128]{1,0:T(8,128)S(1)} %get-tuple-element.41), channel_id=1, source_target_pairs={{0,1},{1,2},{2,3},{3,4},{4,5},{5,6},{6,7},{7,8},{8,9},{9,10},{10,1... | collective-permute-start | bytes 61448 | tf_op jit(solution)/shard_map/ppermute | solution.py:681
  28.9 9.6 %collective-permute-start.4 = (f32[40,128]{1,0:T(8,128)S(1)}, f32[40,128]{1,0:T(8,128)S(1)}, u32[]{:S(2)}, u32[]{:S(2)}) collective-permute-start(f32[40,128]{1,0:T(8,128)S(1)} %get-tuple-element.41), channel_id=1, source_target_pairs={{1,0},{2,1},{3,2},{4,3},{5,4},{6,5},{7,6},{8,7},{9,8},{10,9},{11,1... | collective-permute-start | bytes 61448 | tf_op jit(solution)/shard_map/ppermute | solution.py:681
  33.1 5.4 %collective-permute-start.3 = (f32[40,128]{1,0:T(8,128)S(1)}, f32[40,128]{1,0:T(8,128)S(1)}, u32[]{:S(2)}, u32[]{:S(2)}) collective-permute-start(f32[40,128]{1,0:T(8,128)S(1)} %get-tuple-element.41), channel_id=1, source_target_pairs={{0,16},{16,0},{1,17},{17,1},{2,18},{18,2},{3,19},{19,3},{4,20},{20... | collective-permute-start | bytes 61448 | tf_op jit(solution)/shard_map/ppermute | solution.py:678
